TPU v7x, 32 devices: a whole 2x2x4 slice. The times are simulated.
32 devices in a mesh: grp: 4 (over x, core), ep: 8 (over z, y).
Axes of the slice: x: 2, y: 2, z: 4, core: 2. Of those that a mesh axis runs over, the one named last changes fastest.
Arguments:
- tokens: bfloat16 [16384, 1024], P(('grp', 'ep')), may hold values from -6 to 6
- cotangent: bfloat16 [16384, 1024], P(('grp', 'ep')), may hold values from -6 to 6
- w_qkv: bfloat16 [1024, 3072], replicated, may hold values from -0.1875 to 0.1875
- w_out_attn: bfloat16 [1024, 1024], replicated, may hold values from -1.5 to 1.5
- rel_bias: bfloat16 [16, 512, 512], replicated, may hold values from -3 to 3
- norm_gains: float32 [2, 1024], replicated, may hold values from 0.1 to 1.9
- w_router: bfloat16 [1024, 8], replicated, may hold values from -0.125 to 0.125
- w_gate_up: bfloat16 [8, 1024, 5632], P('ep'), may hold values from -0.1875 to 0.1875
- w_expert_out: bfloat16 [8, 2816, 1024], P('ep'), may hold values from -0.75 to 0.75
- routes: int32 [16384, 2], P(('grp', 'ep')), may hold values from 0 to 7, all different within a row; in each aligned block of 512 rows (0 to 511, 512 to 1023, ...) at most 160 rows name the same one
- spans: int32 [32, 2], P(('grp', 'ep')), may hold values from 0 to 384, as said below
Outputs:
- output: float32 [16384, 1024], P(('grp', 'ep'))
- grad_tokens: float32 [16384, 1024], P(('grp', 'ep'))
- grad_w_qkv: float32 [1024, 3072], P('grp', 'ep')
- grad_w_out_attn: float32 [1024, 1024], P('grp', 'ep')
- grad_rel_bias: float32 [16, 512, 512], P('ep', 'grp')
- grad_norm_gains: float32 [2, 1024], replicated
- grad_w_router: float32 [1024, 8], replicated
- grad_w_gate_up: float32 [8, 1024, 5632], P('ep', 'grp')
- grad_w_expert_out: float32 [8, 2816, 1024], P('ep', 'grp')
Inputs may be any that keep to these rules, and one draw needn't show every extreme that they name: `routes`: each row names 2 different experts; within each aligned block of 512 rows (the rows of one device) no expert is named more than 160 times. `spans`: row s is the start and the length of sequence s's picture span: the length lies between 128 and 256, start + length <= 512; sequence 0's span starts at 0 with length 256, and sequence 1's span has length 128 and ends at 512.
All inputs are finite; a program needn't handle non-finite values.
Results may differ from a plain program's by a relative error of at most 0.02.
Values may be sent and summed in bfloat16 or wider, within the bound.
No kernel may reach another device: no remote copies, remote signals or barrier semaphores. Data moves between devices by JAX's collectives and lax.ppermute only.
A program may use at most 256 MiB of HBM per device.

v0:
```python
import math

import jax
import jax.numpy as jnp
from jax import lax
from jax.sharding import PartitionSpec as P

HEADS = 16
LENGTH = 512


EPSILON = 1e-06


def norm_forward(values):
    inverse = lax.rsqrt(jnp.mean(values * values, axis=-1, keepdims=True) + EPSILON)
    return (values * inverse, inverse)


def norm_backward(grad_out, normed, inverse, norm_gain):
    grad_normed = grad_out * norm_gain
    grad_gain = jnp.sum(grad_out * normed, axis=0)
    grad_input = inverse * (
        grad_normed - normed * jnp.mean(grad_normed * normed, axis=-1, keepdims=True)
    )
    return (grad_input, grad_gain)


def slot_positions(block_routes, expert_count, capacity):
    flat_routes = block_routes.reshape(-1)
    one_hot = (flat_routes[:, None] == jnp.arange(expert_count, dtype=jnp.int32)[None, :]).astype(
        jnp.int32
    )
    earlier = jnp.cumsum(one_hot, axis=0) - one_hot
    slot_counts = jnp.sum(earlier * one_hot, axis=1)
    return (flat_routes * capacity + slot_counts).reshape(block_routes.shape)


def allowed_mask(seq_span):
    query_index = lax.broadcasted_iota(jnp.int32, (LENGTH, LENGTH), 0)
    key_index = lax.broadcasted_iota(jnp.int32, (LENGTH, LENGTH), 1)
    span_end = seq_span[0] + seq_span[1]
    inside = (
        (query_index >= seq_span[0])
        & (query_index < span_end)
        & (key_index >= seq_span[0])
        & (key_index < span_end)
    )
    return (key_index <= query_index) | inside


def split_heads(qkv_seq):
    split_view = qkv_seq.reshape(qkv_seq.shape[0], 3, HEADS, qkv_seq.shape[1] // (3 * HEADS))
    return (split_view[:, 0], split_view[:, 1], split_view[:, 2])


def scores_of(query_heads, key_heads, rel_bias, seq_span, score_scale):
    raw_scores = (
        jnp.einsum("qhd,khd->hqk", query_heads, key_heads, preferred_element_type=jnp.float32)
        * score_scale
        + rel_bias
    )
    return jnp.where(allowed_mask(seq_span)[None], raw_scores, -1e30)


def attention_forward(qkv_rows, spans, rel_bias, score_scale):
    seq_count = spans.shape[0]
    stacked = qkv_rows.reshape(seq_count, LENGTH, qkv_rows.shape[1])

    def one_sequence(seq_item):
        qkv_seq, seq_span = seq_item
        query_heads, key_heads, value_heads = split_heads(qkv_seq)
        scores = scores_of(query_heads, key_heads, rel_bias, seq_span, score_scale)
        row_max = jnp.max(scores, axis=-1, keepdims=True)
        exp_scores = jnp.exp(scores - row_max)
        row_total = jnp.sum(exp_scores, axis=-1, keepdims=True)
        attn_probs = (exp_scores / row_total).astype(jnp.bfloat16)
        mixed_heads = jnp.einsum(
            "hqk,khd->qhd", attn_probs, value_heads, preferred_element_type=jnp.float32
        )
        return (
            mixed_heads.reshape(LENGTH, -1).astype(jnp.bfloat16),
            row_max[..., 0] + jnp.log(row_total[..., 0]),
        )

    mixed_heads, log_total = lax.map(one_sequence, (stacked, spans))
    return (mixed_heads.reshape(-1, mixed_heads.shape[-1]), log_total)


def attention_backward(qkv_rows, grad_mixed, spans, log_total, rel_bias, score_scale):
    seq_count = spans.shape[0]
    stacked = qkv_rows.reshape(seq_count, LENGTH, qkv_rows.shape[1])
    grad_stacked = grad_mixed.reshape(seq_count, LENGTH, grad_mixed.shape[1])

    def one_sequence(grad_bias, seq_item):
        qkv_seq, grad_seq, seq_span, seq_total = seq_item
        query_heads, key_heads, value_heads = split_heads(qkv_seq)
        grad_heads = grad_seq.reshape(LENGTH, HEADS, -1)
        scores = scores_of(query_heads, key_heads, rel_bias, seq_span, score_scale)
        attn_probs = jnp.exp(scores - seq_total[..., None])
        probs_low = attn_probs.astype(jnp.bfloat16)
        grad_value = jnp.einsum(
            "hqk,qhd->khd", probs_low, grad_heads, preferred_element_type=jnp.float32
        ).astype(jnp.bfloat16)
        grad_probs = jnp.einsum(
            "qhd,khd->hqk", grad_heads, value_heads, preferred_element_type=jnp.float32
        )
        grad_scores = attn_probs * (
            grad_probs - jnp.sum(attn_probs * grad_probs, axis=-1, keepdims=True)
        )
        grad_low = grad_scores.astype(jnp.bfloat16)
        grad_query = (
            jnp.einsum("hqk,khd->qhd", grad_low, key_heads, preferred_element_type=jnp.float32)
            * score_scale
        ).astype(jnp.bfloat16)
        grad_key = (
            jnp.einsum("hqk,qhd->khd", grad_low, query_heads, preferred_element_type=jnp.float32)
            * score_scale
        ).astype(jnp.bfloat16)
        joined = jnp.stack([grad_query, grad_key, grad_value], axis=1).reshape(LENGTH, -1)
        return (grad_bias + grad_low.astype(jnp.float32), joined)

    zero_bias = jnp.zeros(rel_bias.shape, jnp.float32)
    grad_bias, joined = lax.scan(one_sequence, zero_bias, (stacked, grad_stacked, spans, log_total))
    return (grad_bias, joined.reshape(-1, qkv_rows.shape[1]))


def body(
    tokens,
    cotangent,
    w_qkv,
    w_out_attn,
    rel_bias,
    norm_gains,
    w_router,
    w_gate_up,
    w_expert_out,
    routes,
    spans,
):
    tok_count = tokens.shape[0]
    model_width = tokens.shape[1]
    ep_size = lax.axis_size("ep")
    local_experts = w_gate_up.shape[0]
    ff_width = w_expert_out.shape[1]
    expert_count = local_experts * ep_size
    capacity = 5 * routes.shape[1] * tok_count // (4 * expert_count)
    score_scale = 1.0 / math.sqrt(model_width // HEADS)
    hidden = tokens.astype(jnp.float32)
    normed_one, inverse_one = norm_forward(hidden)
    a_one = (normed_one * norm_gains[0]).astype(jnp.bfloat16)
    qkv_rows = jnp.dot(a_one, w_qkv, preferred_element_type=jnp.float32).astype(jnp.bfloat16)
    mixed_heads, log_total = attention_forward(qkv_rows, spans, rel_bias, score_scale)
    after_attn = hidden + jnp.dot(mixed_heads, w_out_attn, preferred_element_type=jnp.float32)
    normed_two, inverse_two = norm_forward(after_attn)
    a_two = (normed_two * norm_gains[1]).astype(jnp.bfloat16)
    logits = jnp.dot(a_two, w_router, preferred_element_type=jnp.float32)
    router_probs = jax.nn.softmax(logits, axis=-1)
    position = slot_positions(routes, expert_count, capacity)
    flat_position = position.reshape(-1)
    token_ids = jnp.broadcast_to(
        jnp.arange(tok_count, dtype=jnp.int32)[:, None], position.shape
    ).reshape(-1)
    slot_total = expert_count * capacity
    source_index = jnp.zeros((slot_total,), jnp.int32).at[flat_position].set(token_ids)
    filled = jnp.zeros((slot_total,), jnp.bool_).at[flat_position].set(True)
    send_rows = jnp.where(filled[:, None], a_two[source_index], jnp.zeros((), jnp.bfloat16))
    send_rows = send_rows.reshape(ep_size, local_experts, capacity, model_width)
    slot_rows = lax.all_to_all(send_rows, "ep", split_axis=0, concat_axis=0, tiled=True)
    gate_up = jnp.einsum("secd,edf->secf", slot_rows, w_gate_up, preferred_element_type=jnp.float32)
    activation = (jax.nn.gelu(gate_up[..., :ff_width]) * gate_up[..., ff_width:]).astype(
        jnp.bfloat16
    )
    expert_rows = jnp.einsum(
        "secf,efd->secd", activation, w_expert_out, preferred_element_type=jnp.float32
    ).astype(jnp.bfloat16)
    returned = lax.all_to_all(expert_rows, "ep", split_axis=0, concat_axis=0, tiled=True)
    kept_parts = (returned, slot_rows, gate_up)
    returned = kept_parts[0]
    recv_rows = kept_parts[1]
    returned_flat = returned.reshape(slot_total, model_width)
    picked = returned_flat[position].astype(jnp.float32)
    route_gates = jnp.take_along_axis(router_probs, routes, axis=1)
    output = after_attn + jnp.sum(route_gates[..., None] * picked, axis=1)
    grad_out = cotangent.astype(jnp.float32)
    grad_gates = jnp.sum(picked * grad_out[:, None, :], axis=-1)
    grad_route_rows = (route_gates[..., None] * grad_out[:, None, :]).astype(jnp.bfloat16)
    grad_send = (
        jnp.zeros((slot_total, model_width), jnp.bfloat16)
        .at[flat_position]
        .set(grad_route_rows.reshape(-1, model_width))
    )
    grad_recv = lax.all_to_all(
        grad_send.reshape(ep_size, local_experts, capacity, model_width),
        "ep",
        split_axis=0,
        concat_axis=0,
        tiled=True,
    )
    gate_up = kept_parts[2]
    gate_part = gate_up[..., :ff_width]
    up_part = gate_up[..., ff_width:]
    gelu_value, gelu_pull = jax.vjp(jax.nn.gelu, gate_part)
    activation = (gelu_value * up_part).astype(jnp.bfloat16)
    grad_act = jnp.einsum(
        "secd,efd->secf", grad_recv, w_expert_out, preferred_element_type=jnp.float32
    )
    grad_gate_part = gelu_pull(grad_act * up_part)[0]
    grad_gate_up = jnp.concatenate([grad_gate_part, grad_act * gelu_value], axis=-1).astype(
        jnp.bfloat16
    )
    grad_w_expert = jnp.einsum(
        "secf,secd->efd", activation, grad_recv, preferred_element_type=jnp.float32
    )
    grad_w_gate = jnp.einsum(
        "secd,secf->edf", recv_rows, grad_gate_up, preferred_element_type=jnp.float32
    )
    grad_slot_rows = jnp.einsum(
        "secf,edf->secd", grad_gate_up, w_gate_up, preferred_element_type=jnp.float32
    ).astype(jnp.bfloat16)
    grad_back = lax.all_to_all(grad_slot_rows, "ep", split_axis=0, concat_axis=0, tiled=True)
    expert_parts = (
        lax.psum_scatter(
            grad_w_gate.astype(jnp.bfloat16), "grp", scatter_dimension=1, tiled=True
        ).astype(jnp.float32),
        lax.psum_scatter(
            grad_w_expert.astype(jnp.bfloat16), "grp", scatter_dimension=1, tiled=True
        ).astype(jnp.float32),
    )
    grad_flat = grad_back.reshape(slot_total, model_width)
    grad_a_two = jnp.sum(grad_flat[position].astype(jnp.float32), axis=1)
    chosen = (routes[..., None] == jnp.arange(expert_count, dtype=jnp.int32)).astype(jnp.float32)
    grad_probs = jnp.sum(chosen * grad_gates[..., None], axis=1)
    grad_logits = (
        router_probs * (grad_probs - jnp.sum(router_probs * grad_probs, axis=-1, keepdims=True))
    ).astype(jnp.bfloat16)
    grad_w_route = jnp.einsum("td,te->de", a_two, grad_logits, preferred_element_type=jnp.float32)
    grad_a_two = grad_a_two + jnp.einsum(
        "te,de->td", grad_logits, w_router, preferred_element_type=jnp.float32
    )
    grad_norm_two, grad_gain_two = norm_backward(grad_a_two, normed_two, inverse_two, norm_gains[1])
    grad_after = grad_out + grad_norm_two
    grad_attn_low = grad_after.astype(jnp.bfloat16)
    grad_w_attn = jnp.einsum(
        "td,te->de", mixed_heads, grad_attn_low, preferred_element_type=jnp.float32
    )
    grad_mixed = jnp.einsum(
        "te,de->td", grad_attn_low, w_out_attn, preferred_element_type=jnp.float32
    ).astype(jnp.bfloat16)
    grad_bias, grad_qkv = attention_backward(
        qkv_rows, grad_mixed, spans, log_total, rel_bias, score_scale
    )
    grad_w_proj = jnp.einsum("td,te->de", a_one, grad_qkv, preferred_element_type=jnp.float32)
    grad_a_one = jnp.einsum("te,de->td", grad_qkv, w_qkv, preferred_element_type=jnp.float32)
    grad_norm_one, grad_gain_one = norm_backward(grad_a_one, normed_one, inverse_one, norm_gains[0])
    grad_tokens = grad_after + grad_norm_one
    small_parts = lax.psum((jnp.stack([grad_gain_one, grad_gain_two]), grad_w_route), ("grp", "ep"))
    dense_first = (
        lax.psum_scatter(
            grad_w_proj.astype(jnp.bfloat16), "ep", scatter_dimension=1, tiled=True
        ).astype(jnp.float32),
        lax.psum_scatter(
            grad_w_attn.astype(jnp.bfloat16), "ep", scatter_dimension=1, tiled=True
        ).astype(jnp.float32),
        lax.psum_scatter(
            grad_bias.astype(jnp.bfloat16), "ep", scatter_dimension=0, tiled=True
        ).astype(jnp.float32),
    )
    dense_parts = (
        lax.psum_scatter(
            dense_first[0].astype(jnp.bfloat16), "grp", scatter_dimension=0, tiled=True
        ).astype(jnp.float32),
        lax.psum_scatter(
            dense_first[1].astype(jnp.bfloat16), "grp", scatter_dimension=0, tiled=True
        ).astype(jnp.float32),
        lax.psum_scatter(
            dense_first[2].astype(jnp.bfloat16), "grp", scatter_dimension=1, tiled=True
        ).astype(jnp.float32),
    )
    return (
        output,
        grad_tokens,
        dense_parts[0],
        dense_parts[1],
        dense_parts[2],
        small_parts[0],
        small_parts[1],
        expert_parts[0],
        expert_parts[1],
    )


def solution(mesh):
    placed = (
        P(("grp", "ep"), None),
        P(("grp", "ep"), None),
        P(),
        P(),
        P(),
        P(),
        P(),
        P("ep", None, None),
        P("ep", None, None),
        P(("grp", "ep"), None),
        P(("grp", "ep"), None),
    )
    return jax.shard_map(
        body,
        mesh=mesh,
        in_specs=placed,
        out_specs=(
            P(("grp", "ep"), None),
            P(("grp", "ep"), None),
            P("grp", "ep"),
            P("grp", "ep"),
            P("ep", "grp", None),
            P(),
            P(),
            P("ep", "grp", None),
            P("ep", "grp", None),
        ),
        check_vma=False,
    )
```

profile of v0, /device:TPU:0, one launch (start us, length us, event | category | flops | bytes accessed | tf_op | source)
XLA Modules:
  0.0 1008.1 jit_solution(7619262878816804287)
XLA Ops:
  14.6 8.3 convolution_convert_fusion.1
  27.7 12.3 %copy.110 = bf16[16,512,512]{1,2,0:T(8,128)(2,1)} copy(bf16[16,512,512]{2,1,0:T(8,128)(2,1)} %param.15) | data formatting | bytes 16777216 | tf_op args[4]
  40.3 13.9 %fusion.78 = (f32[16,512]{1,0:T(8,128)S(1)}, f32[16,512,512]{1,2,0:T(8,128)}) fusion(bf16[16,512,512]{1,2,0:T(8,128)(2,1)} %copy.110, bf16[512,3,16,64]{0,3,2,1:T(8,128)(2,1)} %bitcast.187, pred[512,512]{0,1:T(8,128)(4,1)S(1)} %fusion.57), kind=kOutput, calls=%fused_computation.143 | convolution fusion | flops 557834240 | bytes 27557888 | tf_op jit(solution)/shard_map/while/body/eval_jaxpr/qhd,khd->hqk/dot_general | solution.py:59
  54.1 8.3 fusion
  62.5 9.2 fusion.47
  124.7 8.4 scatter_custom_fusion.2
  133.1 32.2 %all-to-all-done = bf16[8,1,160,1024]{3,2,1,0:T(8,128)(2,1)} async-done(((bf16[8,1,160,1024]{3,2,1,0:T(8,128)(2,1)}), bf16[8,1,160,1024]{3,2,1,0:T(8,128)(2,1)}, u32[]{:S(2)}, u32[]{:S(2)}) %all-to-all-start) | async-done | bytes 2621472 | tf_op jit(solution)/shard_map/all_to_all | solution.py:169
  169.9 24.0 %convolution_bitcast_fusion = f32[8,1,160,5632]{3,2,0,1:T(8,128)} fusion(bf16[1,1024,5632]{2,1,0:T(8,128)(2,1)} %param.18, bf16[8,1,160,1024]{3,2,1,0:T(8,128)(2,1)} %all-to-all-done), kind=kOutput, calls=%fused_computation.17 | convolution fusion | flops 14763950080 | bytes 42991616 | tf_op jit(solution)/shard_map/secd,edf->secf/dot_general | solution.py:170
  193.8 35.0 %all-to-all-done.2 = bf16[8,1,160,1024]{3,2,1,0:T(8,128)(2,1)} async-done(((bf16[8,1,160,1024]{3,2,1,0:T(8,128)(2,1)}), bf16[8,1,160,1024]{3,2,1,0:T(8,128)(2,1)}, u32[]{:S(2)}, u32[]{:S(2)}) %all-to-all-start.2) | async-done | bytes 2621472 | tf_op jit(solution)/shard_map/all_to_all | solution.py:193
  228.9 25.1 %fusion.20 = (bf16[8,160,2816]{2,1,0:T(8,128)(2,1)}, bf16[8,160,2816]{2,1,0:T(8,128)(2,1)}, bf16[8,160,2816]{2,1,0:T(8,128)(2,1)S(1)}) fusion(f32[8,1,160,5632]{3,2,0,1:T(8,128)} %convolution_bitcast_fusion, bf16[1,2816,1024]{2,1,0:T(8,128)(2,1)} %param.19, bf16[8,1,160,1024]{3,2,1,0:T(8,128)(2,1)} %all-to-all-done.2), kind=kOutput, calls=%fused_computation.42 | convolution fusion | flops 7475691520 | bytes 58851328 | tf_op jit(solution)/shard_map/secd,efd->secf/dot_general | solution.py:205
  256.8 11.0 %convert_bitcast_fusion.1 = bf16[8,1,160,1024]{3,2,1,0:T(8,128)(2,1)} fusion(bf16[8,160,2816]{2,1,0:T(8,128)(2,1)S(1)} %get-tuple-element.115, bf16[1,2816,1024]{2,1,0:T(8,128)(2,1)} %param.19), kind=kOutput, calls=%fused_computation.66 | convolution fusion | flops 7383285760 | bytes 15597568 | tf_op jit(solution)/shard_map/secf,efd->secd/dot_general | solution.py:174
  272.2 22.0 %convert_bitcast_fusion = bf16[8,1,160,1024]{3,2,1,0:T(8,128)(2,1)} fusion(bf16[1,1024,5632]{2,1,0:T(8,128)(2,1)} %param.18, bf16[8,160,2816]{2,1,0:T(8,128)(2,1)} %get-tuple-element.114, bf16[8,160,2816]{2,1,0:T(8,128)(2,1)} %get-tuple-element.113), kind=kOutput, calls=%fused_computation.65 | convolution fusion | flops 14794096640 | bytes 28573696 | tf_op jit(solution)/shard_map/secf,edf->secd/dot_general | solution.py:218
  294.1 36.9 %all-to-all-done.1 = bf16[8,1,160,1024]{3,2,1,0:T(8,128)(2,1)} async-done(((bf16[8,1,160,1024]{3,2,1,0:T(8,128)(2,1)}), bf16[8,1,160,1024]{3,2,1,0:T(8,128)(2,1)}, u32[]{:S(2)}, u32[]{:S(2)}) %all-to-all-start.1) | async-done | bytes 2621472 | tf_op jit(solution)/shard_map/all_to_all | solution.py:177
  337.6 8.1 gather_fusion.1
  351.2 10.5 %multiply_reduce_fusion.1 = (f32[512,2]{1,0:T(8,128)}, f32[512,1024]{1,0:T(8,128)}) fusion(f32[512,2,1024]{2,1,0:T(2,128)} %reshape.355, f32[512,1024]{1,0:T(8,128)} %convert_element_type.183, f32[512,2]{1,0:T(8,128)S(1)} %copy-done.12), kind=kLoop, calls=%fused_computation.50 | loop fusion | flops 3668992 | bytes 8396800 | tf_op jit(solution)/shard_map/reduce_sum | solution.py:186
  362.9 31.6 %all-to-all-done.3 = bf16[8,1,160,1024]{3,2,1,0:T(8,128)(2,1)} async-done(((bf16[8,1,160,1024]{3,2,1,0:T(8,128)(2,1)}), bf16[8,1,160,1024]{3,2,1,0:T(8,128)(2,1)}, u32[]{:S(2)}, u32[]{:S(2)}) %all-to-all-start.3) | async-done | bytes 2621472 | tf_op jit(solution)/shard_map/all_to_all | solution.py:221
  394.5 8.1 gather_fusion.2
  408.4 8.5 reduce_sum.149
  432.8 11.6 %multiply_reduce_fusion = (f32[16,512]{1,0:T(8,128)S(1)}, f32[16,512,512]{1,2,0:T(8,128)}) fusion(f32[16,512,512]{1,2,0:T(8,128)} %get-tuple-element.125, f32[16,512]{1,0:T(8,128)S(1)} %log_add_fusion, bf16[512,16,64]{0,2,1:T(8,128)(2,1)S(1)} %bitcast.195, bf16[512,3,16,64]{0,3,2,1:T(8,128)(2,1)} %bitcast.189), kind=kOutput, calls=%fused_computation.11 | convolution fusion | flops 549445632 | bytes 35717120 | tf_op jit(solution)/shard_map/while/body/eval_jaxpr/qhd,khd->hqk/dot_general | solution.py:105
  444.4 15.5 %multiply_convert_fusion = bf16[16,512,512]{1,2,0:T(8,128)(2,1)} fusion(f32[16,512,512]{1,2,0:T(8,128)} %get-tuple-element.132, f32[16,512,512]{1,2,0:T(8,128)} %get-tuple-element.125, f32[16,512]{1,0:T(8,128)S(1)} %get-tuple-element.131, f32[16,512]{1,0:T(8,128)S(1)} %log_add_fusion), kind=kLoop, calls=%fused_computation.10 | loop fusion | flops 16777216 | bytes 42008576 | tf_op jit(solution)/shard_map/while/body/eval_jaxpr/convert_element_type | solution.py:111
  470.1 8.6 fusion.53
  486.6 8.7 copy.134
  502.4 12.5 %fusion.25 = bf16[1,2816,1024]{2,1,0:T(8,128)(2,1)} fusion(bf16[8,160,2816]{2,1,0:T(8,128)(2,1)} %copy-done.38, bf16[8,1,160,1024]{3,2,1,0:T(8,128)(2,1)} %all-to-all-done.2), kind=kOutput, calls=%fused_computation.48 | convolution fusion | flops 7384858624 | bytes 15597568 | tf_op jit(solution)/shard_map/secf,secd->efd/dot_general | solution.py:212
  515.0 106.2 %reduce-scatter.25.cloned.1.call-done = bf16[384,1024]{1,0:T(8,128)(2,1)} async-done(((bf16[3072,1024]{1,0:T(8,128)(2,1)}), bf16[384,1024]{1,0:T(8,128)(2,1)}) %reduce-scatter.25.cloned.1.call-update) | async-done | bytes 786448
  623.6 23.5 %fusion.13 = bf16[1,1024,5632]{2,1,0:T(8,128)(2,1)} fusion(bf16[8,160,2816]{2,1,0:T(8,128)(2,1)} %get-tuple-element.114, bf16[8,160,2816]{2,1,0:T(8,128)(2,1)} %get-tuple-element.113, bf16[8,1,160,1024]{3,2,1,0:T(8,128)(2,1)} %all-to-all-done), kind=kOutput, calls=%fused_computation.36 | convolution fusion | flops 14798553088 | bytes 28573696 | tf_op jit(solution)/shard_map/secd,secf->edf/dot_general | solution.py:215
  647.2 124.4 %reduce-scatter.19.cloned.1.call-done = bf16[2,512,512]{1,2,0:T(8,128)(2,1)} async-done(((bf16[16,512,512]{1,2,0:T(8,128)(2,1)}), bf16[2,512,512]{1,2,0:T(8,128)(2,1)}) %reduce-scatter.19.cloned.1.call-update) | async-done | bytes 1048592 | tf_op jit(solution)/shard_map/reduce_scatter | solution.py:265
  778.0 9.1 fusion.39
  787.4 40.8 %all-reduce = (f32[2,1024]{1,0:T(2,128)}, f32[1024,8]{0,1:T(8,128)}) all-reduce(f32[2,1024]{1,0:T(2,128)S(1)} %pad_maximum_fusion.6, f32[1024,8]{0,1:T(8,128)S(1)} %fusion.84), channel_id=1, replica_groups=mesh['grp'=4,'ep'=8] {'grp','ep'}, use_global_device_ids=true, to_apply=%region_28.29 | all-reduce | flops 10240 | bytes 81920 | tf_op jit(solution)/shard_map/psum | solution.py:257
  833.9 18.3 %reduce-scatter.23.cloned.1.call-done = bf16[1,704,1024]{2,1,0:T(8,128)(2,1)} async-done(((bf16[1,2816,1024]{2,1,0:T(8,128)(2,1)}), bf16[1,704,1024]{2,1,0:T(8,128)(2,1)}) %reduce-scatter.23.cloned.1.call-update) | async-done | bytes 1441808 | tf_op jit(solution)/shard_map/reduce_scatter | solution.py:226
  855.5 22.3 %reduce-scatter.15.cloned.1.call-done = bf16[256,384]{1,0:T(8,128)(2,1)} async-done(((bf16[1024,384]{1,0:T(8,128)(2,1)}), bf16[256,384]{1,0:T(8,128)(2,1)}) %reduce-scatter.15.cloned.1.call-update) | async-done | bytes 196624 | tf_op jit(solution)/shard_map/reduce_scatter | solution.py:270
  879.5 91.8 %reduce-scatter.21.cloned.1.call-done = bf16[1,256,5632]{2,1,0:T(8,128)(2,1)} async-done(((bf16[1,1024,5632]{2,1,0:T(8,128)(2,1)}), bf16[1,256,5632]{2,1,0:T(8,128)(2,1)}) %reduce-scatter.21.cloned.1.call-update) | async-done | bytes 2883600 | tf_op jit(solution)/shard_map/reduce_scatter | solution.py:223
  976.3 22.4 %reduce-scatter.29.cloned.1.call-done = bf16[128,1024]{1,0:T(8,128)(2,1)} async-done(((bf16[512,1024]{1,0:T(8,128)(2,1)}), bf16[128,1024]{1,0:T(8,128)(2,1)}) %reduce-scatter.29.cloned.1.call-update) | async-done | bytes 262160
  (187 shorter events, 162.7 us)
Async XLA Ops:
  7.2 64.5 %copy-start = (bf16[1024,1024]{1,0:T(8,128)(2,1)S(1)}, bf16[1024,1024]{1,0:T(8,128)(2,1)}, u32[]{:S(2)}) copy-start(bf16[1024,1024]{1,0:T(8,128)(2,1)} %param.14) | copy-start | bytes 6291460
  12.5 75.3 %copy-start.23 = (f32[1,1024]{1,0:T(1,128)}, f32[1,1024]{1,0:T(1,128)S(1)}, u32[]{:S(2)}) copy-start(f32[1,1024]{1,0:T(1,128)S(1)} %get-tuple-element.118) | copy-start | bytes 12292
  54.1 8.3 copy-start.17
  62.4 9.2 copy-start.19
  62.4 9.2 copy-start.6
  74.3 20.4 %copy-start.31 = (f32[512]{0:T(512)}, f32[512]{0:T(512)S(1)}, u32[]{:S(2)}) copy-start(f32[512]{0:T(512)S(1)} %add_rsqrt_fusion) | copy-start | bytes 6148
  89.7 16.3 %copy-start.1 = (bf16[512,1024]{1,0:T(8,128)(2,1)}, bf16[512,1024]{1,0:T(8,128)(2,1)S(1)}, u32[]{:S(2)}) copy-start(bf16[512,1024]{1,0:T(8,128)(2,1)S(1)} %multiply_convert_fusion.6) | copy-start | bytes 3145732
  98.3 7.8 copy-start.25
  98.3 67.0 %all-to-all-start = ((bf16[8,1,160,1024]{3,2,1,0:T(8,128)(2,1)}), bf16[8,1,160,1024]{3,2,1,0:T(8,128)(2,1)}, u32[]{:S(2)}, u32[]{:S(2)}) async-start(bf16[8,1,160,1024]{3,2,1,0:T(8,128)(2,1)} %broadcast_select_fusion), calls=%async_computation | async-start | bytes 5242880 | tf_op jit(solution)/shard_map/all_to_all | solution.py:169
  106.5 7.1 copy-start.27
  114.1 10.6 %copy-start.11 = (f32[512,2]{1,0:T(8,128)}, f32[512,2]{1,0:T(8,128)S(1)}, u32[]{:S(2)}) copy-start(f32[512,2]{1,0:T(8,128)S(1)} %copy.114) | copy-start | bytes 12292
  165.3 63.6 %all-to-all-start.2 = ((bf16[8,1,160,1024]{3,2,1,0:T(8,128)(2,1)}), bf16[8,1,160,1024]{3,2,1,0:T(8,128)(2,1)}, u32[]{:S(2)}, u32[]{:S(2)}) async-start(bf16[8,1,160,1024]{3,2,1,0:T(8,128)(2,1)} %bitcast.193), calls=%async_computation.2 | async-start | bytes 5242880 | tf_op jit(solution)/shard_map/all_to_all | solution.py:193
  267.8 63.3 %all-to-all-start.1 = ((bf16[8,1,160,1024]{3,2,1,0:T(8,128)(2,1)}), bf16[8,1,160,1024]{3,2,1,0:T(8,128)(2,1)}, u32[]{:S(2)}, u32[]{:S(2)}) async-start(bf16[8,1,160,1024]{3,2,1,0:T(8,128)(2,1)} %convert_bitcast_fusion.1), calls=%async_computation.1 | async-start | bytes 5242880 | tf_op jit(solution)/shard_map/all_to_all | solution.py:177
  294.1 41.4 %copy-start.5 = (bf16[512,1024]{1,0:T(8,128)(2,1)S(1)}, bf16[512,1024]{1,0:T(8,128)(2,1)}, u32[]{:S(2)}) copy-start(bf16[512,1024]{1,0:T(8,128)(2,1)} %param.12) | copy-start | bytes 3145732
  294.1 43.1 %copy-start.35 = (s32[512,2]{0,1:T(2,128)S(1)}, s32[512,2]{0,1:T(2,128)}, u32[]{:S(2)}) copy-start(s32[512,2]{0,1:T(2,128)} %get-tuple-element.120) | copy-start | bytes 12292
  331.1 63.4 %all-to-all-start.3 = ((bf16[8,1,160,1024]{3,2,1,0:T(8,128)(2,1)}), bf16[8,1,160,1024]{3,2,1,0:T(8,128)(2,1)}, u32[]{:S(2)}, u32[]{:S(2)}) async-start(bf16[8,1,160,1024]{3,2,1,0:T(8,128)(2,1)} %convert_bitcast_fusion), calls=%async_computation.3 | async-start | bytes 5242880 | tf_op jit(solution)/shard_map/all_to_all | solution.py:221
  335.5 165.0 %reduce-scatter.27.cloned.1.call-start = ((), (), s32[]{:S(2)}) async-start(), calls=%async_computation.18 | async-start | bytes 2359296
  351.1 11.6 %copy-start.22 = (s32[512,2]{0,1:T(2,128)S(1)}, s32[512,2]{0,1:T(2,128)}, u32[]{:S(2)}) copy-start(s32[512,2]{0,1:T(2,128)} %param.20) | copy-start | bytes 12292
  351.1 11.6 %copy-start.16 = (f32[512,8]{0,1:T(8,128)S(1)}, f32[512,8]{0,1:T(8,128)}, u32[]{:S(2)}) copy-start(f32[512,8]{0,1:T(8,128)} %copy-done.15) | copy-start | bytes 49156
  351.1 11.6 %copy-start.28 = (f32[512]{0:T(512)S(1)}, f32[512]{0:T(512)}, u32[]{:S(2)}) copy-start(f32[512]{0:T(512)} %copy-done.27) | copy-start | bytes 6148
  351.2 11.6 %copy-start.30 = (f32[512]{0:T(512)S(1)}, f32[512]{0:T(512)}, u32[]{:S(2)}) copy-start(f32[512]{0:T(512)} %copy-done.29) | copy-start | bytes 6148
  408.4 8.5 copy-start.24
  408.4 8.5 copy-start.26
  408.4 8.5 copy-start.32
  432.8 188.5 %reduce-scatter.25.cloned.1.call-start = ((), (), s32[]{:S(2)}) async-start(), calls=%async_computation.17 | async-start | bytes 7077888
  495.3 276.3 %reduce-scatter.19.cloned.1.call-start = ((), (), s32[]{:S(2)}) async-start(), calls=%async_computation.14 | async-start | bytes 9437184 | tf_op jit(solution)/shard_map/reduce_scatter | solution.py:265
  496.0 336.3 %reduce-scatter.17.cloned.1.call-start = ((), (), s32[]{:S(2)}) async-start(), calls=%async_computation.13 | async-start | bytes 327680 | tf_op jit(solution)/shard_map/reduce_scatter | solution.py:273
  502.4 349.8 %reduce-scatter.23.cloned.1.call-start = ((), (), s32[]{:S(2)}) async-start(), calls=%async_computation.16 | async-start | bytes 7208960 | tf_op jit(solution)/shard_map/reduce_scatter | solution.py:226
  515.0 362.8 %reduce-scatter.15.cloned.1.call-start = ((), (), s32[]{:S(2)}) async-start(), calls=%async_computation.12 | async-start | bytes 983040 | tf_op jit(solution)/shard_map/reduce_scatter | solution.py:270
  623.6 347.7 %reduce-scatter.21.cloned.1.call-start = ((), (), s32[]{:S(2)}) async-start(), calls=%async_computation.15 | async-start | bytes 14417920 | tf_op jit(solution)/shard_map/reduce_scatter | solution.py:223
  647.1 351.5 %reduce-scatter.29.cloned.1.call-start = ((), (), s32[]{:S(2)}) async-start(), calls=%async_computation.19 | async-start | bytes 1310720
  778.0 9.1 copy-start.2
  (19 other events, 55.5 us)
Sparse Core Ops, SparseCore 0:
  432.9 67.6 reduce-scatter.26
  504.1 117.0 reduce-scatter.24
  624.9 146.7 reduce-scatter.18
  774.5 19.1 reduce-scatter.16
  796.6 55.4 reduce-scatter.22
  854.6 23.1 reduce-scatter.14
  880.4 90.8 reduce-scatter.20
  973.8 24.8 reduce-scatter.28
where the time goes:
time: 1010 us
  waiting for transfers between devices  526 us (52%)
  matrix products  205 us (20%)
  local copies, waits for them, and re-layouts  116 us (11%)
  other arithmetic  82 us (8%)
  blocking collectives  40.8 us (4%)
  starting transfers between devices  21.1 us (2%)
  between operations  16.4 us (2%)
    unnamed x11, waiting for transfers between devices  134 us
    reduce_scatter x1, waiting for transfers between devices, body(): lax.psum_scatter(grad_bias.astype(jnp.bfloat16), 'ep', scatter_dimension=...  124 us
    reduce_scatter x1, waiting for transfers between devices, body(): lax.psum_scatter(grad_w_gate.astype(jnp.bfloat16), 'grp', scatter_dimensi...  91.8 us
    unnamed x89, local copies, waits for them, and re-layouts  45.4 us
    psum x1, blocking collectives, body(): lax.psum((jnp.stack([grad_gain_one, grad_gain_two]), grad_w_route), ('grp...  40.8 us
    all_to_all x1, waiting for transfers between devices, body(): lax.all_to_all(expert_rows, 'ep', split_axis=0, concat_axis=0, tiled=True)  36.9 us
    all_to_all x1, waiting for transfers between devices, body(): lax.all_to_all(grad_send.reshape(ep_size, local_experts, capacity, model_...  35 us
    all_to_all x1, waiting for transfers between devices, body(): lax.all_to_all(send_rows, 'ep', split_axis=0, concat_axis=0, tiled=True)  32.2 us
  transfers between devices with their start and end apart: 12, of which 11 were waited for; matrix products, arithmetic and copies ran while one was open for 23% of the time, Pallas kernels for 0%

commit v1 on v0

v1 whole, which is shorter than its diff:
```python
import functools
import math

import jax
import jax.numpy as jnp
from jax import lax
from jax.experimental import pallas as pl
from jax.experimental.pallas import tpu as pltpu
from jax.sharding import PartitionSpec as P

HEADS = 16
LENGTH = 512
EPSILON = 1e-06
LANES = 128
GELU_C = math.sqrt(2.0 / math.pi)
GELU_A = 0.044715
F32 = jnp.float32
BF16 = jnp.bfloat16
VMEM_LIMIT = 60 * 1024 * 1024


def params(**kw):
    return pltpu.CompilerParams(vmem_limit_bytes=VMEM_LIMIT, **kw)


def cost(flops, nbytes, trans=0):
    return pl.CostEstimate(flops=int(flops), bytes_accessed=int(nbytes), transcendentals=int(trans))


def dot_f32(a, b, dims):
    return lax.dot_general(a, b, (dims, ((), ())), preferred_element_type=F32)


NN = ((1,), (0,))
NT = ((1,), (1,))
TN = ((0,), (0,))


def xor_send(v, axis, k):
    n = lax.axis_size(axis)
    return lax.ppermute(v, axis, [(i, i ^ k) for i in range(n)])


def halving_steps(n_g, n_e):
    g_bits = [("grp", 1 << i) for i in range(n_g.bit_length() - 1)]
    e_bits = [("ep", 1 << i) for i in range(n_e.bit_length() - 1)]
    steps = g_bits[:1]
    rest_g, rest_e = g_bits[1:], e_bits
    while rest_g or rest_e:
        steps += rest_e[:1] + rest_g[:1]
        rest_e, rest_g = rest_e[1:], rest_g[1:]
    return steps


def halve(keep, send, steps):
    total = None
    for i, (axis, k) in enumerate(steps):
        got = xor_send(send, axis, k)
        total = keep.astype(F32) + got.astype(F32)
        if i + 1 < len(steps):
            low = total.astype(BF16)
            keep, send = low[0], low[1]
    return total


def butterfly(v, n_g, n_e):
    for axis, k in halving_steps(n_g, n_e):
        v = v + xor_send(v, axis, k)
    return v


def split_steps(steps, blocks, n_g, n_e):
    def build(i, r_g, r_e):
        if i == len(steps):
            return blocks[(r_g, r_e)]
        axis, k = steps[i]
        parts = []
        for b in (0, 1):
            parts.append(
                build(i + 1, r_g | (k * b if axis == "grp" else 0), r_e | (k * b if axis == "ep" else 0))
            )
        return jnp.stack(parts)

    axis, k = steps[0]
    keep = build(1, 0, 0)
    send = build(1, k if axis == "grp" else 0, k if axis == "ep" else 0)
    return keep, send


def dispatch_kernel(cap, pos_ref, v_ref, *outs):
    tok = v_ref.shape[0]
    first = pos_ref[0:1, :]
    second = pos_ref[1:2, :]
    rows = lax.broadcasted_iota(jnp.int32, (cap, tok), 0)
    for k, out in enumerate(outs):
        here = rows + k * cap
        pick = jnp.where((here == first) | (here == second), 1.0, 0.0).astype(BF16)
        out[...] = dot_f32(pick, v_ref[...], NN).astype(BF16)


def dispatch(pos_rows, values, cap, n_e):
    tok, width = values.shape
    return pl.pallas_call(
        functools.partial(dispatch_kernel, cap),
        out_shape=[jax.ShapeDtypeStruct((cap, width), BF16)] * n_e,
        compiler_params=params(),
        cost_estimate=cost(2 * n_e * cap * tok * width, 2 * tok * width + 2 * n_e * cap * width),
        name="dispatch_rows",
    )(pos_rows, values)


def gathered(pos_ref, parts, cap):
    first = pos_ref[:, 0:1]
    second = pos_ref[:, 1:2]
    lanes = lax.broadcasted_iota(jnp.int32, (pos_ref.shape[0], cap), 1)
    total = None
    for k, part in enumerate(parts):
        here = lanes + k * cap
        pick = jnp.where((here == first) | (here == second), 1.0, 0.0).astype(BF16)
        term = dot_f32(pick, part[...], NN)
        total = term if total is None else total + term
    return total


def combine_kernel(cap, pos_ref, x_ref, *refs):
    parts, out_ref = refs[:-1], refs[-1]
    out_ref[...] = x_ref[...] + gathered(pos_ref, parts, cap)


def combine(pos_cols, after_attn, parts, cap):
    tok, width = after_attn.shape
    blk = 256
    return pl.pallas_call(
        functools.partial(combine_kernel, cap),
        grid=(tok // blk,),
        in_specs=[
            pl.BlockSpec((blk, 2), lambda i: (i, 0)),
            pl.BlockSpec((blk, width), lambda i: (i, 0)),
        ]
        + [pl.BlockSpec((cap, width), lambda i: (0, 0))] * len(parts),
        out_specs=pl.BlockSpec((blk, width), lambda i: (i, 0)),
        out_shape=jax.ShapeDtypeStruct((tok, width), F32),
        compiler_params=params(),
        cost_estimate=cost(2 * tok * cap * len(parts) * width, 10 * tok * width),
        name="combine_rows",
    )(pos_cols, after_attn, *parts)


def return_kernel(cap, pos_ref, x_ref, cot_ref, gain_ref, *refs):
    parts, (dx_ref, low_ref, gg_ref) = refs[:-3], refs[-3:]
    grad = gathered(pos_ref, parts, cap)
    x = x_ref[...]
    inverse = lax.rsqrt(jnp.mean(x * x, axis=-1, keepdims=True) + EPSILON)
    normed = x * inverse
    grad_normed = grad * gain_ref[...]
    dx = cot_ref[...].astype(F32) + inverse * (
        grad_normed - normed * jnp.mean(grad_normed * normed, axis=-1, keepdims=True)
    )
    dx_ref[...] = dx
    low_ref[...] = dx.astype(BF16)

    @pl.when(pl.program_id(0) == 0)
    def _():
        gg_ref[...] = jnp.zeros_like(gg_ref)

    gg_ref[...] += jnp.sum(grad * normed, axis=0, keepdims=True)


def return_grads(pos_cols, after_attn, cotangent, gain, parts, cap):
    tok, width = after_attn.shape
    blk = 256
    row = pl.BlockSpec((blk, width), lambda i: (i, 0))
    one = pl.BlockSpec((1, width), lambda i: (0, 0))
    return pl.pallas_call(
        functools.partial(return_kernel, cap),
        grid=(tok // blk,),
        in_specs=[pl.BlockSpec((blk, 2), lambda i: (i, 0)), row, row, one]
        + [pl.BlockSpec((cap, width), lambda i: (0, 0))] * len(parts),
        out_specs=[row, row, one],
        out_shape=[
            jax.ShapeDtypeStruct((tok, width), F32),
            jax.ShapeDtypeStruct((tok, width), BF16),
            jax.ShapeDtypeStruct((1, width), F32),
        ],
        compiler_params=params(),
        cost_estimate=cost(2 * tok * cap * len(parts) * width, 16 * tok * width),
        name="return_rows",
    )(pos_cols, after_attn, cotangent, gain, *parts)


def expert_kernel(cap, n_blk, experts, aliased, *refs):
    me_ref, x_ref, d_ref, wg_ref, wu_ref, wr_ref, wrt_ref = refs[:7]
    refs = refs[7 + (3 if aliased else 0) :]
    act_ref, dg_ref, du_ref, dl_ref, p_ref = refs[:5]
    outs = refs[5 : 5 + n_blk]
    acc_ref, gate_ref, prob_ref = refs[5 + n_blk :]
    j = pl.program_id(0)
    rows_all = x_ref.shape[0]
    lane = lax.broadcasted_iota(jnp.int32, (rows_all, LANES), 1)

    @pl.when(j == 0)
    def _():
        logits = dot_f32(x_ref[...], wr_ref[...], NN)
        logits = jnp.where(lane < experts, logits, -1e30)
        exps = jnp.exp(logits - jnp.max(logits, axis=-1, keepdims=True))
        probs = exps / jnp.sum(exps, axis=-1, keepdims=True)
        prob_ref[...] = probs
        own = jnp.sum(jnp.where(lane == me_ref[0], probs, 0.0), axis=-1, keepdims=True)
        p_ref[...] = jnp.broadcast_to(own, p_ref.shape)
        acc_ref[...] = jnp.zeros_like(acc_ref)
        gate_ref[...] = jnp.zeros_like(gate_ref)

    for b in range(n_blk):
        rows = slice(b * cap, (b + 1) * cap)
        x = x_ref[rows, :]
        z = dot_f32(x, wg_ref[...], NN)
        up = dot_f32(x, wu_ref[...], NN)
        back = d_ref[rows, :].astype(F32)
        reps = z.shape[1] // LANES
        own = jnp.concatenate([p_ref[rows, :]] * reps, axis=1)
        zz = z * z
        th = jnp.tanh(GELU_C * z * (1.0 + GELU_A * zz))
        half = 0.5 + 0.5 * th
        gelu = z * half
        slope = half + 0.5 * GELU_C * z * (1.0 - th * th) * (1.0 + 3.0 * GELU_A * zz)
        act = (gelu * up).astype(BF16)
        act_ref[rows, :] = act
        share = act.astype(F32) * back
        gate_ref[rows, :] += sum(share[:, i * LANES : (i + 1) * LANES] for i in range(reps))
        dact = back * own
        dg = (dact * up * slope).astype(BF16)
        du = (dact * gelu).astype(BF16)
        dg_ref[rows, :] = dg
        du_ref[rows, :] = du
        acc_ref[rows, :] += dot_f32(dg, wg_ref[...], NT) + dot_f32(du, wu_ref[...], NT)

    @pl.when(j == pl.num_programs(0) - 1)
    def _():
        dgate = jnp.sum(gate_ref[...], axis=-1, keepdims=True)
        dl = dgate * p_ref[...] * (jnp.where(lane == me_ref[0], 1.0, 0.0) - prob_ref[...])
        dl = dl.astype(BF16)
        dl_ref[...] = dl
        total = acc_ref[...] + dot_f32(dl, wrt_ref[...], NN)
        for b, out in enumerate(outs):
            out[...] = total[b * cap : (b + 1) * cap, :].astype(BF16)


def expert_chunk(me, rows, dact, w_gate_up, wr_pad, wr_pad_t, experts, cap, start, total_rows, earlier):
    ff = dact.shape[1]
    tile = 256
    steps = ff // tile
    n_rows, width = rows.shape
    n_blk = n_rows // cap
    at = start // n_rows
    whole = pl.BlockSpec(memory_space=pl.ANY)
    part = pl.BlockSpec((n_rows, tile), lambda j, m: (at, j))
    wide = pl.BlockSpec((n_rows, LANES), lambda j, m: (0, 0))
    aliased = earlier is not None
    call = pl.pallas_call(
        functools.partial(expert_kernel, cap, n_blk, experts, aliased),
        grid_spec=pltpu.PrefetchScalarGridSpec(
            num_scalar_prefetch=1,
            grid=(steps,),
            in_specs=[
                pl.BlockSpec((n_rows, width), lambda j, m: (0, 0)),
                part,
                pl.BlockSpec((width, tile), lambda j, m: (0, j)),
                pl.BlockSpec((width, tile), lambda j, m: (0, j + steps)),
                pl.BlockSpec((width, LANES), lambda j, m: (0, 0)),
                pl.BlockSpec((LANES, width), lambda j, m: (0, 0)),
            ]
            + ([whole] * 3 if aliased else []),
            out_specs=[part, part, part, wide, wide]
            + [pl.BlockSpec((cap, width), lambda j, m: (0, 0))] * n_blk,
            scratch_shapes=[
                pltpu.VMEM((n_rows, width), F32),
                pltpu.VMEM((n_rows, LANES), F32),
                pltpu.VMEM((n_rows, LANES), F32),
            ],
        ),
        out_shape=[jax.ShapeDtypeStruct((total_rows, ff), BF16)] * 3
        + [
            jax.ShapeDtypeStruct((n_rows, LANES), BF16),
            jax.ShapeDtypeStruct((n_rows, LANES), F32),
        ]
        + [jax.ShapeDtypeStruct((cap, width), BF16)] * n_blk,
        input_output_aliases={7: 0, 8: 1, 9: 2} if aliased else {},
        compiler_params=params(),
        cost_estimate=cost(
            8 * n_rows * width * ff, 4 * width * ff + 10 * n_rows * ff + 4 * n_rows * width, n_rows * ff
        ),
        name="expert_rows",
    )
    args = (me, rows, dact, w_gate_up, w_gate_up, wr_pad, wr_pad_t)
    out = call(*args, *(earlier if aliased else ()))
    return out[:3], out[3], out[4], out[5:]


def relative(v, axis, me, n):
    return jnp.stack([lax.dynamic_index_in_dim(v, me ^ r, axis, keepdims=False) for r in range(n)], axis)


def blocks_of(full, n_g, n_e, me_g, me_e):
    rows, cols = full.shape
    view = full.reshape(n_g, rows // n_g, n_e, cols // n_e)
    out = {}
    for r_g in range(n_g):
        one = lax.dynamic_index_in_dim(view, me_g ^ r_g, 0, keepdims=False)
        for r_e in range(n_e):
            out[(r_g, r_e)] = lax.dynamic_index_in_dim(one, me_e ^ r_e, 1, keepdims=False)
    return out


def wgrad_kernel(n_g, steps, me_ref, a_ref, b_ref, keep_ref, send_ref, full_ref):
    full_ref[...] = dot_f32(a_ref[...], b_ref[...], TN)
    rows = full_ref.shape[0] // n_g
    for r_g in range(n_g):
        at = pl.multiple_of((me_ref[0] ^ r_g) * rows, rows)
        where = tuple(
            (1 if r_g & k else 0) if axis == "grp" else 0 for axis, k in steps[1:]
        )
        out = send_ref if r_g & 1 else keep_ref
        out[where] = full_ref[pl.ds(at, rows), :].astype(BF16)


def wgrad(me, a, b, n_g, n_e, steps):
    tok, m = a.shape
    n = b.shape[1]
    if (n // n_e) % LANES or n_e == 1:
        full = dot_f32(a, b, TN).astype(BF16)
        return split_steps(steps, blocks_of(full, n_g, n_e, me[0], me[1]), n_g, n_e)
    rows, cols = m // n_g, n // n_e
    lead = tuple(2 for _ in steps[1:])
    block = tuple(2 if axis == "grp" else 1 for axis, _ in steps[1:]) + (rows, cols)

    def out_index(r, me_ref):
        return tuple(
            (1 - (r & k == 0)) if axis == "grp" and False else (0 if axis == "grp" else (r // k) % 2)
            for axis, k in steps[1:]
        ) + (0, 0)

    spec = pl.BlockSpec(block, out_index)
    return pl.pallas_call(
        functools.partial(wgrad_kernel, n_g, steps),
        grid_spec=pltpu.PrefetchScalarGridSpec(
            num_scalar_prefetch=1,
            grid=(n_e,),
            in_specs=[
                pl.BlockSpec((tok, m), lambda r, me_ref: (0, 0)),
                pl.BlockSpec((tok, cols), lambda r, me_ref: (0, me_ref[1] ^ r)),
            ],
            out_specs=[spec, spec],
            scratch_shapes=[pltpu.VMEM((m, cols), F32)],
        ),
        out_shape=[jax.ShapeDtypeStruct(lead + (rows, cols), BF16)] * 2,
        compiler_params=params(),
        cost_estimate=cost(2 * tok * m * n, 2 * tok * (m + n) + 2 * m * n),
        name="weight_grad",
    )(me, a, b)


def gate_up_kernel(n_g, half, me_ref, a_ref, g_ref, u_ref, keep_ref, send_ref, full_ref):
    j = pl.program_id(0)

    @pl.when(j < half)
    def _():
        full_ref[...] = dot_f32(a_ref[...], g_ref[...], TN)

    @pl.when(j >= half)
    def _():
        full_ref[...] = dot_f32(a_ref[...], u_ref[...], TN)

    rows = full_ref.shape[0] // n_g
    for r_g in range(n_g):
        at = pl.multiple_of((me_ref[0] ^ r_g) * rows, rows)
        out = send_ref if r_g & 1 else keep_ref
        out[r_g // 2] = full_ref[pl.ds(at, rows), :].astype(BF16)


def gate_up_grad(me, rows, dg, du, n_g):
    total, width = rows.shape
    ff = dg.shape[1]
    tile = 256
    half = ff // tile
    spec = pl.BlockSpec((n_g // 2, width // n_g, tile), lambda j, m: (0, 0, j))
    return pl.pallas_call(
        functools.partial(gate_up_kernel, n_g, half),
        grid_spec=pltpu.PrefetchScalarGridSpec(
            num_scalar_prefetch=1,
            grid=(2 * half,),
            in_specs=[
                pl.BlockSpec((total, width), lambda j, m: (0, 0)),
                pl.BlockSpec((total, tile), lambda j, m: (0, jnp.minimum(j, half - 1))),
                pl.BlockSpec((total, tile), lambda j, m: (0, jnp.maximum(j - half, 0))),
            ],
            out_specs=[spec, spec],
            scratch_shapes=[pltpu.VMEM((width, tile), F32)],
        ),
        out_shape=[jax.ShapeDtypeStruct((n_g // 2, width // n_g, 2 * ff), BF16)] * 2,
        compiler_params=params(),
        cost_estimate=cost(4 * total * width * ff, 2 * total * (width + 2 * ff) + 4 * width * ff),
        name="gate_up_grad",
    )(me, rows, dg, du)


def halve_groups(keep, send, n_g):
    bits = [1 << i for i in range(n_g.bit_length() - 1)]
    got = xor_send(send, "grp", bits[0])
    total = keep.astype(F32) + got.astype(F32)
    for k in bits[:0:-1]:
        low = total.astype(BF16)
        half = low.shape[0] // 2
        got = xor_send(low[half:], "grp", k)
        total = low[:half].astype(F32) + got.astype(F32)
    return total[0]


def allowed_mask(seq_span):
    query_index = lax.broadcasted_iota(jnp.int32, (LENGTH, LENGTH), 0)
    key_index = lax.broadcasted_iota(jnp.int32, (LENGTH, LENGTH), 1)
    span_end = seq_span[0] + seq_span[1]
    inside = (
        (query_index >= seq_span[0])
        & (query_index < span_end)
        & (key_index >= seq_span[0])
        & (key_index < span_end)
    )
    return (key_index <= query_index) | inside


def split_heads(qkv_seq):
    split_view = qkv_seq.reshape(qkv_seq.shape[0], 3, HEADS, qkv_seq.shape[1] // (3 * HEADS))
    return (split_view[:, 0], split_view[:, 1], split_view[:, 2])


def scores_of(query_heads, key_heads, rel_bias, seq_span, score_scale):
    raw_scores = (
        jnp.einsum("qhd,khd->hqk", query_heads, key_heads, preferred_element_type=F32) * score_scale
        + rel_bias
    )
    return jnp.where(allowed_mask(seq_span)[None], raw_scores, -1e30)


def attention_forward(qkv_seq, seq_span, rel_bias, score_scale):
    query_heads, key_heads, value_heads = split_heads(qkv_seq)
    scores = scores_of(query_heads, key_heads, rel_bias, seq_span, score_scale)
    row_max = jnp.max(scores, axis=-1, keepdims=True)
    exp_scores = jnp.exp(scores - row_max)
    row_total = jnp.sum(exp_scores, axis=-1, keepdims=True)
    attn_probs = (exp_scores / row_total).astype(BF16)
    mixed_heads = jnp.einsum("hqk,khd->qhd", attn_probs, value_heads, preferred_element_type=F32)
    return (
        mixed_heads.reshape(LENGTH, -1).astype(BF16),
        row_max[..., 0] + jnp.log(row_total[..., 0]),
    )


def attention_backward(qkv_seq, grad_seq, seq_span, seq_total, rel_bias, score_scale):
    query_heads, key_heads, value_heads = split_heads(qkv_seq)
    grad_heads = grad_seq.reshape(LENGTH, HEADS, -1)
    scores = scores_of(query_heads, key_heads, rel_bias, seq_span, score_scale)
    attn_probs = jnp.exp(scores - seq_total[..., None])
    probs_low = attn_probs.astype(BF16)
    grad_value = jnp.einsum(
        "hqk,qhd->khd", probs_low, grad_heads, preferred_element_type=F32
    ).astype(BF16)
    grad_probs = jnp.einsum("qhd,khd->hqk", grad_heads, value_heads, preferred_element_type=F32)
    grad_scores = attn_probs * (
        grad_probs - jnp.sum(attn_probs * grad_probs, axis=-1, keepdims=True)
    )
    grad_low = grad_scores.astype(BF16)
    grad_query = (
        jnp.einsum("hqk,khd->qhd", grad_low, key_heads, preferred_element_type=F32) * score_scale
    ).astype(BF16)
    grad_key = (
        jnp.einsum("hqk,qhd->khd", grad_low, query_heads, preferred_element_type=F32) * score_scale
    ).astype(BF16)
    joined = jnp.stack([grad_query, grad_key, grad_value], axis=1).reshape(LENGTH, -1)
    return (grad_low, joined)


def norm_forward(values):
    inverse = lax.rsqrt(jnp.mean(values * values, axis=-1, keepdims=True) + EPSILON)
    return (values * inverse, inverse)


def norm_backward(grad_out, normed, inverse, norm_gain):
    grad_normed = grad_out * norm_gain
    grad_gain = jnp.sum(grad_out * normed, axis=0)
    grad_input = inverse * (
        grad_normed - normed * jnp.mean(grad_normed * normed, axis=-1, keepdims=True)
    )
    return (grad_input, grad_gain)


def body(
    tokens,
    cotangent,
    w_qkv,
    w_out_attn,
    rel_bias,
    norm_gains,
    w_router,
    w_gate_up,
    w_expert_out,
    routes,
    spans,
):
    tok, width = tokens.shape
    n_g, n_e = lax.axis_size("grp"), lax.axis_size("ep")
    assert w_gate_up.shape[0] == 1 and spans.shape[0] == 1 and tok == LENGTH
    assert n_g & (n_g - 1) == 0 and n_e & (n_e - 1) == 0 and n_g > 1 and n_e > 3
    experts = n_e
    ff = w_expert_out.shape[1]
    cap = 5 * routes.shape[1] * tok // (4 * experts)
    slots = experts * cap
    score_scale = 1.0 / math.sqrt(width // HEADS)
    me_g, me_e = lax.axis_index("grp"), lax.axis_index("ep")
    me = jnp.stack([me_g, me_e]).astype(jnp.int32)
    steps = halving_steps(n_g, n_e)
    w_gu, w_eo = w_gate_up[0], w_expert_out[0]

    flipped = (routes ^ me_e).T
    ids = lax.broadcasted_iota(jnp.int32, (experts, tok), 0)
    named = [ids == flipped[k : k + 1] for k in range(2)]
    counts = (named[0] | named[1]).astype(BF16)
    before = lax.broadcasted_iota(jnp.int32, (tok, tok), 0) < lax.broadcasted_iota(
        jnp.int32, (tok, tok), 1
    )
    earlier = dot_f32(counts, before.astype(BF16), NN)
    pos_rows = jnp.stack(
        [
            jnp.sum(jnp.where(one, earlier, 0.0), axis=0).astype(jnp.int32) + flipped[k] * cap
            for k, one in enumerate(named)
        ]
    )
    pos_cols = pos_rows.T

    cot_parts = dispatch(pos_rows, cotangent, cap, n_e)
    cot_rows = jnp.concatenate(
        [cot_parts[0]] + [xor_send(cot_parts[k], "ep", k) for k in range(1, n_e)]
    )

    hidden = tokens.astype(F32)
    normed_one, inverse_one = norm_forward(hidden)
    a_one = (normed_one * norm_gains[0]).astype(BF16)
    qkv_rows = dot_f32(a_one, w_qkv, NN).astype(BF16)
    mixed_heads, log_total = attention_forward(qkv_rows, spans[0], rel_bias, score_scale)
    after_attn = hidden + dot_f32(mixed_heads, w_out_attn, NN)
    normed_two, _ = norm_forward(after_attn)
    a_two = (normed_two * norm_gains[1]).astype(BF16)

    parts = dispatch(pos_rows, a_two, cap, n_e)
    parts = [parts[0]] + [xor_send(parts[k], "ep", k) for k in range(1, n_e)]
    dact = dot_f32(cot_rows, w_eo, NT)
    wr_pad = jnp.pad(w_router, ((0, 0), (0, LANES - experts)))
    wr_pad_t = wr_pad.T
    state, dls, owns, back = None, [], [], []
    for lo, hi in ((0, n_e // 2), (n_e // 2, 3 * n_e // 4), (3 * n_e // 4, n_e)):
        state, dl, own, outs = expert_chunk(
            me[1:], jnp.concatenate(parts[lo:hi]), dact, w_gu, wr_pad, wr_pad_t, experts, cap, lo * cap, slots, state
        )
        dls.append(dl)
        owns.append(own)
        for k in range(lo, hi):
            back.append(outs[k - lo] if k == 0 else xor_send(outs[k - lo], "ep", k))
    act, dg, du = state
    rows = jnp.concatenate(parts)
    own = jnp.concatenate(owns)[:, :1]
    grad_route = dot_f32(rows, jnp.concatenate(dls), TN)[:, :experts]

    gated = (dot_f32(act, w_eo, NN) * own).astype(BF16).reshape(n_e, cap, width)
    gated = [gated[0]] + [xor_send(gated[k], "ep", k) for k in range(1, n_e)]
    deo = (cot_rows.astype(F32) * own).astype(BF16)
    grad_eo = dot_f32(act, deo, TN).astype(BF16)
    grad_eo = grad_eo.reshape(n_g, ff // n_g, width)
    grad_eo = [lax.dynamic_index_in_dim(grad_eo, me_g ^ r, 0, keepdims=False) for r in range(n_g)]
    grad_w_expert = halve_groups(jnp.stack(grad_eo[0::2]), jnp.stack(grad_eo[1::2]), n_g)[None]
    grad_w_gate = halve_groups(*gate_up_grad(me[:1], rows, dg, du, n_g), n_g)[None]

    grad_after, grad_attn_low, grad_gain_two = return_grads(
        pos_cols, after_attn, cotangent, norm_gains[1:], back, cap
    )
    output = combine(pos_cols, after_attn, gated, cap)
    g_attn = wgrad(me, mixed_heads, grad_attn_low, n_g, n_e, steps)
    grad_mixed = dot_f32(grad_attn_low, w_out_attn, NT).astype(BF16)
    grad_bias, grad_qkv = attention_backward(
        qkv_rows, grad_mixed, spans[0], log_total, rel_bias, score_scale
    )
    hpe, rpg = HEADS // n_e, LENGTH // n_g
    bias_view = grad_bias.reshape(n_e, hpe, n_g, rpg, LENGTH)
    bias_view = relative(relative(bias_view, 0, me_e, n_e), 2, me_g, n_g)
    bias_blocks = {
        (r_g, r_e): bias_view[r_e, :, r_g] for r_g in range(n_g) for r_e in range(n_e)
    }
    g_bias = split_steps(steps, bias_blocks, n_g, n_e)
    g_qkv = wgrad(me, a_one, grad_qkv, n_g, n_e, steps)
    grad_a_one = dot_f32(grad_qkv, w_qkv, NT)
    grad_norm_one, grad_gain_one = norm_backward(grad_a_one, normed_one, inverse_one, norm_gains[0])
    grad_tokens = grad_after + grad_norm_one
    early = butterfly(jnp.concatenate([grad_gain_two, grad_route.T]), n_g, n_e)
    late = butterfly(grad_gain_one[None], n_g, n_e)
    return (
        output,
        grad_tokens,
        halve(*g_qkv, steps),
        halve(*g_attn, steps),
        halve(*g_bias, steps),
        jnp.concatenate([late, early[:1]]),
        early[1:].T,
        grad_w_gate,
        grad_w_expert,
    )


def solution(mesh):
    placed = (
        P(("grp", "ep"), None),
        P(("grp", "ep"), None),
        P(),
        P(),
        P(),
        P(),
        P(),
        P("ep", None, None),
        P("ep", None, None),
        P(("grp", "ep"), None),
        P(("grp", "ep"), None),
    )
    return jax.shard_map(
        body,
        mesh=mesh,
        in_specs=placed,
        out_specs=(
            P(("grp", "ep"), None),
            P(("grp", "ep"), None),
            P("grp", "ep"),
            P("grp", "ep"),
            P("ep", "grp", None),
            P(),
            P(),
            P("ep", "grp", None),
            P("ep", "grp", None),
        ),
        check_vma=False,
    )
```

time: 1010 us -> 729 us (0.72)
  waiting for transfers between devices: 526 us -> 212 us
  Pallas kernels: 0 us -> 145 us
  matrix products: 205 us -> 105 us
  starting transfers between devices: 21.1 us -> 108 us
  local copies, waits for them, and re-layouts: 116 us -> 68.9 us
  blocking collectives: 40.8 us -> 0 us
  between operations: 16.4 us -> 3.73 us
    reduce_scatter x5 -> x0, waiting for transfers between devices: 257 us -> none  [the longest x1 124 us: body(): lax.psum_scatter(grad_bias.astype(jnp.bfloat16), 'ep', scatter_dimension=...]
    ppermute x0 -> x57, waiting for transfers between devices: none -> 212 us  [xor_send(): return lax.ppermute(v, axis, [(i, i ^ k) for i in range(n)])]
    pallas_call x0 -> x10, Pallas kernels: none -> 145 us  [the longest x3 76.8 us: expert_chunk(): out = call(*args, *(earlier if aliased else ()))]
    all_to_all x4 -> x0, waiting for transfers between devices: 136 us -> none  [the longest x1 36.9 us: body(): lax.all_to_all(expert_rows, 'ep', split_axis=0, concat_axis=0, tiled=True)]
    unnamed x11 -> x0, waiting for transfers between devices: 134 us -> none
    ppermute x0 -> x57, starting transfers between devices: none -> 108 us  [xor_send(): return lax.ppermute(v, axis, [(i, i ^ k) for i in range(n)])]
    dot_general x20 -> x14, matrix products: 191 us -> 96.8 us  [the longest x9 62.7 us: dot_f32(): return lax.dot_general(a, b, (dims, ((), ())), preferred_element_type=F32)]
    psum x1 -> x0, blocking collectives: 40.8 us -> none  [body(): lax.psum((jnp.stack([grad_gain_one, grad_gain_two]), grad_w_route), ('grp...]
  transfers between devices with their start and end apart: 12 -> 57, of which waited for: 11 -> 21; matrix products, arithmetic and copies ran while one was open for 23% -> 23% of each run, Pallas kernels for 0% -> 17%
where the time goes in v1:
time: 729 us; the launch traced here: 720 us
  waiting for transfers between devices  212 us (29%)
  Pallas kernels  145 us (20%)
  starting transfers between devices  108 us (15%)
  matrix products  105 us (14%)
  other arithmetic  77.3 us (11%)
  local copies, waits for them, and re-layouts  68.9 us (9%)
    ppermute x57, waiting for transfers between devices, xor_send(): return lax.ppermute(v, axis, [(i, i ^ k) for i in range(n)])  212 us
    ppermute x57, starting transfers between devices, xor_send(): return lax.ppermute(v, axis, [(i, i ^ k) for i in range(n)])  108 us
    pallas_call x3, Pallas kernels, expert_chunk(): out = call(*args, *(earlier if aliased else ()))  76.8 us
    dot_general x9, matrix products, dot_f32(): return lax.dot_general(a, b, (dims, ((), ())), preferred_element_type=F32)  62.7 us
    unnamed x156, local copies, waits for them, and re-layouts  33.9 us
    pallas_call x1, Pallas kernels, gate_up_grad(): pl.pallas_call(functools.partial(gate_up_kernel, n_g, half), grid_spec=pl...  28.2 us
    pallas_call x2, Pallas kernels, wgrad(): pl.pallas_call(functools.partial(wgrad_kernel, n_g, steps), grid_spec=plt...  20 us
  transfers between devices with their start and end apart: 57, of which 21 were waited for; matrix products, arithmetic and copies ran while one was open for 23% of the time, Pallas kernels for 17%

profile of v1, /device:TPU:0, one launch (start us, length us, event | category | flops | bytes accessed | tf_op | source)
XLA Modules:
  0.0 720.0 jit_solution(12413556969605193840)
XLA Ops:
  9.5 7.5 %convolution_convert_fusion.1 = bf16[512,3072]{1,0:T(8,128)(2,1)} fusion(bf16[512,1024]{1,0:T(8,128)(2,1)S(1)} %fusion.19.a_ref, bf16[1024,3072]{1,0:T(8,128)(2,1)} %param.13), kind=kOutput, calls=%fused_computation.23 | convolution fusion | flops 3222798336 | bytes 10485760 | tf_op jit(solution)/shard_map/dot_general | solution.py:31
  21.9 8.4 %fusion.58 = (f32[16,512]{1,0:T(8,128)S(1)}, f32[16,512,512]{2,1,0:T(8,128)S(1)}) fusion(bf16[16,512,512]{2,1,0:T(8,128)(2,1)} %param.15, bf16[512,3,16,64]{0,3,2,1:T(8,128)(2,1)} %bitcast.368, pred[512,512]{1,0:T(8,128)(4,1)S(1)} %fusion.39), kind=kOutput, calls=%fused_computation.234 | convolution fusion | flops 557834240 | bytes 27557888 | tf_op jit(solution)/shard_map/qhd,khd->hqk/dot_general | solution.py:438
  36.2 6.2 fusion.28
  79.0 5.7 collective-permute-done.4
  88.4 20.5 %collective-permute-done.5 = bf16[160,1024]{1,0:T(8,128)(2,1)S(1)} collective-permute-done((bf16[160,1024]{1,0:T(8,128)(2,1)}, bf16[160,1024]{1,0:T(8,128)(2,1)S(1)}, u32[]{:S(2)}, u32[]{:S(2)}) %collective-permute-start.5) | collective-permute-done | bytes 327712 | tf_op jit(solution)/shard_map/ppermute | solution.py:41
  120.2 12.5 %collective-permute-start.10 = (bf16[160,1024]{1,0:T(8,128)(2,1)}, bf16[160,1024]{1,0:T(8,128)(2,1)S(1)}, u32[]{:S(2)}, u32[]{:S(2)}) collective-permute-start(bf16[160,1024]{1,0:T(8,128)(2,1)} %get-tuple-element.68), channel_id=1, source_target_pairs={{0,5},{1,4},{2,7},{3,6},{4,1},{5,0},{6,3},{7,2},{8,13},{9,12},{10,... | collective-permute-start | bytes 983048 | tf_op jit(solution)/shard_map/ppermute | solution.py:41
  133.5 11.7 %collective-permute-start.9 = (bf16[160,1024]{1,0:T(8,128)(2,1)}, bf16[160,1024]{1,0:T(8,128)(2,1)S(1)}, u32[]{:S(2)}, u32[]{:S(2)}) collective-permute-start(bf16[160,1024]{1,0:T(8,128)(2,1)} %get-tuple-element.67), channel_id=1, source_target_pairs={{0,4},{1,5},{2,6},{3,7},{4,0},{5,1},{6,2},{7,3},{8,12},{9,13},{10,... | collective-permute-start | bytes 983048 | tf_op jit(solution)/shard_map/ppermute | solution.py:41
  146.0 13.8 %fusion.8.refs_2_ = f32[1280,2816]{1,0:T(8,128)} fusion(bf16[1280,1024]{1,0:T(8,128)(2,1)} %constant_dynamic-update-slice_fusion, bf16[1,2816,1024]{2,1,0:T(8,128)(2,1)} %param.19), kind=kOutput, calls=%fused_computation.16 | convolution fusion | flops 7381975040 | bytes 22806528 | tf_op jit(solution)/shard_map/dot_general | solution.py:31
  168.7 35.5 %expert_rows.3 = (bf16[1280,2816]{1,0:T(8,128)(2,1)}, bf16[1280,2816]{1,0:T(8,128)(2,1)}, bf16[1280,2816]{1,0:T(8,128)(2,1)}, bf16[640,128]{1,0:T(8,128)(2,1)}, ...) custom-call(s32[1]{0:T(128)} %bitcast.15.refs_0_, ...), custom_call_target="tpu_custom_call" | custom-call | flops 14763950080 | bytes 32178176 | tf_op jit(solution)/shard_map/expert_rows/pallas_call | solution.py:295
  205.1 20.6 %expert_rows.4 = (bf16[1280,2816]{1,0:T(8,128)(2,1)}, bf16[1280,2816]{1,0:T(8,128)(2,1)}, bf16[1280,2816]{1,0:T(8,128)(2,1)}, bf16[320,128]{1,0:T(8,128)(2,1)}, ...) custom-call(s32[1]{0:T(128)} %bitcast.15.refs_0_, ...), custom_call_target="tpu_custom_call", output_to_operand_aliasing={{0}: (7, {}), {1}: (8, {}), {2}: (9, {})} | custom-call | flops 7381975040 | bytes 21856256 | tf_op jit(solution)/shard_map/expert_rows/pallas_call | solution.py:295
  227.6 20.7 %expert_rows.5 = (bf16[1280,2816]{1,0:T(8,128)(2,1)}, bf16[1280,2816]{1,0:T(8,128)(2,1)}, bf16[1280,2816]{1,0:T(8,128)(2,1)}, bf16[320,128]{1,0:T(8,128)(2,1)}, ...) custom-call(s32[1]{0:T(128)} %bitcast.15.refs_0_, ...), custom_call_target="tpu_custom_call", output_to_operand_aliasing={{0}: (7, {}), {1}: (8, {}), {2}: (9, {})} | custom-call | flops 7381975040 | bytes 21856256 | tf_op jit(solution)/shard_map/expert_rows/pallas_call | solution.py:295
  249.7 13.3 %convolution_convert_fusion = bf16[2816,1024]{1,0:T(8,128)(2,1)} fusion(bf16[1280,2816]{1,0:T(8,128)(2,1)} %get-tuple-element.79, bf16[1280,1024]{1,0:T(8,128)(2,1)} %constant_dynamic-update-slice_fusion, f32[1280]{0:T(1024)S(1)} %fusion.43), kind=kOutput, calls=%fused_computation.20 | convolution fusion | flops 7388790784 | bytes 15602688 | tf_op jit(solution)/shard_map/dot_general | solution.py:31
  263.1 11.4 %multiply_convert_fusion.2 = bf16[1280,1024]{1,0:T(8,128)(2,1)} fusion(bf16[1280,2816]{1,0:T(8,128)(2,1)S(1)} %bitcast.367, bf16[1,2816,1024]{2,1,0:T(8,128)(2,1)} %param.19, f32[1280]{0:T(1024)S(1)} %fusion.43), kind=kOutput, calls=%fused_computation.22 | convolution fusion | flops 7384596480 | bytes 15602688 | tf_op jit(solution)/shard_map/dot_general | solution.py:31
  276.3 5.8 collective-permute-start.25
  289.4 28.2 %gate_up_grad.1 = (bf16[2,256,5632]{2,1,0:T(8,128)(2,1)}, bf16[2,256,5632]{2,1,0:T(8,128)(2,1)}) custom-call(s32[1]{0:T(128)} %bitcast.28.me_ref, bf16[1280,1024]{1,0:T(8,128)(2,1)} %constant_dynamic-update-slice_fusion.8.a_ref, bf16[1280,2816]{1,0:T(8,128)(2,1)} %get-tuple-element.101.g_ref, bf16[1280,2816]{1,0:T(8,128)(2,1)} %get-tuple-element.102.u_ref), custom_call_target="tpu_custom_call" | custom-call | flops 14763950080 | bytes 28573696 | tf_op jit(solution)/shard_map/gate_up_grad/pallas_call | solution.py:386
  338.3 7.1 return_rows.1
  350.3 12.4 %multiply_reduce_fusion = (f32[16,512]{1,0:T(8,128)S(1)}, f32[16,512,512]{2,1,0:T(8,128)}) fusion(f32[16,512,512]{2,1,0:T(8,128)} %copy-done.1, f32[16,512]{1,0:T(8,128)S(1)} %log_add_fusion, bf16[512,16,64]{0,2,1:T(8,128)(2,1)S(1)} %bitcast.375, bf16[512,3,16,64]{0,3,2,1:T(8,128)(2,1)} %bitcast.370), kind=kOutput, calls=%fused_computation.1 | convolution fusion | flops 549445632 | bytes 35717120 | tf_op jit(solution)/shard_map/qhd,khd->hqk/dot_general | solution.py:467
  362.8 12.3 %multiply_convert_fusion = bf16[16,512,512]{2,1,0:T(8,128)(2,1)S(1)} fusion(f32[16,512,512]{2,1,0:T(8,128)} %get-tuple-element.166, f32[16,512,512]{2,1,0:T(8,128)} %copy-done.1, f32[16,512]{1,0:T(8,128)S(1)} %get-tuple-element.165, f32[16,512]{1,0:T(8,128)S(1)} %log_add_fusion), kind=kLoop, calls=%fused_computation | loop fusion | flops 16777216 | bytes 42008576 | tf_op jit(solution)/shard_map/convert_element_type | solution.py:471
  375.1 8.3 %fusion.32 = bf16[512,1,16,64]{0,3,2,1:T(8,128)(2,1)} fusion(bf16[16,512,512]{2,1,0:T(8,128)(2,1)S(1)} %multiply_convert_fusion, bf16[512,3,16,64]{0,3,2,1:T(8,128)(2,1)} %bitcast.371), kind=kOutput, calls=%fused_computation.67 | convolution fusion | flops 537919488 | bytes 10485760 | tf_op jit(solution)/shard_map/hqk,khd->qhd/dot_general | solution.py:473
  392.7 8.0 %fusion.24 = (f32[1024]{0:T(1024)S(1)}, f32[512]{0:T(512)S(1)}, f32[512,1024]{1,0:T(8,128)}) fusion(bf16[512,1024]{1,0:T(8,128)(2,1)S(1)} %copy-done.4, f32[512]{0:T(512)S(1)} %copy-done.53, f32[1024]{0:T(1024)S(1)} %bitcast.383, bf16[512,3072]{0,1:T(8,128)(2,1)S(1)} %bitcast.373, bf16[1024,3072]{1,0:T(8,128)(2,1)} %param.13), kind=kOutput, calls=%fused_computation.45 | convolution fusion | flops 3224893952 | bytes 12595200 | tf_op jit(solution)/shard_map/dot_general | solution.py:31
  422.4 11.2 %weight_grad.2 = (bf16[2,2,2,2,256,384]{5,4,3,2,1,0:T(8,128)(2,1)}, bf16[2,2,2,2,256,384]{5,4,3,2,1,0:T(8,128)(2,1)}) custom-call(s32[2]{0:T(128)} %pad_add_fusion.1.me_ref, bf16[512,1024]{1,0:T(8,128)(2,1)} %copy-done.30, bf16[512,3072]{1,0:T(8,128)(2,1)} %copy.73.b_ref), custom_call_target="tpu_custom_call" | custom-call | flops 3221225472 | bytes 10485760 | tf_op jit(solution)/shard_map/weight_grad/pallas_call | solution.py:343
  437.9 8.8 %weight_grad.3 = (bf16[2,2,2,2,256,128]{5,4,3,2,1,0:T(8,128)(2,1)}, bf16[2,2,2,2,256,128]{5,4,3,2,1,0:T(8,128)(2,1)}) custom-call(s32[2]{0:T(128)} %pad_add_fusion.1.me_ref, bf16[512,1024]{1,0:T(8,128)(2,1)} %copy.74.a_ref, bf16[512,1024]{1,0:T(8,128)(2,1)} %get-tuple-element.92.b_ref), custom_call_target="tpu_custom_call" | custom-call | flops 1073741824 | bytes 4194304 | tf_op jit(solution)/shard_map/weight_grad/pallas_call | solution.py:343
  459.3 12.3 %collective-permute-done.16.refs_3_ = bf16[160,1024]{1,0:T(8,128)(2,1)S(1)} collective-permute-done((bf16[160,1024]{1,0:T(8,128)(2,1)S(1)}, bf16[160,1024]{1,0:T(8,128)(2,1)S(1)}, u32[]{:S(2)}, u32[]{:S(2)}) %collective-permute-start.16) | collective-permute-done | bytes 327712 | tf_op jit(solution)/shard_map/ppermute | solution.py:41
  482.8 23.0 %collective-permute-done.18.refs_5_ = bf16[160,1024]{1,0:T(8,128)(2,1)S(1)} collective-permute-done((bf16[160,1024]{1,0:T(8,128)(2,1)S(1)}, bf16[160,1024]{1,0:T(8,128)(2,1)S(1)}, u32[]{:S(2)}, u32[]{:S(2)}) %collective-permute-start.18) | collective-permute-done | bytes 327712 | tf_op jit(solution)/shard_map/ppermute | solution.py:41
  508.3 12.1 %collective-permute-start.46 = (f32[1,1024]{1,0:T(1,128)S(1)}, f32[1,1024]{1,0:T(1,128)S(1)}, u32[]{:S(2)}, u32[]{:S(2)}) collective-permute-start(f32[1,1024]{1,0:T(1,128)S(1)} %add.215), channel_id=1, source_target_pairs={{0,2},{1,3},{2,0},{3,1},{4,6},{5,7},{6,4},{7,5},{8,10},{9,11},{10,... | collective-permute-start | bytes 12296 | tf_op jit(solution)/shard_map/ppermute | solution.py:41
  561.4 22.3 %collective-permute-done.29 = bf16[2,2,2,256,384]{4,3,2,1,0:T(8,128)(2,1)S(1)} collective-permute-done((bf16[2,2,2,256,384]{4,3,2,1,0:T(8,128)(2,1)S(1)}, bf16[2,2,2,256,384]{4,3,2,1,0:T(8,128)(2,1)S(1)}, u32[]{:S(2)}, u32[]{:S(2)}) %collective-permute-start.29) | collective-permute-done | bytes 1572896 | tf_op jit(solution)/shard_map/ppermute | solution.py:41
  585.6 42.3 %collective-permute-done.39 = bf16[2,2,2,2,128,512]{5,4,3,2,1,0:T(8,128)(2,1)S(1)} collective-permute-done((bf16[2,2,2,2,128,512]{5,4,3,2,1,0:T(8,128)(2,1)S(1)}, bf16[2,2,2,2,128,512]{5,4,3,2,1,0:T(8,128)(2,1)S(1)}, u32[]{:S(2)}, u32[]{:S(2)}) %collective-permute-start.39) | collective-permute-done | bytes 2097184 | tf_op jit(solution)/shard_map/ppermute | solution.py:41
  630.3 5.7 add_convert_fusion
  639.3 16.9 %collective-permute-done.40 = bf16[2,2,2,128,512]{4,3,2,1,0:T(8,128)(2,1)} collective-permute-done((bf16[2,2,2,128,512]{4,3,2,1,0:T(8,128)(2,1)}, bf16[2,2,2,128,512]{4,3,2,1,0:T(8,128)(2,1)}, u32[]{:S(2)}, u32[]{:S(2)}) %collective-permute-start.40) | collective-permute-done | bytes 1048608 | tf_op jit(solution)/shard_map/ppermute | solution.py:41
  660.9 11.8 %collective-permute-done.41 = bf16[2,2,128,512]{3,2,1,0:T(8,128)(2,1)S(1)} collective-permute-done((bf16[2,2,128,512]{3,2,1,0:T(8,128)(2,1)S(1)}, bf16[2,2,128,512]{3,2,1,0:T(8,128)(2,1)S(1)}, u32[]{:S(2)}, u32[]{:S(2)}) %collective-permute-start.41) | collective-permute-done | bytes 524320 | tf_op jit(solution)/shard_map/ppermute | solution.py:41
  677.3 7.6 %collective-permute-done.42 = bf16[2,128,512]{2,1,0:T(8,128)(2,1)S(1)} collective-permute-done((bf16[2,128,512]{2,1,0:T(8,128)(2,1)S(1)}, bf16[2,128,512]{2,1,0:T(8,128)(2,1)S(1)}, u32[]{:S(2)}, u32[]{:S(2)}) %collective-permute-start.42) | collective-permute-done | bytes 262176 | tf_op jit(solution)/shard_map/ppermute | solution.py:41
  685.7 30.5 %collective-permute-done.54 = bf16[1,256,5632]{2,1,0:T(8,128)(2,1)S(1)} collective-permute-done((bf16[1,256,5632]{2,1,0:T(8,128)(2,1)S(1)}, bf16[1,256,5632]{2,1,0:T(8,128)(2,1)S(1)}, u32[]{:S(2)}, u32[]{:S(2)}) %collective-permute-start.54) | collective-permute-done | bytes 2883616 | tf_op jit(solution)/shard_map/ppermute | solution.py:41
  (382 shorter events, 241.8 us)
Async XLA Ops:
  52.3 107.5 %collective-permute-start.11 = (bf16[160,1024]{1,0:T(8,128)(2,1)}, bf16[160,1024]{1,0:T(8,128)(2,1)S(1)}, u32[]{:S(2)}, u32[]{:S(2)}) collective-permute-start(bf16[160,1024]{1,0:T(8,128)(2,1)} %get-tuple-element.70), channel_id=1, source_target_pairs={{0,1},{1,0},{2,3},{3,2},{4,5},{5,4},{6,7},{7,6},{8,9},{9,8},{10,11... | collective-permute-start | bytes 983048 | tf_op jit(solution)/shard_map/ppermute | solution.py:41
  55.3 106.9 %collective-permute-start.12 = (bf16[160,1024]{1,0:T(8,128)(2,1)}, bf16[160,1024]{1,0:T(8,128)(2,1)}, u32[]{:S(2)}, u32[]{:S(2)}) collective-permute-start(bf16[160,1024]{1,0:T(8,128)(2,1)} %get-tuple-element.71), channel_id=1, source_target_pairs={{0,2},{1,3},{2,0},{3,1},{4,6},{5,7},{6,4},{7,5},{8,10},{9,11},{10,... | collective-permute-start | bytes 983048 | tf_op jit(solution)/shard_map/ppermute | solution.py:41
  72.7 36.3 %collective-permute-start.5 = (bf16[160,1024]{1,0:T(8,128)(2,1)}, bf16[160,1024]{1,0:T(8,128)(2,1)S(1)}, u32[]{:S(2)}, u32[]{:S(2)}) collective-permute-start(bf16[160,1024]{1,0:T(8,128)(2,1)} %get-tuple-element.63), channel_id=1, source_target_pairs={{0,4},{1,5},{2,6},{3,7},{4,0},{5,1},{6,2},{7,3},{8,12},{9,13},{10,... | collective-permute-start | bytes 983048 | tf_op jit(solution)/shard_map/ppermute | solution.py:41
  77.0 40.6 %collective-permute-start.6 = (bf16[160,1024]{1,0:T(8,128)(2,1)}, bf16[160,1024]{1,0:T(8,128)(2,1)S(1)}, u32[]{:S(2)}, u32[]{:S(2)}) collective-permute-start(bf16[160,1024]{1,0:T(8,128)(2,1)} %get-tuple-element.64), channel_id=1, source_target_pairs={{0,5},{1,4},{2,7},{3,6},{4,1},{5,0},{6,3},{7,2},{8,13},{9,12},{10,... | collective-permute-start | bytes 983048 | tf_op jit(solution)/shard_map/ppermute | solution.py:41
  84.7 35.5 %collective-permute-start.7 = (bf16[160,1024]{1,0:T(8,128)(2,1)}, bf16[160,1024]{1,0:T(8,128)(2,1)S(1)}, u32[]{:S(2)}, u32[]{:S(2)}) collective-permute-start(bf16[160,1024]{1,0:T(8,128)(2,1)} %get-tuple-element.65), channel_id=1, source_target_pairs={{0,6},{1,7},{2,4},{3,5},{4,2},{5,3},{6,0},{7,1},{8,14},{9,15},{10,... | collective-permute-start | bytes 983048 | tf_op jit(solution)/shard_map/ppermute | solution.py:41
  117.6 49.0 %collective-permute-start.13 = (bf16[160,1024]{1,0:T(8,128)(2,1)S(1)}, bf16[160,1024]{1,0:T(8,128)(2,1)S(1)}, u32[]{:S(2)}, u32[]{:S(2)}) collective-permute-start(bf16[160,1024]{1,0:T(8,128)(2,1)S(1)} %copy-done.57), channel_id=1, source_target_pairs={{0,3},{1,2},{2,1},{3,0},{4,7},{5,6},{6,5},{7,4},{8,11},{9,10},{10,... | collective-permute-start | bytes 983048 | tf_op jit(solution)/shard_map/ppermute | solution.py:41
  120.2 83.9 %collective-permute-start.10 = (bf16[160,1024]{1,0:T(8,128)(2,1)}, bf16[160,1024]{1,0:T(8,128)(2,1)S(1)}, u32[]{:S(2)}, u32[]{:S(2)}) collective-permute-start(bf16[160,1024]{1,0:T(8,128)(2,1)} %get-tuple-element.68), channel_id=1, source_target_pairs={{0,5},{1,4},{2,7},{3,6},{4,1},{5,0},{6,3},{7,2},{8,13},{9,12},{10,... | collective-permute-start | bytes 983048 | tf_op jit(solution)/shard_map/ppermute | solution.py:41
  133.5 70.7 %collective-permute-start.9 = (bf16[160,1024]{1,0:T(8,128)(2,1)}, bf16[160,1024]{1,0:T(8,128)(2,1)S(1)}, u32[]{:S(2)}, u32[]{:S(2)}) collective-permute-start(bf16[160,1024]{1,0:T(8,128)(2,1)} %get-tuple-element.67), channel_id=1, source_target_pairs={{0,4},{1,5},{2,6},{3,7},{4,0},{5,1},{6,2},{7,3},{8,12},{9,13},{10,... | collective-permute-start | bytes 983048 | tf_op jit(solution)/shard_map/ppermute | solution.py:41
  159.8 65.8 %collective-permute-start = (bf16[160,1024]{1,0:T(8,128)(2,1)}, bf16[160,1024]{1,0:T(8,128)(2,1)S(1)}, u32[]{:S(2)}, u32[]{:S(2)}) collective-permute-start(bf16[160,1024]{1,0:T(8,128)(2,1)} %get-tuple-element.57), channel_id=1, source_target_pairs={{0,6},{1,7},{2,4},{3,5},{4,2},{5,3},{6,0},{7,1},{8,14},{9,15},{10,... | collective-permute-start | bytes 983048 | tf_op jit(solution)/shard_map/ppermute | solution.py:41
  162.2 63.5 %collective-permute-start.1 = (bf16[160,1024]{1,0:T(8,128)(2,1)}, bf16[160,1024]{1,0:T(8,128)(2,1)}, u32[]{:S(2)}, u32[]{:S(2)}) collective-permute-start(bf16[160,1024]{1,0:T(8,128)(2,1)} %get-tuple-element.58), channel_id=1, source_target_pairs={{0,7},{1,6},{2,5},{3,4},{4,3},{5,2},{6,1},{7,0},{8,15},{9,14},{10,... | collective-permute-start | bytes 983048 | tf_op jit(solution)/shard_map/ppermute | solution.py:41
  274.4 50.5 %collective-permute-start.26 = (bf16[160,1024]{1,0:T(8,128)(2,1)}, bf16[160,1024]{1,0:T(8,128)(2,1)}, u32[]{:S(2)}, u32[]{:S(2)}) collective-permute-start(bf16[160,1024]{1,0:T(8,128)(2,1)} %get-tuple-element.89), channel_id=1, source_target_pairs={{0,6},{1,7},{2,4},{3,5},{4,2},{5,3},{6,0},{7,1},{8,14},{9,15},{10,... | collective-permute-start | bytes 983048 | tf_op jit(solution)/shard_map/ppermute | solution.py:41
  275.9 49.1 %collective-permute-start.27 = (bf16[160,1024]{1,0:T(8,128)(2,1)}, bf16[160,1024]{1,0:T(8,128)(2,1)}, u32[]{:S(2)}, u32[]{:S(2)}) collective-permute-start(bf16[160,1024]{1,0:T(8,128)(2,1)} %get-tuple-element.90), channel_id=1, source_target_pairs={{0,7},{1,6},{2,5},{3,4},{4,3},{5,2},{6,1},{7,0},{8,15},{9,14},{10,... | collective-permute-start | bytes 983048 | tf_op jit(solution)/shard_map/ppermute | solution.py:41
  276.3 56.4 %collective-permute-start.24 = (bf16[160,1024]{1,0:T(8,128)(2,1)}, bf16[160,1024]{1,0:T(8,128)(2,1)}, u32[]{:S(2)}, u32[]{:S(2)}) collective-permute-start(bf16[160,1024]{1,0:T(8,128)(2,1)} %get-tuple-element.87), channel_id=1, source_target_pairs={{0,4},{1,5},{2,6},{3,7},{4,0},{5,1},{6,2},{7,3},{8,12},{9,13},{10,... | collective-permute-start | bytes 983048 | tf_op jit(solution)/shard_map/ppermute | solution.py:41
  276.3 56.4 %collective-permute-start.25 = (bf16[160,1024]{1,0:T(8,128)(2,1)}, bf16[160,1024]{1,0:T(8,128)(2,1)}, u32[]{:S(2)}, u32[]{:S(2)}) collective-permute-start(bf16[160,1024]{1,0:T(8,128)(2,1)} %get-tuple-element.88), channel_id=1, source_target_pairs={{0,5},{1,4},{2,7},{3,6},{4,1},{5,0},{6,3},{7,2},{8,13},{9,12},{10,... | collective-permute-start | bytes 983048 | tf_op jit(solution)/shard_map/ppermute | solution.py:41
  282.1 51.2 %collective-permute-start.21 = (bf16[160,1024]{1,0:T(8,128)(2,1)}, bf16[160,1024]{1,0:T(8,128)(2,1)}, u32[]{:S(2)}, u32[]{:S(2)}) collective-permute-start(bf16[160,1024]{1,0:T(8,128)(2,1)} %get-tuple-element.84), channel_id=1, source_target_pairs={{0,1},{1,0},{2,3},{3,2},{4,5},{5,4},{6,7},{7,6},{8,9},{9,8},{10,11... | collective-permute-start | bytes 983048 | tf_op jit(solution)/shard_map/ppermute | solution.py:41
  332.7 118.6 %collective-permute-start.14 = (bf16[160,1024]{1,0:T(8,128)(2,1)}, bf16[160,1024]{1,0:T(8,128)(2,1)}, u32[]{:S(2)}, u32[]{:S(2)}) collective-permute-start(bf16[160,1024]{1,0:T(8,128)(2,1)} %get-tuple-element.151), channel_id=1, source_target_pairs={{0,1},{1,0},{2,3},{3,2},{4,5},{5,4},{6,7},{7,6},{8,9},{9,8},{10,11... | collective-permute-start | bytes 983048 | tf_op jit(solution)/shard_map/ppermute | solution.py:41
  332.8 118.7 %collective-permute-start.15 = (bf16[160,1024]{1,0:T(8,128)(2,1)}, bf16[160,1024]{1,0:T(8,128)(2,1)}, u32[]{:S(2)}, u32[]{:S(2)}) collective-permute-start(bf16[160,1024]{1,0:T(8,128)(2,1)} %get-tuple-element.150), channel_id=1, source_target_pairs={{0,2},{1,3},{2,0},{3,1},{4,6},{5,7},{6,4},{7,5},{8,10},{9,11},{10,... | collective-permute-start | bytes 983048 | tf_op jit(solution)/shard_map/ppermute | solution.py:41
  405.6 41.1 %collective-permute-start.43 = (f32[1,1024]{1,0:T(1,128)S(1)}, f32[1,1024]{1,0:T(1,128)S(1)}, u32[]{:S(2)}, u32[]{:S(2)}) collective-permute-start(f32[1,1024]{1,0:T(1,128)S(1)} %bitcast.388), channel_id=1, source_target_pairs={{0,8},{8,0},{16,24},{24,16},{1,9},{9,1},{17,25},{25,17},{2,10},{10... | collective-permute-start | bytes 12296 | tf_op jit(solution)/shard_map/ppermute | solution.py:41
  421.9 124.5 %collective-permute-start.38 = (bf16[2,2,2,2,2,128,512]{6,5,4,3,2,1,0:T(8,128)(2,1)}, bf16[2,2,2,2,2,128,512]{6,5,4,3,2,1,0:T(8,128)(2,1)}, u32[]{:S(2)}, u32[]{:S(2)}) collective-permute-start(bf16[2,2,2,2,2,128,512]{6,5,4,3,2,1,0:T(8,128)(2,1)} %pad_maximum_fusion), channel_id=1, source_target_pairs={{0,8},{8,0},{16,24},{24,16},{1,9},{9,1},{17,25},{25,17},{2,10},{10... | collective-permute-start | bytes 12582920 | tf_op jit(solution)/shard_map/ppermute | solution.py:41
  433.6 108.5 %collective-permute-start.28 = (bf16[2,2,2,2,256,384]{5,4,3,2,1,0:T(8,128)(2,1)}, bf16[2,2,2,2,256,384]{5,4,3,2,1,0:T(8,128)(2,1)}, u32[]{:S(2)}, u32[]{:S(2)}) collective-permute-start(bf16[2,2,2,2,256,384]{5,4,3,2,1,0:T(8,128)(2,1)} %get-tuple-element.94), channel_id=1, source_target_pairs={{0,8},{8,0},{16,24},{24,16},{1,9},{9,1},{17,25},{25,17},{2,10},{10... | collective-permute-start | bytes 9437192 | tf_op jit(solution)/shard_map/ppermute | solution.py:41
  446.6 33.6 %collective-permute-start.33 = (bf16[2,2,2,2,256,128]{5,4,3,2,1,0:T(8,128)(2,1)}, bf16[2,2,2,2,256,128]{5,4,3,2,1,0:T(8,128)(2,1)S(1)}, u32[]{:S(2)}, u32[]{:S(2)}) collective-permute-start(bf16[2,2,2,2,256,128]{5,4,3,2,1,0:T(8,128)(2,1)} %get-tuple-element.96), channel_id=1, source_target_pairs={{0,8},{8,0},{16,24},{24,16},{1,9},{9,1},{17,25},{25,17},{2,10},{10... | collective-permute-start | bytes 3145736 | tf_op jit(solution)/shard_map/ppermute | solution.py:41
  475.2 30.7 %collective-permute-start.18 = (bf16[160,1024]{1,0:T(8,128)(2,1)S(1)}, bf16[160,1024]{1,0:T(8,128)(2,1)S(1)}, u32[]{:S(2)}, u32[]{:S(2)}) collective-permute-start(bf16[160,1024]{1,0:T(8,128)(2,1)S(1)} %copy-done.33), channel_id=1, source_target_pairs={{0,5},{1,4},{2,7},{3,6},{4,1},{5,0},{6,3},{7,2},{8,13},{9,12},{10,... | collective-permute-start | bytes 983048 | tf_op jit(solution)/shard_map/ppermute | solution.py:41
  477.4 28.5 %collective-permute-start.19 = (bf16[160,1024]{1,0:T(8,128)(2,1)S(1)}, bf16[160,1024]{1,0:T(8,128)(2,1)S(1)}, u32[]{:S(2)}, u32[]{:S(2)}) collective-permute-start(bf16[160,1024]{1,0:T(8,128)(2,1)S(1)} %copy-done.32), channel_id=1, source_target_pairs={{0,6},{1,7},{2,4},{3,5},{4,2},{5,3},{6,0},{7,1},{8,14},{9,15},{10,... | collective-permute-start | bytes 983048 | tf_op jit(solution)/shard_map/ppermute | solution.py:41
  480.2 28.1 %collective-permute-start.20 = (bf16[160,1024]{1,0:T(8,128)(2,1)S(1)}, bf16[160,1024]{1,0:T(8,128)(2,1)S(1)}, u32[]{:S(2)}, u32[]{:S(2)}) collective-permute-start(bf16[160,1024]{1,0:T(8,128)(2,1)S(1)} %copy-done.31), channel_id=1, source_target_pairs={{0,7},{1,6},{2,5},{3,4},{4,3},{5,2},{6,1},{7,0},{8,15},{9,14},{10,... | collective-permute-start | bytes 983048 | tf_op jit(solution)/shard_map/ppermute | solution.py:41
  505.9 124.4 %collective-permute-start.53 = (bf16[2,256,5632]{2,1,0:T(8,128)(2,1)}, bf16[2,256,5632]{2,1,0:T(8,128)(2,1)}, u32[]{:S(2)}, u32[]{:S(2)}) collective-permute-start(bf16[2,256,5632]{2,1,0:T(8,128)(2,1)} %get-tuple-element.104), channel_id=1, source_target_pairs={{0,8},{8,0},{16,24},{24,16},{1,9},{9,1},{17,25},{25,17},{2,10},{10... | collective-permute-start | bytes 17301512 | tf_op jit(solution)/shard_map/ppermute | solution.py:41
  546.3 37.3 %collective-permute-start.29 = (bf16[2,2,2,256,384]{4,3,2,1,0:T(8,128)(2,1)S(1)}, bf16[2,2,2,256,384]{4,3,2,1,0:T(8,128)(2,1)S(1)}, u32[]{:S(2)}, u32[]{:S(2)}) collective-permute-start(bf16[2,2,2,256,384]{4,3,2,1,0:T(8,128)(2,1)S(1)} %slice_bitcast_fusion.2), channel_id=1, source_target_pairs={{0,1},{1,0},{2,3},{3,2},{4,5},{5,4},{6,7},{7,6},{8,9},{9,8},{10,11... | collective-permute-start | bytes 4718600 | tf_op jit(solution)/shard_map/ppermute | solution.py:41
  551.1 76.7 %collective-permute-start.39 = (bf16[2,2,2,2,128,512]{5,4,3,2,1,0:T(8,128)(2,1)S(1)}, bf16[2,2,2,2,128,512]{5,4,3,2,1,0:T(8,128)(2,1)S(1)}, u32[]{:S(2)}, u32[]{:S(2)}) collective-permute-start(bf16[2,2,2,2,128,512]{5,4,3,2,1,0:T(8,128)(2,1)S(1)} %slice_bitcast_fusion), channel_id=1, source_target_pairs={{0,1},{1,0},{2,3},{3,2},{4,5},{5,4},{6,7},{7,6},{8,9},{9,8},{10,11... | collective-permute-start | bytes 6291464 | tf_op jit(solution)/shard_map/ppermute | solution.py:41
  557.1 100.6 %collective-permute-start.37 = (bf16[256,128]{1,0:T(8,128)(2,1)S(1)}, bf16[256,128]{1,0:T(8,128)(2,1)S(1)}, u32[]{:S(2)}, u32[]{:S(2)}) collective-permute-start(bf16[256,128]{1,0:T(8,128)(2,1)S(1)} %slice_bitcast_fusion.31), channel_id=1, source_target_pairs={{0,4},{1,5},{2,6},{3,7},{4,0},{5,1},{6,2},{7,3},{8,12},{9,13},{10,... | collective-permute-start | bytes 196616 | tf_op jit(solution)/shard_map/ppermute | solution.py:41
  560.6 112.4 %collective-permute-start.56 = (bf16[1,704,1024]{2,1,0:T(8,128)(2,1)}, bf16[1,704,1024]{2,1,0:T(8,128)(2,1)}, u32[]{:S(2)}, u32[]{:S(2)}) collective-permute-start(bf16[1,704,1024]{2,1,0:T(8,128)(2,1)} %slice.390), channel_id=1, source_target_pairs={{0,16},{8,24},{16,0},{24,8},{1,17},{9,25},{17,1},{25,9},{2,18},{10... | collective-permute-start | bytes 4325384 | tf_op jit(solution)/shard_map/ppermute | solution.py:41
  585.0 52.8 %collective-permute-start.30 = (bf16[2,2,256,384]{3,2,1,0:T(8,128)(2,1)}, bf16[2,2,256,384]{3,2,1,0:T(8,128)(2,1)}, u32[]{:S(2)}, u32[]{:S(2)}) collective-permute-start(bf16[2,2,256,384]{3,2,1,0:T(8,128)(2,1)} %slice_bitcast_fusion.15), channel_id=1, source_target_pairs={{0,16},{8,24},{16,0},{24,8},{1,17},{9,25},{17,1},{25,9},{2,18},{10... | collective-permute-start | bytes 2359304 | tf_op jit(solution)/shard_map/ppermute | solution.py:41
  629.8 26.3 %collective-permute-start.40 = (bf16[2,2,2,128,512]{4,3,2,1,0:T(8,128)(2,1)}, bf16[2,2,2,128,512]{4,3,2,1,0:T(8,128)(2,1)}, u32[]{:S(2)}, u32[]{:S(2)}) collective-permute-start(bf16[2,2,2,128,512]{4,3,2,1,0:T(8,128)(2,1)} %slice_bitcast_fusion.4), channel_id=1, source_target_pairs={{0,16},{8,24},{16,0},{24,8},{1,17},{9,25},{17,1},{25,9},{2,18},{10... | collective-permute-start | bytes 3145736 | tf_op jit(solution)/shard_map/ppermute | solution.py:41
  636.2 80.0 %collective-permute-start.54 = (bf16[1,256,5632]{2,1,0:T(8,128)(2,1)S(1)}, bf16[1,256,5632]{2,1,0:T(8,128)(2,1)S(1)}, u32[]{:S(2)}, u32[]{:S(2)}) collective-permute-start(bf16[1,256,5632]{2,1,0:T(8,128)(2,1)S(1)} %slice.388), channel_id=1, source_target_pairs={{0,16},{8,24},{16,0},{24,8},{1,17},{9,25},{17,1},{25,9},{2,18},{10... | collective-permute-start | bytes 8650760 | tf_op jit(solution)/shard_map/ppermute | solution.py:41
  (92 other events, 1122.3 us)

commit v2 on v1

v2 whole, which is shorter than its diff:
```python
import functools
import math

import jax
import jax.numpy as jnp
from jax import lax
from jax.experimental import pallas as pl
from jax.experimental.pallas import tpu as pltpu
from jax.sharding import PartitionSpec as P

HEADS = 16
LENGTH = 512
EPSILON = 1e-06
LANES = 128
GELU_C = math.sqrt(2.0 / math.pi)
GELU_A = 0.044715
F32 = jnp.float32
BF16 = jnp.bfloat16
VMEM_LIMIT = 60 * 1024 * 1024


def params(**kw):
    return pltpu.CompilerParams(vmem_limit_bytes=VMEM_LIMIT, **kw)


def cost(flops, nbytes, trans=0):
    return pl.CostEstimate(flops=int(flops), bytes_accessed=int(nbytes), transcendentals=int(trans))


def dot_f32(a, b, dims):
    return lax.dot_general(a, b, (dims, ((), ())), preferred_element_type=F32)


NN = ((1,), (0,))
NT = ((1,), (1,))
TN = ((0,), (0,))


def xor_send(v, axis, k):
    n = lax.axis_size(axis)
    return lax.ppermute(v, axis, [(i, i ^ k) for i in range(n)])


def swap_rows(v):
    return lax.all_to_all(v, "ep", split_axis=0, concat_axis=0, tiled=True)


def bits_of(n):
    return [1 << i for i in range(n.bit_length() - 1)]


def total_of(terms):
    return sum(t.astype(F32) for t in terms)


def after(value, *others):
    return lax.optimization_barrier((value, *others))[0]


def next_send(way):
    terms, order, names = way
    at = names.index(order[0])
    return total_of([lax.index_in_dim(t, 1, at, keepdims=False) for t in terms]).astype(BF16)


def exchange(way, send):
    terms, order, names = way
    at = names.index(order[0])
    got = xor_send(send, *order[0])
    kept = [lax.index_in_dim(t, 0, at, keepdims=False) for t in terms]
    return kept + [got], order[1:], names[:at] + names[at + 1 :]


def finish(way):
    while way[1]:
        way = exchange(way, next_send(way))
    return total_of(way[0])


def three_ways(keep, got, n_g, n_e):
    g_bits = [("grp", k) for k in bits_of(n_g)]
    e_bits = [("ep", k) for k in bits_of(n_e)]
    names = e_bits[::-1] + g_bits[:0:-1]
    rest, first, others = g_bits[1:], e_bits[:1], e_bits[1:]
    orders = [first + rest + others, others + first + rest, rest + first + others]
    rows, cols = keep.shape[2:]
    cuts = [0, 3 * rows // 8, 5 * rows // 8, rows]
    view = (2,) * len(names) + (rows, cols)
    both = [keep.reshape(view), got.reshape(view)]
    return [
        ([t[..., cuts[i] : cuts[i + 1], :] for t in both], order, names)
        for i, order in enumerate(orders)
    ]


def group_way(keep, got, n_g):
    g_bits = [("grp", k) for k in bits_of(n_g)]
    names = g_bits[:0:-1]
    view = (2,) * len(names) + keep.shape[1:]
    return [keep.reshape(view), got.reshape(view)], g_bits[1:], names


def place_kernel(experts, cap, chunks, routes_ref, v_ref, pos_ref, out_ref):
    tok = v_ref.shape[0]
    short = cap // chunks
    ids = lax.broadcasted_iota(jnp.int32, (LANES, tok), 0)
    named = [ids == routes_ref[k : k + 1, :] for k in range(2)]
    counts = jnp.where(named[0] | named[1], 1.0, 0.0).astype(BF16)
    before = lax.broadcasted_iota(jnp.int32, (tok, tok), 0) < lax.broadcasted_iota(
        jnp.int32, (tok, tok), 1
    )
    earlier = dot_f32(counts, jnp.where(before, 1.0, 0.0).astype(BF16), NN)
    for k in range(2):
        slot = jnp.sum(jnp.where(named[k], earlier, 0.0), axis=0, keepdims=True).astype(jnp.int32)
        owner = routes_ref[k : k + 1, :]
        pos_ref[k : k + 1, :] = owner * cap + slot
        chunk = jnp.zeros_like(slot)
        for c in range(1, chunks):
            chunk += jnp.where(slot >= c * short, 1, 0)
        pos_ref[2 + k : 3 + k, :] = chunk * (experts * short) + owner * short + slot - chunk * short
    first, second = pos_ref[0:1, :], pos_ref[1:2, :]
    rows = lax.broadcasted_iota(jnp.int32, (cap, tok), 0)
    for e in range(experts):
        here = rows + e * cap
        pick = jnp.where((here == first) | (here == second), 1.0, 0.0).astype(BF16)
        out_ref[e * cap : (e + 1) * cap, :] = dot_f32(pick, v_ref[...], NN).astype(BF16)


def place(routes_t, values, experts, cap, chunks):
    tok, width = values.shape
    return pl.pallas_call(
        functools.partial(place_kernel, experts, cap, chunks),
        out_shape=[
            jax.ShapeDtypeStruct((4, tok), jnp.int32),
            jax.ShapeDtypeStruct((experts * cap, width), BF16),
        ],
        compiler_params=params(),
        cost_estimate=cost(2 * experts * cap * tok * width, 2 * tok * width + 2 * experts * cap * width),
        name="place_rows",
    )(routes_t, values)


def dispatch_kernel(pos_ref, v_ref, *outs):
    tok = v_ref.shape[0]
    first, second = pos_ref[2:3, :], pos_ref[3:4, :]
    at = 0
    for out in outs:
        total = out.shape[0]
        step = total // 4
        rows = lax.broadcasted_iota(jnp.int32, (step, tok), 0)
        for b in range(4):
            here = rows + at
            pick = jnp.where((here == first) | (here == second), 1.0, 0.0).astype(BF16)
            out[b * step : (b + 1) * step, :] = dot_f32(pick, v_ref[...], NN).astype(BF16)
            at += step


def dispatch(pos, values, slots, chunks):
    tok, width = values.shape
    return pl.pallas_call(
        dispatch_kernel,
        out_shape=[jax.ShapeDtypeStruct((slots // chunks, width), BF16)] * chunks,
        compiler_params=params(),
        cost_estimate=cost(2 * slots * tok * width, 2 * tok * width + 2 * slots * width),
        name="dispatch_rows",
    )(pos, values)


def gathered(first, second, parts):
    total, at = None, 0
    for part in parts:
        n = part.shape[0]
        here = lax.broadcasted_iota(jnp.int32, (first.shape[0], n), 1) + at
        pick = jnp.where((here == first) | (here == second), 1.0, 0.0).astype(BF16)
        term = dot_f32(pick, part[...], NN)
        total = term if total is None else total + term
        at += n
    return total


def combine_kernel(pos_ref, x_ref, part_ref, out_ref):
    out_ref[...] = x_ref[...] + gathered(pos_ref[:, 0:1], pos_ref[:, 1:2], [part_ref])


def combine(pos_cols, after_attn, gated):
    tok, width = after_attn.shape
    blk = 256
    return pl.pallas_call(
        combine_kernel,
        grid=(tok // blk,),
        in_specs=[
            pl.BlockSpec((blk, 4), lambda i: (i, 0)),
            pl.BlockSpec((blk, width), lambda i: (i, 0)),
            pl.BlockSpec(gated.shape, lambda i: (0, 0)),
        ],
        out_specs=pl.BlockSpec((blk, width), lambda i: (i, 0)),
        out_shape=jax.ShapeDtypeStruct((tok, width), F32),
        compiler_params=params(),
        cost_estimate=cost(2 * tok * gated.shape[0] * width, 10 * tok * width),
        name="combine_rows",
    )(pos_cols, after_attn, gated)


def return_kernel(pos_ref, x_ref, cot_ref, gain_ref, *refs):
    parts, (dx_ref, low_ref, gg_ref) = refs[:-3], refs[-3:]
    grad = gathered(pos_ref[:, 2:3], pos_ref[:, 3:4], parts)
    x = x_ref[...]
    inverse = lax.rsqrt(jnp.mean(x * x, axis=-1, keepdims=True) + EPSILON)
    normed = x * inverse
    grad_normed = grad * gain_ref[...]
    dx = cot_ref[...].astype(F32) + inverse * (
        grad_normed - normed * jnp.mean(grad_normed * normed, axis=-1, keepdims=True)
    )
    dx_ref[...] = dx
    low_ref[...] = dx.astype(BF16)

    @pl.when(pl.program_id(0) == 0)
    def _():
        gg_ref[...] = jnp.zeros_like(gg_ref)

    gg_ref[...] += jnp.sum(grad * normed, axis=0, keepdims=True)


def return_grads(pos_cols, after_attn, cotangent, gain, parts):
    tok, width = after_attn.shape
    blk = 256
    row = pl.BlockSpec((blk, width), lambda i: (i, 0))
    one = pl.BlockSpec((1, width), lambda i: (0, 0))
    slots = sum(p.shape[0] for p in parts)
    return pl.pallas_call(
        return_kernel,
        grid=(tok // blk,),
        in_specs=[pl.BlockSpec((blk, 4), lambda i: (i, 0)), row, row, one]
        + [pl.BlockSpec(p.shape, lambda i: (0, 0)) for p in parts],
        out_specs=[row, row, one],
        out_shape=[
            jax.ShapeDtypeStruct((tok, width), F32),
            jax.ShapeDtypeStruct((tok, width), BF16),
            jax.ShapeDtypeStruct((1, width), F32),
        ],
        compiler_params=params(),
        cost_estimate=cost(2 * tok * slots * width, 16 * tok * width),
        name="return_rows",
    )(pos_cols, after_attn, cotangent, gain, *parts)


def expert_kernel(experts, aliased, *refs):
    me_ref, x_ref, c_ref, d_ref, wg_ref, wu_ref, wr_ref, wrt_ref = refs[:8]
    refs = refs[8 + (3 if aliased else 0) :]
    act_ref, dg_ref, du_ref, out_ref, deo_ref, own_ref, gr_ref = refs[:7]
    acc_ref, gate_ref, prob_ref, p_ref = refs[7:]
    j = pl.program_id(0)
    rows_all = x_ref.shape[0]
    n_src, _, short, tile = d_ref.shape
    width = x_ref.shape[1]
    lane = lax.broadcasted_iota(jnp.int32, (rows_all, LANES), 1)

    @pl.when(j == 0)
    def _():
        logits = dot_f32(x_ref[...], wr_ref[...], NN)
        logits = jnp.where(lane < experts, logits, -1e30)
        exps = jnp.exp(logits - jnp.max(logits, axis=-1, keepdims=True))
        probs = exps / jnp.sum(exps, axis=-1, keepdims=True)
        prob_ref[...] = probs
        own = jnp.sum(jnp.where(lane == me_ref[1], probs, 0.0), axis=-1, keepdims=True)
        p_ref[...] = jnp.broadcast_to(own, p_ref.shape)
        own_ref[...] = p_ref[...].reshape(n_src, 1, short, LANES)
        wide = jnp.concatenate([p_ref[...]] * (width // LANES), axis=1)
        deo_ref[...] = (c_ref[...].reshape(rows_all, width).astype(F32) * wide).astype(BF16)
        acc_ref[...] = jnp.zeros_like(acc_ref)
        gate_ref[...] = jnp.zeros_like(gate_ref)

    n_blk = n_src // 2
    for b in range(n_blk):
        rows = slice(2 * b * short, 2 * (b + 1) * short)
        x = x_ref[rows, :]
        z = dot_f32(x, wg_ref[...], NN)
        up = dot_f32(x, wu_ref[...], NN)
        back = d_ref[2 * b : 2 * b + 2].reshape(2 * short, tile).astype(F32)
        reps = tile // LANES
        own = jnp.concatenate([p_ref[rows, :]] * reps, axis=1)
        zz = z * z
        th = jnp.tanh(GELU_C * z * (1.0 + GELU_A * zz))
        half = 0.5 + 0.5 * th
        gelu = z * half
        slope = half + 0.5 * GELU_C * z * (1.0 - th * th) * (1.0 + 3.0 * GELU_A * zz)
        act = (gelu * up).astype(BF16)
        act_ref[rows, :] = act
        share = act.astype(F32) * back
        gate_ref[rows, :] += sum(share[:, i * LANES : (i + 1) * LANES] for i in range(reps))
        dact = back * own
        dg = (dact * up * slope).astype(BF16)
        du = (dact * gelu).astype(BF16)
        dg_ref[rows, :] = dg
        du_ref[rows, :] = du
        acc_ref[rows, :] += dot_f32(dg, wg_ref[...], NT) + dot_f32(du, wu_ref[...], NT)

    @pl.when(j == pl.num_programs(0) - 1)
    def _():
        dgate = jnp.sum(gate_ref[...], axis=-1, keepdims=True)
        dl = dgate * p_ref[...] * (jnp.where(lane == me_ref[1], 1.0, 0.0) - prob_ref[...])
        dl = dl.astype(BF16)
        out_ref[...] = (acc_ref[...] + dot_f32(dl, wrt_ref[...], NN)).astype(BF16)
        gr_ref[...] = dot_f32(dl, x_ref[...], TN)[: gr_ref.shape[0], :]


def expert_chunk(me, rows, cot, dact, w_gate_up, wr_pad, wr_pad_t, experts, c, total_rows, earlier):
    n_src, chunks, short, width = cot.shape
    ff = dact.shape[-1]
    tile = 256
    steps = ff // tile
    n_rows = rows.shape[0]
    whole = pl.BlockSpec(memory_space=pl.ANY)
    part = pl.BlockSpec((n_rows, tile), lambda j, m: (c, j))
    aliased = earlier is not None
    few = -(-experts // 8) * 8
    call = pl.pallas_call(
        functools.partial(expert_kernel, experts, aliased),
        grid_spec=pltpu.PrefetchScalarGridSpec(
            num_scalar_prefetch=1,
            grid=(steps,),
            in_specs=[
                pl.BlockSpec((n_rows, width), lambda j, m: (0, 0)),
                pl.BlockSpec((n_src, 1, short, width), lambda j, m: (0, c, 0, 0)),
                pl.BlockSpec((n_src, 1, short, tile), lambda j, m: (0, c, 0, j)),
                pl.BlockSpec((width, tile), lambda j, m: (0, j)),
                pl.BlockSpec((width, tile), lambda j, m: (0, j + steps)),
                pl.BlockSpec((width, LANES), lambda j, m: (0, 0)),
                pl.BlockSpec((LANES, width), lambda j, m: (0, 0)),
            ]
            + ([whole] * 3 if aliased else []),
            out_specs=[
                part,
                part,
                part,
                pl.BlockSpec((n_rows, width), lambda j, m: (0, 0)),
                pl.BlockSpec((n_rows, width), lambda j, m: (0, 0)),
                pl.BlockSpec((n_src, 1, short, LANES), lambda j, m: (0, 0, 0, 0)),
                pl.BlockSpec((few, width), lambda j, m: (0, 0)),
            ],
            scratch_shapes=[
                pltpu.VMEM((n_rows, width), F32),
                pltpu.VMEM((n_rows, LANES), F32),
                pltpu.VMEM((n_rows, LANES), F32),
                pltpu.VMEM((n_rows, LANES), F32),
            ],
        ),
        out_shape=[jax.ShapeDtypeStruct((total_rows, ff), BF16)] * 3
        + [
            jax.ShapeDtypeStruct((n_rows, width), BF16),
            jax.ShapeDtypeStruct((n_rows, width), BF16),
            jax.ShapeDtypeStruct((n_src, 1, short, LANES), F32),
            jax.ShapeDtypeStruct((few, width), F32),
        ],
        input_output_aliases={8: 0, 9: 1, 10: 2} if aliased else {},
        compiler_params=params(),
        cost_estimate=cost(
            8 * n_rows * width * ff, 4 * width * ff + 10 * n_rows * ff + 4 * n_rows * width, n_rows * ff
        ),
        name="expert_rows",
    )
    out = call(me, rows, cot, dact, w_gate_up, w_gate_up, wr_pad, wr_pad_t, *(earlier if aliased else ()))
    return out[:3], out[3:]


def gated_kernel(chunks, act_ref, w_ref, *refs):
    own_refs, out_ref = refs[:-1], refs[-1]
    n_src, _, short, width = out_ref.shape
    n_rows = n_src * short
    for c in range(chunks):

        @pl.when(pl.program_id(0) == c)
        def _():
            own = jnp.concatenate([own_refs[c][...].reshape(n_rows, LANES)] * (width // LANES), axis=1)
            eo = dot_f32(act_ref[...], w_ref[...], NN) * own
            out_ref[...] = eo.astype(BF16).reshape(n_src, 1, short, width)


def gated_rows(act, w_eo, owns):
    chunks = len(owns)
    n_src, _, short, _ = owns[0].shape
    total, ff = act.shape
    width = w_eo.shape[1]
    return pl.pallas_call(
        functools.partial(gated_kernel, chunks),
        grid=(chunks,),
        in_specs=[
            pl.BlockSpec((total // chunks, ff), lambda c: (c, 0)),
            pl.BlockSpec((ff, width), lambda c: (0, 0)),
        ]
        + [pl.BlockSpec(o.shape, lambda c: (0, 0, 0, 0)) for o in owns],
        out_specs=pl.BlockSpec((n_src, 1, short, width), lambda c: (0, c, 0, 0)),
        out_shape=jax.ShapeDtypeStruct((n_src, chunks, short, width), BF16),
        compiler_params=params(),
        cost_estimate=cost(2 * total * ff * width, 2 * total * (ff + width) + 2 * ff * width),
        name="gated_rows",
    )(act, w_eo, *owns)


def share_rows(me_g, n_g, full_ref, keep_ref, send_ref):
    rows = full_ref.shape[0] // n_g
    for r_g in range(n_g):
        at = pl.multiple_of((me_g ^ r_g) * rows, rows)
        out = send_ref if r_g & 1 else keep_ref
        block = full_ref[pl.ds(at, rows), :].astype(BF16)
        if len(out.shape) == 4:
            out[0, r_g // 2] = block
        else:
            out[r_g // 2] = block


def weight_kernel(n_g, me_ref, a_ref, o_ref, b0_ref, b1_ref, b2_ref, d_ref, keep_ref, send_ref, full_ref, at_ref, ot_ref):
    @pl.when(pl.program_id(0) == 0)
    def _():
        at_ref[...] = a_ref[...].T
        ot_ref[...] = o_ref[...].T

    for i, b in enumerate((b0_ref, b1_ref, b2_ref)):
        full_ref[:, i * LANES : (i + 1) * LANES] = dot_f32(at_ref[...], b[0], NN)
    full_ref[:, 3 * LANES :] = dot_f32(ot_ref[...], d_ref[...], NN)
    share_rows(me_ref[0], n_g, full_ref, keep_ref, send_ref)


def weight_grads(me, a_one, mixed, grad_qkv, grad_low, n_g, n_e):
    tok, width = a_one.shape
    heads_wide = width // LANES
    block = pl.BlockSpec((1, n_g // 2, width // n_g, 4 * LANES), lambda r, m: (r, 0, 0, 0))

    def plane(t):
        def index(r, m):
            at = 3 * (m[1] ^ r) + t
            return (at // heads_wide, 0, at % heads_wide)

        return pl.BlockSpec((1, tok, LANES), index)

    return pl.pallas_call(
        functools.partial(weight_kernel, n_g),
        grid_spec=pltpu.PrefetchScalarGridSpec(
            num_scalar_prefetch=1,
            grid=(n_e,),
            in_specs=[
                pl.BlockSpec((tok, width), lambda r, m: (0, 0)),
                pl.BlockSpec((tok, width), lambda r, m: (0, 0)),
                plane(0),
                plane(1),
                plane(2),
                pl.BlockSpec((tok, LANES), lambda r, m: (0, m[1] ^ r)),
            ],
            out_specs=[block, block],
            scratch_shapes=[
                pltpu.VMEM((width, 4 * LANES), F32),
                pltpu.VMEM((width, tok), BF16),
                pltpu.VMEM((width, tok), BF16),
            ],
        ),
        out_shape=[jax.ShapeDtypeStruct((n_e, n_g // 2, width // n_g, 4 * LANES), BF16)] * 2,
        compiler_params=params(),
        cost_estimate=cost(8 * tok * width * width, 12 * tok * width + 8 * width * width),
        name="weight_grads",
    )(me, a_one, mixed, grad_qkv, grad_qkv, grad_qkv, grad_low)


def relative(v, axis, me, n):
    return jnp.stack([lax.dynamic_index_in_dim(v, me ^ r, axis, keepdims=False) for r in range(n)], axis)


def own_blocks(view, me_g, me_e, n_g, n_e):
    view = relative(relative(view, 0, me_e, n_e), 1, me_g, n_g)
    return view[:, 0::2], view[:, 1::2]


def gate_up_kernel(n_g, half, n_part, me_ref, *refs):
    parts, (g_ref, u_ref, keep_ref, send_ref, full_ref, t_ref) = refs[:n_part], refs[n_part:]
    j = pl.program_id(0)

    @pl.when(j == 0)
    def _():
        at = 0
        for part in parts:
            t_ref[:, at : at + part.shape[0]] = part[...].T
            at += part.shape[0]

    @pl.when(j < half)
    def _():
        full_ref[...] = dot_f32(t_ref[...], g_ref[...], NN)

    @pl.when(j >= half)
    def _():
        full_ref[...] = dot_f32(t_ref[...], u_ref[...], NN)

    share_rows(me_ref[0], n_g, full_ref, keep_ref, send_ref)


def gate_up_grad(me, parts, dg, du, n_g):
    total, ff = dg.shape
    width = parts[0].shape[1]
    tile = 256
    half = ff // tile
    spec = pl.BlockSpec((n_g // 2, width // n_g, tile), lambda j, m: (0, 0, j))
    return pl.pallas_call(
        functools.partial(gate_up_kernel, n_g, half, len(parts)),
        grid_spec=pltpu.PrefetchScalarGridSpec(
            num_scalar_prefetch=1,
            grid=(2 * half,),
            in_specs=[pl.BlockSpec(p.shape, lambda j, m: (0, 0)) for p in parts]
            + [
                pl.BlockSpec((total, tile), lambda j, m: (0, jnp.minimum(j, half - 1))),
                pl.BlockSpec((total, tile), lambda j, m: (0, jnp.maximum(j - half, 0))),
            ],
            out_specs=[spec, spec],
            scratch_shapes=[pltpu.VMEM((width, tile), F32), pltpu.VMEM((width, total), BF16)],
        ),
        out_shape=[jax.ShapeDtypeStruct((n_g // 2, width // n_g, 2 * ff), BF16)] * 2,
        compiler_params=params(),
        cost_estimate=cost(4 * total * width * ff, 2 * total * (width + 2 * ff) + 4 * width * ff),
        name="gate_up_grad",
    )(me, *parts, dg, du)


def out_grad_kernel(n_g, n_part, me_ref, act_ref, *refs):
    parts, (keep_ref, send_ref, full_ref, t_ref) = refs[:n_part], refs[n_part:]

    @pl.when(pl.program_id(0) == 0)
    def _():
        t_ref[...] = act_ref[...].T

    total, at = None, 0
    for part in parts:
        n = part.shape[0]
        term = dot_f32(t_ref[:, at : at + n], part[...], NN)
        total = term if total is None else total + term
        at += n
    full_ref[...] = total
    share_rows(me_ref[0], n_g, full_ref, keep_ref, send_ref)


def out_grad(me, act, parts, n_g):
    total, ff = act.shape
    width = parts[0].shape[1]
    tile = 256
    spec = pl.BlockSpec((n_g // 2, ff // n_g, tile), lambda j, m: (0, 0, j))
    return pl.pallas_call(
        functools.partial(out_grad_kernel, n_g, len(parts)),
        grid_spec=pltpu.PrefetchScalarGridSpec(
            num_scalar_prefetch=1,
            grid=(width // tile,),
            in_specs=[pl.BlockSpec((total, ff), lambda j, m: (0, 0))]
            + [pl.BlockSpec((p.shape[0], tile), lambda j, m: (0, j)) for p in parts],
            out_specs=[spec, spec],
            scratch_shapes=[pltpu.VMEM((ff, tile), F32), pltpu.VMEM((ff, total), BF16)],
        ),
        out_shape=[jax.ShapeDtypeStruct((n_g // 2, ff // n_g, width), BF16)] * 2,
        compiler_params=params(),
        cost_estimate=cost(2 * total * width * ff, 2 * total * (width + ff) + 2 * width * ff),
        name="out_grad",
    )(me, act, *parts)


def fill_mask(start, length, mask_ref):
    tok = mask_ref.shape[0]
    query = lax.broadcasted_iota(jnp.int32, (tok, tok), 0)
    key = lax.broadcasted_iota(jnp.int32, (tok, tok), 1)
    end = start + length
    inside = (query >= start) & (query < end) & (key >= start) & (key < end)
    mask_ref[...] = jnp.where((key <= query) | inside, 0.0, -1e30)


def half_lanes(v, h):
    lane = lax.broadcasted_iota(jnp.int32, v.shape, 1)
    return jnp.where((lane >= LANES // 2) == (h == 1), v, jnp.zeros_like(v))


def forward_kernel(blk, scale, s_ref, q_ref, k_ref, v_ref, b_ref, o_ref, lse_ref, mask_ref):
    tok = q_ref.shape[0]
    pair = pl.program_id(0)

    @pl.when(pair == 0)
    def _():
        fill_mask(s_ref[2], s_ref[3], mask_ref)
        lse_ref[...] = jnp.zeros_like(lse_ref)

    lane = lax.broadcasted_iota(jnp.int32, (blk, LANES), 1)
    values = [half_lanes(v_ref[...], h) for h in range(2)]
    for i in range(tok // blk):
        rows = slice(i * blk, (i + 1) * blk)
        mixed, lse = None, lse_ref[rows, :]
        for h in range(2):
            q = half_lanes(q_ref[rows, :] * scale, h)
            s = dot_f32(q, k_ref[...], NT) + b_ref[h, rows, :].astype(F32) + mask_ref[rows, :]
            top = jnp.max(s, axis=-1, keepdims=True)
            e = jnp.exp(s - top)
            total = jnp.sum(e, axis=-1, keepdims=True)
            p = (e * (1.0 / total)).astype(BF16)
            o = dot_f32(p, values[h], NN)
            mixed = o if mixed is None else mixed + o
            lse = jnp.where(lane == 2 * pair + h, top + jnp.log(total), lse)
        o_ref[rows, :] = mixed.astype(BF16)
        lse_ref[rows, :] = lse


def attention_forward(scalars, qkv, rel_bias, scale):
    tok, width = qkv.shape[0], qkv.shape[1] // 3
    pairs = width // LANES
    column = lambda p: pl.BlockSpec((tok, LANES), lambda i, m: (0, p * pairs + i))
    return pl.pallas_call(
        functools.partial(forward_kernel, 128, scale),
        grid_spec=pltpu.PrefetchScalarGridSpec(
            num_scalar_prefetch=1,
            grid=(pairs,),
            in_specs=[
                column(0),
                column(1),
                column(2),
                pl.BlockSpec((2, tok, tok), lambda i, m: (i, 0, 0)),
            ],
            out_specs=[
                pl.BlockSpec((tok, LANES), lambda i, m: (0, i)),
                pl.BlockSpec((tok, LANES), lambda i, m: (0, 0)),
            ],
            scratch_shapes=[pltpu.VMEM((tok, tok), F32)],
        ),
        out_shape=[
            jax.ShapeDtypeStruct((tok, width), BF16),
            jax.ShapeDtypeStruct((tok, LANES), F32),
        ],
        compiler_params=params(),
        cost_estimate=cost(8 * tok * tok * width, 8 * tok * width + 32 * tok * tok, 16 * tok * tok),
        name="attention_forward",
    )(scalars, qkv, qkv, qkv, rel_bias)


def backward_kernel(n_g, scale, per_owner, s_ref, q_ref, k_ref, v_ref, do_ref, b_ref, lse_ref, *refs):
    outs, (dqkv_ref, mask_ref) = refs[:-2], refs[-2:]
    tok = q_ref.shape[0]
    rows = tok // n_g
    pair = s_ref[1] ^ pl.program_id(0) if per_owner else pl.program_id(0)

    @pl.when(pl.program_id(0) == 0)
    def _():
        fill_mask(s_ref[2], s_ref[3], mask_ref)

    lane = lax.broadcasted_iota(jnp.int32, (rows, LANES), 1)
    keys = [half_lanes(k_ref[...], h) for h in range(2)]
    grad_k = grad_v = None
    for r_g in range(n_g):
        at = pl.multiple_of((s_ref[0] ^ r_g) * rows, rows) if per_owner else r_g * rows
        here = pl.ds(at, rows)
        grad_q = None
        for h in range(2):
            q = half_lanes(q_ref[here, :] * scale, h)
            do = half_lanes(do_ref[here, :], h)
            lse = jnp.sum(jnp.where(lane == 2 * pair + h, lse_ref[here, :], 0.0), axis=-1, keepdims=True)
            s = dot_f32(q, k_ref[...], NT) + b_ref[h, here, :].astype(F32) + mask_ref[here, :]
            p = jnp.exp(s - lse)
            dp = dot_f32(do, v_ref[...], NT)
            ds = p * (dp - jnp.sum(p * dp, axis=-1, keepdims=True))
            ds = ds.astype(BF16)
            if per_owner:
                outs[r_g & 1][0, r_g // 2, h * rows : (h + 1) * rows, :] = ds
            else:
                outs[0][h, here, :] = ds
            dv = dot_f32(p.astype(BF16), do, TN)
            dk = dot_f32(ds, q, TN)
            dq = dot_f32(ds, keys[h], NN)
            grad_v = dv if grad_v is None else grad_v + dv
            grad_k = dk if grad_k is None else grad_k + dk
            grad_q = dq if grad_q is None else grad_q + dq
        dqkv_ref[0, here, :] = (grad_q * scale).astype(BF16)
    dqkv_ref[1] = grad_k.astype(BF16)
    dqkv_ref[2] = grad_v.astype(BF16)


def attention_backward(scalars, qkv, grad_mixed, rel_bias, lse, scale, n_g, n_e, per_owner):
    tok, width = grad_mixed.shape
    pairs = width // LANES
    turn = (lambda i, m: m[1] ^ i) if per_owner else (lambda i, m: i)
    column = lambda p: pl.BlockSpec((tok, LANES), lambda i, m: (0, p * pairs + turn(i, m)))
    if per_owner:
        block = pl.BlockSpec((1, n_g // 2, 2 * tok // n_g, tok), lambda i, m: (i, 0, 0, 0))
        bias_specs = [block, block]
        bias_shapes = [jax.ShapeDtypeStruct((n_e, n_g // 2, 2 * tok // n_g, tok), BF16)] * 2
    else:
        bias_specs = [pl.BlockSpec((2, tok, tok), lambda i, m: (i, 0, 0))]
        bias_shapes = [jax.ShapeDtypeStruct((2 * pairs, tok, tok), BF16)]
    return pl.pallas_call(
        functools.partial(backward_kernel, n_g, scale, per_owner),
        grid_spec=pltpu.PrefetchScalarGridSpec(
            num_scalar_prefetch=1,
            grid=(pairs,),
            in_specs=[
                column(0),
                column(1),
                column(2),
                column(0),
                pl.BlockSpec((2, tok, tok), lambda i, m: (turn(i, m), 0, 0)),
                pl.BlockSpec((tok, LANES), lambda i, m: (0, 0)),
            ],
            out_specs=bias_specs + [pl.BlockSpec((3, tok, LANES), lambda i, m: (0, 0, turn(i, m)))],
            scratch_shapes=[pltpu.VMEM((tok, tok), F32)],
        ),
        out_shape=bias_shapes + [jax.ShapeDtypeStruct((3, tok, width), BF16)],
        compiler_params=params(),
        cost_estimate=cost(20 * tok * tok * width, 16 * tok * width + 64 * tok * tok, 16 * tok * tok),
        name="attention_backward",
    )(scalars, qkv, qkv, qkv, grad_mixed, rel_bias, lse)


def norm_forward(values):
    inverse = lax.rsqrt(jnp.mean(values * values, axis=-1, keepdims=True) + EPSILON)
    return (values * inverse, inverse)


def norm_backward(grad_out, normed, inverse, norm_gain):
    grad_normed = grad_out * norm_gain
    grad_gain = jnp.sum(grad_out * normed, axis=0)
    grad_input = inverse * (
        grad_normed - normed * jnp.mean(grad_normed * normed, axis=-1, keepdims=True)
    )
    return (grad_input, grad_gain)


def body(
    tokens,
    cotangent,
    w_qkv,
    w_out_attn,
    rel_bias,
    norm_gains,
    w_router,
    w_gate_up,
    w_expert_out,
    routes,
    spans,
):
    tok, width = tokens.shape
    n_g, n_e = lax.axis_size("grp"), lax.axis_size("ep")
    assert w_gate_up.shape[0] == 1 and spans.shape[0] == 1 and tok == LENGTH
    assert n_g & (n_g - 1) == 0 and n_e & (n_e - 1) == 0 and n_g > 1 and n_e > 3
    assert width == HEADS * LANES // 2
    experts = n_e
    cap = 5 * routes.shape[1] * tok // (4 * experts)
    chunks = 2 if cap % 32 == 0 else 1
    short = cap // chunks
    slots = experts * cap
    scale = 1.0 / math.sqrt(width // HEADS)
    me_g, me_e = lax.axis_index("grp"), lax.axis_index("ep")
    me = jnp.stack([me_g, me_e, spans[0, 0], spans[0, 1]]).astype(jnp.int32)
    w_gu, w_eo = w_gate_up[0], w_expert_out[0]

    pos, cot_out = place(routes.T, cotangent, experts, cap, chunks)
    pos_cols = pos.T
    tokens = after(tokens, cot_out)
    cot_rows = swap_rows(cot_out)

    hidden = tokens.astype(F32)
    normed_one, inverse_one = norm_forward(hidden)
    a_one = (normed_one * norm_gains[0]).astype(BF16)
    qkv_rows = dot_f32(a_one, w_qkv, NN).astype(BF16)
    mixed_heads, lse = attention_forward(me, qkv_rows, rel_bias, scale)
    after_attn = hidden + dot_f32(mixed_heads, w_out_attn, NN)
    normed_two, _ = norm_forward(after_attn)
    a_two = (normed_two * norm_gains[1]).astype(BF16)

    parts = dispatch(pos, after(a_two, cot_rows), slots, chunks)
    dact = dot_f32(cot_rows, w_eo, NT).astype(BF16)
    parts = [swap_rows(p if c == 0 else after(p, dact)) for c, p in enumerate(parts)]
    dact = dact.reshape(n_e, chunks, short, -1)
    cot_view = cot_rows.reshape(n_e, chunks, short, width)
    wr_pad = jnp.pad(w_router, ((0, 0), (0, LANES - experts)))
    wr_pad_t = wr_pad.T
    state, back, deos, owns, grad_route = None, [], [], [], 0.0
    for c in range(chunks):
        state, (dxe, deo, own, gr) = expert_chunk(
            me, parts[c], cot_view, dact, w_gu, wr_pad, wr_pad_t, experts, c, slots, state
        )
        back.append(swap_rows(dxe))
        deos.append(deo)
        owns.append(own)
        grad_route = grad_route + gr[:experts]
    act, dg, du = state

    core = ("grp", 1)
    gate_keep, gate_out = gate_up_grad(me, parts, after(dg, *back[:-1]), du, n_g)
    gate = group_way(gate_keep, xor_send(gate_out, *core), n_g)
    gated = gated_rows(after(act, gate_out, *back), w_eo, owns).reshape(slots, width)
    gate_send = next_send(gate)
    gate = exchange(gate, gate_send)

    grad_after, grad_attn_low, grad_gain_two = return_grads(
        pos_cols, after_attn, cotangent, norm_gains[1:], [after(back[0], gated, gate_send)] + back[1:]
    )
    gated = swap_rows(after(gated, *back))
    grad_mixed = dot_f32(grad_attn_low, w_out_attn, NT).astype(BF16)
    rows_g, rows_t = width // n_g, tok // n_g
    per_owner = n_e * LANES == width
    *grad_bias, grad_qkv = attention_backward(
        me, qkv_rows, grad_mixed, rel_bias, lse, scale, n_g, n_e, per_owner
    )
    if not per_owner:
        bias = grad_bias[0].reshape(n_e, HEADS // n_e, n_g, rows_t, tok).transpose(0, 2, 1, 3, 4)
        grad_bias = own_blocks(bias.reshape(n_e, n_g, -1, tok), me_g, me_e, n_g, n_e)
    bias = three_ways(grad_bias[0], xor_send(grad_bias[1], *core), n_g, n_e)
    grad_a_one = sum(
        dot_f32(grad_qkv[i], w_qkv[:, i * width : (i + 1) * width], NT) for i in range(3)
    )
    sends = [next_send(way) for way in bias]
    bias = [exchange(way, send) for way, send in zip(bias, sends)]
    grad_qkv_late = after(grad_qkv, *sends)
    if per_owner:
        weights = weight_grads(me, a_one, mixed_heads, grad_qkv_late, grad_attn_low, n_g, n_e)
    else:
        flat = jnp.concatenate([grad_qkv_late[i] for i in range(3)], axis=1)
        full = [dot_f32(a_one, flat, TN), dot_f32(mixed_heads, grad_attn_low, TN)]
        full = [f.astype(BF16).reshape(n_g, rows_g, n_e, -1) for f in full]
        full = jnp.concatenate(full, axis=-1).transpose(2, 0, 1, 3)
        weights = own_blocks(full, me_g, me_e, n_g, n_e)
    deos[0] = after(deos[0], weights[1], gate[0][-1])
    weights = three_ways(weights[0], xor_send(weights[1], *core), n_g, n_e)
    out_keep, out_send = out_grad(me, act, deos, n_g)
    expert_out = group_way(out_keep, xor_send(out_send, *core), n_g)
    sends = [after(next_send(way), out_send) for way in weights]
    weights = [exchange(way, send) for way, send in zip(weights, sends)]
    output = combine(pos_cols, after(after_attn, *sends), gated)
    out_send = next_send(expert_out)
    expert_out = exchange(expert_out, out_send)
    sends = [after(next_send(way), *sends) for way in bias]
    bias = [exchange(way, send) for way, send in zip(bias, sends)]
    grad_norm_one, grad_gain_one = norm_backward(grad_a_one, normed_one, inverse_one, norm_gains[0])
    grad_tokens = grad_after + grad_norm_one
    small = jnp.concatenate([grad_gain_one[None], grad_gain_two, grad_route])
    small = lax.all_gather(small, ("grp", "ep"))
    gate[0][-1] = after(gate[0][-1], *sends)
    grad_w_gate = finish(gate)[None]
    sends = [after(next_send(way), out_send) for way in weights]
    weights = [exchange(way, send) for way, send in zip(weights, sends)]
    sends = [after(next_send(way), grad_w_gate, output, *sends) for way in bias]
    bias = [exchange(way, send) for way, send in zip(bias, sends)]
    expert_out[0][0] = after(expert_out[0][0], *sends)
    grad_w_expert = finish(expert_out)[None]
    small = jnp.sum(after(small, *sends), axis=0)
    g_bias = jnp.concatenate([finish(way) for way in bias]).reshape(HEADS // n_e, rows_t, tok)
    g_weights = jnp.concatenate([finish(way) for way in weights])
    wide = 3 * width // n_e
    return (
        output,
        grad_tokens,
        g_weights[:, :wide],
        g_weights[:, wide:],
        g_bias,
        small[:2],
        small[2:].T,
        grad_w_gate,
        grad_w_expert,
    )


def solution(mesh):
    placed = (
        P(("grp", "ep"), None),
        P(("grp", "ep"), None),
        P(),
        P(),
        P(),
        P(),
        P(),
        P("ep", None, None),
        P("ep", None, None),
        P(("grp", "ep"), None),
        P(("grp", "ep"), None),
    )
    return jax.shard_map(
        body,
        mesh=mesh,
        in_specs=placed,
        out_specs=(
            P(("grp", "ep"), None),
            P(("grp", "ep"), None),
            P("grp", "ep"),
            P("grp", "ep"),
            P("ep", "grp", None),
            P(),
            P(),
            P("ep", "grp", None),
            P("ep", "grp", None),
        ),
        check_vma=False,
    )
```

time: 729 us -> 575 us (0.79)
  waiting for transfers between devices: 212 us -> 128 us
  Pallas kernels: 145 us -> 219 us
  matrix products: 105 us -> 37.1 us
  starting transfers between devices: 108 us -> 67 us
  local copies, waits for them, and re-layouts: 68.9 us -> 32.3 us
  between operations: 3.73 us -> 15 us
  other arithmetic: 77.3 us -> 66.3 us
    ppermute x57 -> x30, waiting for transfers between devices: 212 us -> 55.2 us  [xor_send(): return lax.ppermute(v, axis, [(i, i ^ k) for i in range(n)])]
    pallas_call x10 -> x12, Pallas kernels: 145 us -> 219 us  [the longest x2 73.9 us: expert_chunk(): call(me, rows, cot, dact, w_gate_up, w_gate_up, wr_pad, wr_pad_t, *(earli...]
    ppermute x57 -> x30, starting transfers between devices: 108 us -> 33.8 us  [xor_send(): return lax.ppermute(v, axis, [(i, i ^ k) for i in range(n)])]
    all_to_all x0 -> x6, waiting for transfers between devices: none -> 72.5 us  [swap_rows(): return lax.all_to_all(v, 'ep', split_axis=0, concat_axis=0, tiled=True)]
    dot_general x6 -> x0, matrix products: 42.6 us -> none  [the longest x1 12.4 us: attention_backward(): jnp.einsum('qhd,khd->hqk', grad_heads, value_heads, preferred_element_typ...]
    all_to_all x0 -> x6, starting transfers between devices: none -> 33 us  [swap_rows(): return lax.all_to_all(v, 'ep', split_axis=0, concat_axis=0, tiled=True)]
    unnamed x156 -> x93, local copies, waits for them, and re-layouts: 33.9 us -> 4.83 us
    dot_general x9 -> x7, matrix products: 62.7 us -> 37.1 us  [dot_f32(): return lax.dot_general(a, b, (dims, ((), ())), preferred_element_type=F32)]
  transfers between devices with their start and end apart: 57 -> 37, of which waited for: 21 -> 13; matrix products, arithmetic and copies ran while one was open for 23% -> 21% of each run, Pallas kernels for 17% -> 26%
where the time goes in v2:
time: 575 us; the launch traced here: 565 us
  Pallas kernels  219 us (38%)
  waiting for transfers between devices  128 us (22%)
  starting transfers between devices  67 us (12%)
  other arithmetic  66.3 us (12%)
  matrix products  37.1 us (6%)
  local copies, waits for them, and re-layouts  32.3 us (6%)
  between operations  15 us (3%)
    pallas_call x2, Pallas kernels, expert_chunk(): call(me, rows, cot, dact, w_gate_up, w_gate_up, wr_pad, wr_pad_t, *(earli...  73.9 us
    all_to_all x6, waiting for transfers between devices, swap_rows(): return lax.all_to_all(v, 'ep', split_axis=0, concat_axis=0, tiled=True)  72.5 us
    ppermute x30, waiting for transfers between devices, xor_send(): return lax.ppermute(v, axis, [(i, i ^ k) for i in range(n)])  55.2 us
    dot_general x7, matrix products, dot_f32(): return lax.dot_general(a, b, (dims, ((), ())), preferred_element_type=F32)  37.1 us
    ppermute x30, starting transfers between devices, xor_send(): return lax.ppermute(v, axis, [(i, i ^ k) for i in range(n)])  33.8 us
    all_to_all x6, starting transfers between devices, swap_rows(): return lax.all_to_all(v, 'ep', split_axis=0, concat_axis=0, tiled=True)  33 us
    convert_element_type x22, other arithmetic, next_send(): total_of([lax.index_in_dim(t, 1, at, keepdims=False) for t in terms])  32.3 us
    pallas_call x1, Pallas kernels, attention_backward(): pl.pallas_call(functools.partial(backward_kernel, n_g, scale, per_owner),...  30.5 us
  transfers between devices with their start and end apart: 37, of which 13 were waited for; matrix products, arithmetic and copies ran while one was open for 21% of the time, Pallas kernels for 26%

profile of v2, /device:TPU:0, one launch (start us, length us, event | category | flops | bytes accessed | tf_op | source)
XLA Modules:
  0.0 564.6 jit_solution(2406216275628369910)
XLA Ops:
  7.2 4.7 place_rows.1
  11.9 7.4 %all-to-all-start = ((bf16[8,160,1024]{2,1,0:T(8,128)(2,1)}), bf16[8,160,1024]{2,1,0:T(8,128)(2,1)}, u32[]{:S(2)}, u32[]{:S(2)}) async-start(bf16[8,160,1024]{2,1,0:T(8,128)(2,1)} %bitcast.371), calls=%async_computation | async-start | bytes 5242880 | tf_op jit(solution)/shard_map/all_to_all | solution.py:45
  23.4 7.5 %convolution_convert_fusion.1.q_ref.k_ref.v_ref = bf16[512,3072]{1,0:T(8,128)(2,1)} fusion(bf16[512,1024]{1,0:T(8,128)(2,1)S(1)} %fusion.8.a_ref, bf16[1024,3072]{1,0:T(8,128)(2,1)} %param.13), kind=kOutput, calls=%fused_computation.4 | convolution fusion | flops 3222798336 | bytes 10485760 | tf_op jit(solution)/shard_map/dot_general | solution.py:31
  30.9 19.8 %attention_forward.1 = (bf16[512,1024]{1,0:T(8,128)(2,1)}, f32[512,128]{1,0:T(8,128)}) custom-call(s32[4]{0:T(128)} %pad_add_fusion.s_ref.refs_0_.me_ref, bf16[512,3072]{1,0:T(8,128)(2,1)} %convolution_convert_fusion.1.q_ref.k_ref.v_ref, bf16[512,3072]{1,0:T(8,128)(2,1)} %convolution_convert_fusion.1.q_ref.k_ref.v_ref, ...), custom_call_target="tpu_custom_call" | custom-call | flops 2147483648 | bytes 12582912 | tf_op jit(solution)/shard_map/attention_forward/pallas_call | solution.py:605
  55.9 23.0 %all-to-all-done = bf16[8,160,1024]{2,1,0:T(8,128)(2,1)} async-done(((bf16[8,160,1024]{2,1,0:T(8,128)(2,1)}), bf16[8,160,1024]{2,1,0:T(8,128)(2,1)}, u32[]{:S(2)}, u32[]{:S(2)}) %all-to-all-start) | async-done | bytes 2621472 | tf_op jit(solution)/shard_map/all_to_all | solution.py:45
  78.9 3.8 dispatch_rows.1
  82.7 4.3 all-to-all-start.1
  87.0 12.8 %convolution_convert_fusion = bf16[1280,2816]{1,0:T(8,128)(2,1)} fusion(bf16[1280,1024]{1,0:T(8,128)(2,1)} %bitcast.9, bf16[1,2816,1024]{2,1,0:T(8,128)(2,1)} %param.19), kind=kOutput, calls=%fused_computation | convolution fusion | flops 7385579520 | bytes 15597568 | tf_op jit(solution)/shard_map/dot_general | solution.py:31
  99.8 18.3 %all-to-all-done.1 = bf16[8,80,1024]{2,1,0:T(8,128)(2,1)} async-done(((bf16[8,80,1024]{2,1,0:T(8,128)(2,1)}), bf16[8,80,1024]{2,1,0:T(8,128)(2,1)}, u32[]{:S(2)}, u32[]{:S(2)}) %all-to-all-start.1) | async-done | bytes 1310752 | tf_op jit(solution)/shard_map/all_to_all | solution.py:45
  118.0 4.5 all-to-all-start.3
  124.2 36.9 %expert_rows.2 = (bf16[1280,2816]{1,0:T(8,128)(2,1)}, bf16[1280,2816]{1,0:T(8,128)(2,1)}, bf16[1280,2816]{1,0:T(8,128)(2,1)}, bf16[640,1024]{1,0:T(8,128)(2,1)},...) custom-call(s32[4]{0:T(128)} %pad_add_fusion.s_ref.refs_0_.me_ref, ...), custom_call_target="tpu_custom_call" | custom-call | flops 14763950080 | bytes 32178176 | tf_op jit(solution)/shard_map/expert_rows/pallas_call | solution.py:362
  161.2 6.0 %all-to-all-start.2 = ((bf16[8,80,1024]{2,1,0:T(8,128)(2,1)}), bf16[8,80,1024]{2,1,0:T(8,128)(2,1)}, u32[]{:S(2)}, u32[]{:S(2)}) async-start(bf16[8,80,1024]{2,1,0:T(8,128)(2,1)} %bitcast.376), calls=%async_computation.2 | async-start | bytes 2621440 | tf_op jit(solution)/shard_map/all_to_all | solution.py:45
  167.2 36.9 %expert_rows.3 = (bf16[1280,2816]{1,0:T(8,128)(2,1)}, bf16[1280,2816]{1,0:T(8,128)(2,1)}, bf16[1280,2816]{1,0:T(8,128)(2,1)}, bf16[640,1024]{1,0:T(8,128)(2,1)},...) custom-call(s32[4]{0:T(128)} %pad_add_fusion.s_ref.refs_0_.me_ref, ...), custom_call_target="tpu_custom_call", output_to_operand_aliasing={{0}: (8, {}), {1}: (9, {}), {2}: (10, {})} | custom-call | flops 14763950080 | bytes 32178176 | tf_op jit(solution)/shard_map/expert_rows/pallas_call | solution.py:362
  204.1 28.7 %gate_up_grad.1 = (bf16[2,256,5632]{2,1,0:T(8,128)(2,1)}, bf16[2,256,5632]{2,1,0:T(8,128)(2,1)}) custom-call(s32[4]{0:T(128)} %pad_add_fusion.s_ref.refs_0_.me_ref, bf16[640,1024]{1,0:T(8,128)(2,1)} %bitcast.11.refs_1_.refs_0_, bf16[640,1024]{1,0:T(8,128)(2,1)} %bitcast.20.refs_1_, bf16[1280,2816]{1,0:T(8,128)(2,1)} %get-tuple-element.80.refs_2_, ...), custom_call_target="tpu_custom_call" | custom-call | flops 14763950080 | bytes 28573696 | tf_op jit(solution)/shard_map/gate_up_grad/pallas_call | solution.py:500
  232.8 6.5 %all-to-all-start.4 = ((bf16[8,80,1024]{2,1,0:T(8,128)(2,1)}), bf16[8,80,1024]{2,1,0:T(8,128)(2,1)}, u32[]{:S(2)}, u32[]{:S(2)}) async-start(bf16[8,80,1024]{2,1,0:T(8,128)(2,1)} %bitcast.374), calls=%async_computation.4 | async-start | bytes 2621440 | tf_op jit(solution)/shard_map/all_to_all | solution.py:45
  240.1 31.2 %all-to-all-done.4 = bf16[8,80,1024]{2,1,0:T(8,128)(2,1)} async-done(((bf16[8,80,1024]{2,1,0:T(8,128)(2,1)}), bf16[8,80,1024]{2,1,0:T(8,128)(2,1)}, u32[]{:S(2)}, u32[]{:S(2)}) %all-to-all-start.4) | async-done | bytes 1310752 | tf_op jit(solution)/shard_map/all_to_all | solution.py:45
  271.3 12.7 %gated_rows.1 = bf16[8,2,80,1024]{3,2,1,0:T(8,128)(2,1)} custom-call(bf16[1280,2816]{1,0:T(8,128)(2,1)} %get-tuple-element.84.act_ref, bf16[2816,1024]{1,0:T(8,128)(2,1)} %bitcast.384, f32[8,1,80,128]{3,2,1,0:T(8,128)} %get-tuple-element.85.refs_0_, f32[8,1,80,128]{3,2,1,0:T(8,128)} %get-tuple-element.86.refs_1_), custom_call_target="tpu_custom_call" | custom-call | flops 7381975040 | bytes 15597568 | tf_op jit(solution)/shard_map/gated_rows/pallas_call | solution.py:384
  284.1 4.9 fusion.5
  289.0 6.6 %return_rows.1 = (f32[512,1024]{1,0:T(8,128)}, bf16[512,1024]{1,0:T(8,128)(2,1)}, f32[1,1024]{1,0:T(1,128)}) custom-call(s32[512,4]{1,0:T(8,128)} %bitcast.372, f32[512,1024]{1,0:T(8,128)} %copy-done.1, bf16[512,1024]{1,0:T(8,128)(2,1)} %cot_ref.1, f32[1,1024]{1,0:T(1,128)} %copy-done.35, bf16[640,1024]{1,0:T(8,128)(2,1)} %bitcast.18.refs_0_, ...), custom_call_target="tpu_custom_call" | custom-call | flops 1342177280 | bytes 8388608 | tf_op jit(solution)/shard_map/return_rows/pallas_call | solution.py:230
  299.1 30.5 %attention_backward.1 = (bf16[8,2,256,512]{3,2,1,0:T(8,128)(2,1)}, bf16[8,2,256,512]{3,2,1,0:T(8,128)(2,1)}, bf16[3,512,1024]{2,1,0:T(8,128)(2,1)}) custom-call(s32[4]{0:T(128)} %pad_add_fusion.s_ref.refs_0_.me_ref, bf16[512,3072]{1,0:T(8,128)(2,1)} %convolution_convert_fusion.1.q_ref.k_ref.v_ref, ...), custom_call_target="tpu_custom_call" | custom-call | flops 5368709120 | bytes 25165824 | tf_op jit(solution)/shard_map/attention_backward/pallas_call | solution.py:685
  329.6 4.4 all-to-all-start.5
  342.0 4.6 fusion.13
  366.5 15.7 %weight_grads.1 = (bf16[8,2,256,512]{3,2,1,0:T(8,128)(2,1)}, bf16[8,2,256,512]{3,2,1,0:T(8,128)(2,1)}) custom-call(s32[4]{0:T(128)} %pad_add_fusion.s_ref.refs_0_.me_ref, bf16[512,1024]{1,0:T(8,128)(2,1)} %copy-done.29, bf16[512,1024]{1,0:T(8,128)(2,1)} %get-tuple-element.69.o_ref, bf16[3,512,1024]{2,1,0:T(8,128)(2,1)} %get-tuple-element.94.b0_ref.b1_ref.b2_ref, ...), custom_call_target="tpu_custom_call" | custom-call | flops 4294967296 | bytes 14680064 | tf_op jit(solution)/shard_map/weight_grads/pallas_call | solution.py:436
  382.3 20.0 %collective-permute-done.3 = bf16[256,5632]{1,0:T(8,128)(2,1)} collective-permute-done((bf16[256,5632]{1,0:T(8,128)(2,1)}, bf16[256,5632]{1,0:T(8,128)(2,1)}, u32[]{:S(2)}, u32[]{:S(2)}) %collective-permute-start.3) | collective-permute-done | bytes 2883616 | tf_op jit(solution)/shard_map/ppermute | solution.py:41
  402.3 17.5 %out_grad.1 = (bf16[2,704,1024]{2,1,0:T(8,128)(2,1)}, bf16[2,704,1024]{2,1,0:T(8,128)(2,1)}) custom-call(s32[4]{0:T(128)} %pad_add_fusion.s_ref.refs_0_.me_ref, bf16[1280,2816]{1,0:T(8,128)(2,1)} %get-tuple-element.84.act_ref, bf16[640,1024]{1,0:T(8,128)(2,1)} %get-tuple-element.98.refs_0_, bf16[640,1024]{1,0:T(8,128)(2,1)} %get-tuple-element.99.refs_1_), custom_call_target="tpu_custom_call" | custom-call | flops 7381975040 | bytes 15597568 | tf_op jit(solution)/shard_map/out_grad/pallas_call | solution.py:542
  452.7 6.8 %fusion = f32[1,256,5632]{2,1,0:T(8,128)} fusion(bf16[256,5632]{1,0:T(8,128)(2,1)} %collective-permute-done.3, bf16[2,256,5632]{2,1,0:T(8,128)(2,1)} %collective-permute-done, bf16[2,256,5632]{2,1,0:T(8,128)(2,1)S(1)} %bitcast.352), kind=kLoop, calls=%fused_computation.2 | loop fusion | flops 7208960 | bytes 14417920 | tf_op jit(solution)/shard_map/broadcast_in_dim | solution.py:833
  462.2 5.2 combine_rows.1
  469.8 10.2 %collective-permute-done.18 = bf16[2,2,96,512]{3,2,1,0:T(8,128)(2,1)} collective-permute-done((bf16[2,2,96,512]{3,2,1,0:T(8,128)(2,1)}, bf16[2,2,96,512]{3,2,1,0:T(8,128)(2,1)}, u32[]{:S(2)}, u32[]{:S(2)}) %collective-permute-start.18) | collective-permute-done | bytes 393248 | tf_op jit(solution)/shard_map/ppermute | solution.py:41
  493.8 5.6 collective-permute-done.13
  511.8 4.4 fusion.7
  519.5 3.8 collective-permute-done.11
  541.9 4.3 collective-permute-done.7
  (235 shorter events, 140.2 us)
Async XLA Ops:
  11.9 67.0 %all-to-all-start = ((bf16[8,160,1024]{2,1,0:T(8,128)(2,1)}), bf16[8,160,1024]{2,1,0:T(8,128)(2,1)}, u32[]{:S(2)}, u32[]{:S(2)}) async-start(bf16[8,160,1024]{2,1,0:T(8,128)(2,1)} %bitcast.371), calls=%async_computation | async-start | bytes 5242880 | tf_op jit(solution)/shard_map/all_to_all | solution.py:45
  82.7 35.3 %all-to-all-start.1 = ((bf16[8,80,1024]{2,1,0:T(8,128)(2,1)}), bf16[8,80,1024]{2,1,0:T(8,128)(2,1)}, u32[]{:S(2)}, u32[]{:S(2)}) async-start(bf16[8,80,1024]{2,1,0:T(8,128)(2,1)} %bitcast.377), calls=%async_computation.1 | async-start | bytes 2621440 | tf_op jit(solution)/shard_map/all_to_all | solution.py:45
  118.0 43.1 %all-to-all-start.3 = ((bf16[8,80,1024]{2,1,0:T(8,128)(2,1)}), bf16[8,80,1024]{2,1,0:T(8,128)(2,1)}, u32[]{:S(2)}, u32[]{:S(2)}) async-start(bf16[8,80,1024]{2,1,0:T(8,128)(2,1)} %bitcast.375), calls=%async_computation.3 | async-start | bytes 2621440 | tf_op jit(solution)/shard_map/all_to_all | solution.py:45
  161.2 42.9 %all-to-all-start.2 = ((bf16[8,80,1024]{2,1,0:T(8,128)(2,1)}), bf16[8,80,1024]{2,1,0:T(8,128)(2,1)}, u32[]{:S(2)}, u32[]{:S(2)}) async-start(bf16[8,80,1024]{2,1,0:T(8,128)(2,1)} %bitcast.376), calls=%async_computation.2 | async-start | bytes 2621440 | tf_op jit(solution)/shard_map/all_to_all | solution.py:45
  232.8 51.3 %collective-permute-start = (bf16[2,256,5632]{2,1,0:T(8,128)(2,1)}, bf16[2,256,5632]{2,1,0:T(8,128)(2,1)}, u32[]{:S(2)}, u32[]{:S(2)}) collective-permute-start(bf16[2,256,5632]{2,1,0:T(8,128)(2,1)} %get-tuple-element.82), channel_id=1, source_target_pairs={{0,8},{8,0},{16,24},{24,16},{1,9},{9,1},{17,25},{25,17},{2,10},{10... | collective-permute-start | bytes 17301512 | tf_op jit(solution)/shard_map/ppermute | solution.py:41
  232.8 38.5 %all-to-all-start.4 = ((bf16[8,80,1024]{2,1,0:T(8,128)(2,1)}), bf16[8,80,1024]{2,1,0:T(8,128)(2,1)}, u32[]{:S(2)}, u32[]{:S(2)}) async-start(bf16[8,80,1024]{2,1,0:T(8,128)(2,1)} %bitcast.374), calls=%async_computation.4 | async-start | bytes 2621440 | tf_op jit(solution)/shard_map/all_to_all | solution.py:45
  329.6 25.0 %collective-permute-start.1 = (bf16[8,2,256,512]{3,2,1,0:T(8,128)(2,1)}, bf16[8,2,256,512]{3,2,1,0:T(8,128)(2,1)}, u32[]{:S(2)}, u32[]{:S(2)}) collective-permute-start(bf16[8,2,256,512]{3,2,1,0:T(8,128)(2,1)} %get-tuple-element.93), channel_id=1, source_target_pairs={{0,8},{8,0},{16,24},{24,16},{1,9},{9,1},{17,25},{25,17},{2,10},{10... | collective-permute-start | bytes 12582920 | tf_op jit(solution)/shard_map/ppermute | solution.py:41
  329.6 132.6 %all-to-all-start.5 = ((bf16[8,160,1024]{2,1,0:T(8,128)(2,1)}), bf16[8,160,1024]{2,1,0:T(8,128)(2,1)}, u32[]{:S(2)}, u32[]{:S(2)}) async-start(bf16[8,160,1024]{2,1,0:T(8,128)(2,1)} %bitcast.370), calls=%async_computation.5 | async-start | bytes 5242880 | tf_op jit(solution)/shard_map/all_to_all | solution.py:45
  334.0 170.1 %all-gather.4.cloned.1.call-start = ((), (), s32[]{:S(2)}) async-start(), calls=%async_computation.6 | async-start | bytes 2162688 | tf_op jit(solution)/shard_map/all_gather | solution.py:831
  334.2 68.1 %collective-permute-start.3 = (bf16[256,5632]{1,0:T(8,128)(2,1)}, bf16[256,5632]{1,0:T(8,128)(2,1)}, u32[]{:S(2)}, u32[]{:S(2)}) collective-permute-start(bf16[256,5632]{1,0:T(8,128)(2,1)} %fusion.5), channel_id=1, source_target_pairs={{0,16},{8,24},{16,0},{24,8},{1,17},{9,25},{17,1},{25,9},{2,18},{10... | collective-permute-start | bytes 8650760 | tf_op jit(solution)/shard_map/ppermute | solution.py:41
  358.1 69.7 %collective-permute-start.17 = (bf16[2,2,2,96,512]{4,3,1,0,2:T(8,128)(2,1)}, bf16[2,2,2,96,512]{4,3,1,0,2:T(8,128)(2,1)}, u32[]{:S(2)}, u32[]{:S(2)}) collective-permute-start(bf16[2,2,2,96,512]{4,3,1,0,2:T(8,128)(2,1)} %fusion.30), channel_id=1, source_target_pairs={{0,1},{1,0},{2,3},{3,2},{4,5},{5,4},{6,7},{7,6},{8,9},{9,8},{10,11... | collective-permute-start | bytes 2359304 | tf_op jit(solution)/shard_map/ppermute | solution.py:41
  362.0 64.0 %collective-permute-start.19 = (bf16[2,2,2,64,512]{4,3,2,1,0:T(8,128)(2,1)}, bf16[2,2,2,64,512]{4,3,2,1,0:T(8,128)(2,1)}, u32[]{:S(2)}, u32[]{:S(2)}) collective-permute-start(bf16[2,2,2,64,512]{4,3,2,1,0:T(8,128)(2,1)} %fusion.35), channel_id=1, source_target_pairs={{0,2},{1,3},{2,0},{3,1},{4,6},{5,7},{6,4},{7,5},{8,10},{9,11},{10,... | collective-permute-start | bytes 1572872 | tf_op jit(solution)/shard_map/ppermute | solution.py:41
  366.0 65.5 %collective-permute-start.20 = (bf16[2,2,2,96,512]{4,3,0,1,2:T(8,128)(2,1)}, bf16[2,2,2,96,512]{4,3,0,1,2:T(8,128)(2,1)}, u32[]{:S(2)}, u32[]{:S(2)}) collective-permute-start(bf16[2,2,2,96,512]{4,3,0,1,2:T(8,128)(2,1)} %fusion.31), channel_id=1, source_target_pairs={{0,16},{8,24},{16,0},{24,8},{1,17},{9,25},{17,1},{25,9},{2,18},{10... | collective-permute-start | bytes 2359304 | tf_op jit(solution)/shard_map/ppermute | solution.py:41
  382.2 56.7 %collective-permute-start.2 = (bf16[8,2,256,512]{3,2,1,0:T(8,128)(2,1)}, bf16[8,2,256,512]{3,2,1,0:T(8,128)(2,1)}, u32[]{:S(2)}, u32[]{:S(2)}) collective-permute-start(bf16[8,2,256,512]{3,2,1,0:T(8,128)(2,1)} %get-tuple-element.96), channel_id=1, source_target_pairs={{0,8},{8,0},{16,24},{24,16},{1,9},{9,1},{17,25},{25,17},{2,10},{10... | collective-permute-start | bytes 12582920 | tf_op jit(solution)/shard_map/ppermute | solution.py:41
  419.8 15.4 %collective-permute-start.5 = (bf16[2,704,1024]{2,1,0:T(8,128)(2,1)}, bf16[2,704,1024]{2,1,0:T(8,128)(2,1)S(1)}, u32[]{:S(2)}, u32[]{:S(2)}) collective-permute-start(bf16[2,704,1024]{2,1,0:T(8,128)(2,1)} %get-tuple-element.100), channel_id=1, source_target_pairs={{0,8},{8,0},{16,24},{24,16},{1,9},{9,1},{17,25},{25,17},{2,10},{10... | collective-permute-start | bytes 8650760 | tf_op jit(solution)/shard_map/ppermute | solution.py:41
  437.2 74.3 %collective-permute-start.29 = (bf16[704,1024]{1,0:T(8,128)(2,1)}, bf16[704,1024]{1,0:T(8,128)(2,1)}, u32[]{:S(2)}, u32[]{:S(2)}) collective-permute-start(bf16[704,1024]{1,0:T(8,128)(2,1)} %fusion.23), channel_id=1, source_target_pairs={{0,16},{8,24},{16,0},{24,8},{1,17},{9,25},{17,1},{25,9},{2,18},{10... | collective-permute-start | bytes 4325384 | tf_op jit(solution)/shard_map/ppermute | solution.py:41
  446.4 44.4 %collective-permute-start.4 = (bf16[2,2,2,96,512]{4,3,0,1,2:T(8,128)(2,1)}, bf16[2,2,2,96,512]{4,3,0,1,2:T(8,128)(2,1)}, u32[]{:S(2)}, u32[]{:S(2)}) collective-permute-start(bf16[2,2,2,96,512]{4,3,0,1,2:T(8,128)(2,1)} %fusion.32), channel_id=1, source_target_pairs={{0,1},{1,0},{2,3},{3,2},{4,5},{5,4},{6,7},{7,6},{8,9},{9,8},{10,11... | collective-permute-start | bytes 2359304 | tf_op jit(solution)/shard_map/ppermute | solution.py:41
  448.2 37.9 %collective-permute-start.9 = (bf16[2,2,2,64,512]{4,3,2,1,0:T(8,128)(2,1)}, bf16[2,2,2,64,512]{4,3,2,1,0:T(8,128)(2,1)}, u32[]{:S(2)}, u32[]{:S(2)}) collective-permute-start(bf16[2,2,2,64,512]{4,3,2,1,0:T(8,128)(2,1)} %fusion.36), channel_id=1, source_target_pairs={{0,2},{1,3},{2,0},{3,1},{4,6},{5,7},{6,4},{7,5},{8,10},{9,11},{10,... | collective-permute-start | bytes 1572872 | tf_op jit(solution)/shard_map/ppermute | solution.py:41
  449.8 30.2 %collective-permute-start.18 = (bf16[2,2,96,512]{3,2,1,0:T(8,128)(2,1)}, bf16[2,2,96,512]{3,2,1,0:T(8,128)(2,1)}, u32[]{:S(2)}, u32[]{:S(2)}) collective-permute-start(bf16[2,2,96,512]{3,2,1,0:T(8,128)(2,1)} %fusion.40), channel_id=1, source_target_pairs={{0,16},{8,24},{16,0},{24,8},{1,17},{9,25},{17,1},{25,9},{2,18},{10... | collective-permute-start | bytes 1179656 | tf_op jit(solution)/shard_map/ppermute | solution.py:41
  450.2 17.2 %collective-permute-start.23 = (bf16[2,2,64,512]{3,2,1,0:T(8,128)(2,1)}, bf16[2,2,64,512]{3,2,1,0:T(8,128)(2,1)}, u32[]{:S(2)}, u32[]{:S(2)}) collective-permute-start(bf16[2,2,64,512]{3,2,1,0:T(8,128)(2,1)} %fusion.37), channel_id=1, source_target_pairs={{0,4},{1,5},{2,6},{3,7},{4,0},{5,1},{6,2},{7,3},{8,12},{9,13},{10,... | collective-permute-start | bytes 786440 | tf_op jit(solution)/shard_map/ppermute | solution.py:41
  467.4 16.0 %collective-permute-start.26 = (bf16[2,2,96,512]{3,2,0,1:T(8,128)(2,1)}, bf16[2,2,96,512]{3,2,0,1:T(8,128)(2,1)S(1)}, u32[]{:S(2)}, u32[]{:S(2)}) collective-permute-start(bf16[2,2,96,512]{3,2,0,1:T(8,128)(2,1)} %fusion.41), channel_id=1, source_target_pairs={{0,1},{1,0},{2,3},{3,2},{4,5},{5,4},{6,7},{7,6},{8,9},{9,8},{10,11... | collective-permute-start | bytes 1179656 | tf_op jit(solution)/shard_map/ppermute | solution.py:41
  480.0 19.4 %collective-permute-start.13 = (bf16[2,2,2,96,512]{4,3,1,0,2:T(8,128)(2,1)}, bf16[2,2,2,96,512]{4,3,1,0,2:T(8,128)(2,1)S(1)}, u32[]{:S(2)}, u32[]{:S(2)}) collective-permute-start(bf16[2,2,2,96,512]{4,3,1,0,2:T(8,128)(2,1)} %fusion.33), channel_id=1, source_target_pairs={{0,16},{8,24},{16,0},{24,8},{1,17},{9,25},{17,1},{25,9},{2,18},{10... | collective-permute-start | bytes 2359304 | tf_op jit(solution)/shard_map/ppermute | solution.py:41
  488.1 19.7 %collective-permute-start.10 = (bf16[2,2,64,512]{3,2,1,0:T(8,128)(2,1)}, bf16[2,2,64,512]{3,2,1,0:T(8,128)(2,1)}, u32[]{:S(2)}, u32[]{:S(2)}) collective-permute-start(bf16[2,2,64,512]{3,2,1,0:T(8,128)(2,1)} %fusion.38), channel_id=1, source_target_pairs={{0,4},{1,5},{2,6},{3,7},{4,0},{5,1},{6,2},{7,3},{8,12},{9,13},{10,... | collective-permute-start | bytes 786440 | tf_op jit(solution)/shard_map/ppermute | solution.py:41
  500.4 24.5 %collective-permute-start.21 = (bf16[2,96,512]{2,1,0:T(8,128)(2,1)}, bf16[2,96,512]{2,1,0:T(8,128)(2,1)}, u32[]{:S(2)}, u32[]{:S(2)}) collective-permute-start(bf16[2,96,512]{2,1,0:T(8,128)(2,1)} %fusion.47), channel_id=1, source_target_pairs={{0,2},{1,3},{2,0},{3,1},{4,6},{5,7},{6,4},{7,5},{8,10},{9,11},{10,... | collective-permute-start | bytes 589832 | tf_op jit(solution)/shard_map/ppermute | solution.py:41
  502.1 14.7 %collective-permute-start.24 = (bf16[2,64,512]{2,1,0:T(8,128)(2,1)}, bf16[2,64,512]{2,1,0:T(8,128)(2,1)}, u32[]{:S(2)}, u32[]{:S(2)}) collective-permute-start(bf16[2,64,512]{2,1,0:T(8,128)(2,1)} %fusion.43), channel_id=1, source_target_pairs={{0,1},{1,0},{2,3},{3,2},{4,5},{5,4},{6,7},{7,6},{8,9},{9,8},{10,11... | collective-permute-start | bytes 393224 | tf_op jit(solution)/shard_map/ppermute | solution.py:41
  503.6 23.8 %collective-permute-start.27 = (bf16[2,96,512]{2,1,0:T(8,128)(2,1)}, bf16[2,96,512]{2,1,0:T(8,128)(2,1)}, u32[]{:S(2)}, u32[]{:S(2)}) collective-permute-start(bf16[2,96,512]{2,1,0:T(8,128)(2,1)} %fusion.48), channel_id=1, source_target_pairs={{0,2},{1,3},{2,0},{3,1},{4,6},{5,7},{6,4},{7,5},{8,10},{9,11},{10,... | collective-permute-start | bytes 589832 | tf_op jit(solution)/shard_map/ppermute | solution.py:41
  507.8 31.7 %collective-permute-start.6 = (bf16[2,2,96,512]{3,2,1,0:T(8,128)(2,1)}, bf16[2,2,96,512]{3,2,1,0:T(8,128)(2,1)S(1)}, u32[]{:S(2)}, u32[]{:S(2)}) collective-permute-start(bf16[2,2,96,512]{3,2,1,0:T(8,128)(2,1)} %fusion.42), channel_id=1, source_target_pairs={{0,16},{8,24},{16,0},{24,8},{1,17},{9,25},{17,1},{25,9},{2,18},{10... | collective-permute-start | bytes 1179656 | tf_op jit(solution)/shard_map/ppermute | solution.py:41
  511.5 28.4 %collective-permute-start.14 = (bf16[2,2,96,512]{3,2,1,0:T(8,128)(2,1)}, bf16[2,2,96,512]{3,2,1,0:T(8,128)(2,1)S(1)}, u32[]{:S(2)}, u32[]{:S(2)}) collective-permute-start(bf16[2,2,96,512]{3,2,1,0:T(8,128)(2,1)} %fusion.39), channel_id=1, source_target_pairs={{0,1},{1,0},{2,3},{3,2},{4,5},{5,4},{6,7},{7,6},{8,9},{9,8},{10,11... | collective-permute-start | bytes 1179656 | tf_op jit(solution)/shard_map/ppermute | solution.py:41
  523.3 7.7 %collective-permute-start.25 = (bf16[64,512]{1,0:T(8,128)(2,1)S(1)}, bf16[64,512]{1,0:T(8,128)(2,1)S(1)}, u32[]{:S(2)}, u32[]{:S(2)}) collective-permute-start(bf16[64,512]{1,0:T(8,128)(2,1)S(1)} %fusion.58), channel_id=1, source_target_pairs={{0,16},{8,24},{16,0},{24,8},{1,17},{9,25},{17,1},{25,9},{2,18},{10... | collective-permute-start | bytes 196616 | tf_op jit(solution)/shard_map/ppermute | solution.py:41
  524.8 7.7 %collective-permute-start.12 = (bf16[64,512]{1,0:T(8,128)(2,1)S(1)}, bf16[64,512]{1,0:T(8,128)(2,1)S(1)}, u32[]{:S(2)}, u32[]{:S(2)}) collective-permute-start(bf16[64,512]{1,0:T(8,128)(2,1)S(1)} %fusion.60), channel_id=1, source_target_pairs={{0,16},{8,24},{16,0},{24,8},{1,17},{9,25},{17,1},{25,9},{2,18},{10... | collective-permute-start | bytes 196616 | tf_op jit(solution)/shard_map/ppermute | solution.py:41
  527.4 7.4 %collective-permute-start.22 = (bf16[96,512]{1,0:T(8,128)(2,1)S(1)}, bf16[96,512]{1,0:T(8,128)(2,1)S(1)}, u32[]{:S(2)}, u32[]{:S(2)}) collective-permute-start(bf16[96,512]{1,0:T(8,128)(2,1)S(1)} %fusion.52), channel_id=1, source_target_pairs={{0,4},{1,5},{2,6},{3,7},{4,0},{5,1},{6,2},{7,3},{8,12},{9,13},{10,... | collective-permute-start | bytes 294920 | tf_op jit(solution)/shard_map/ppermute | solution.py:41
  540.0 9.5 %collective-permute-start.15 = (bf16[2,96,512]{2,1,0:T(8,128)(2,1)S(1)}, bf16[2,96,512]{2,1,0:T(8,128)(2,1)S(1)}, u32[]{:S(2)}, u32[]{:S(2)}) collective-permute-start(bf16[2,96,512]{2,1,0:T(8,128)(2,1)S(1)} %fusion.46), channel_id=1, source_target_pairs={{0,2},{1,3},{2,0},{3,1},{4,6},{5,7},{6,4},{7,5},{8,10},{9,11},{10,... | collective-permute-start | bytes 589832 | tf_op jit(solution)/shard_map/ppermute | solution.py:41
  (50 other events, 680.2 us)
Sparse Core Ops, SparseCore 0:
  347.4 78.6 all-gather.3

commit v3 on v2

--- a/solution.py
+++ b/solution.py
@@ -49,55 +49,129 @@
     return [1 << i for i in range(n.bit_length() - 1)]
 
 
-def total_of(terms):
-    return sum(t.astype(F32) for t in terms)
-
-
 def after(value, *others):
     return lax.optimization_barrier((value, *others))[0]
 
 
-def next_send(way):
-    terms, order, names = way
-    at = names.index(order[0])
-    return total_of([lax.index_in_dim(t, 1, at, keepdims=False) for t in terms]).astype(BF16)
-
-
-def exchange(way, send):
-    terms, order, names = way
-    at = names.index(order[0])
-    got = xor_send(send, *order[0])
-    kept = [lax.index_in_dim(t, 0, at, keepdims=False) for t in terms]
-    return kept + [got], order[1:], names[:at] + names[at + 1 :]
-
-
-def finish(way):
-    while way[1]:
-        way = exchange(way, next_send(way))
-    return total_of(way[0])
-
-
-def three_ways(keep, got, n_g, n_e):
+def halving_orders(n_g, n_e):
     g_bits = [("grp", k) for k in bits_of(n_g)]
     e_bits = [("ep", k) for k in bits_of(n_e)]
-    names = e_bits[::-1] + g_bits[:0:-1]
     rest, first, others = g_bits[1:], e_bits[:1], e_bits[1:]
-    orders = [first + rest + others, others + first + rest, rest + first + others]
-    rows, cols = keep.shape[2:]
-    cuts = [0, 3 * rows // 8, 5 * rows // 8, rows]
-    view = (2,) * len(names) + (rows, cols)
-    both = [keep.reshape(view), got.reshape(view)]
-    return [
-        ([t[..., cuts[i] : cuts[i + 1], :] for t in both], order, names)
-        for i, order in enumerate(orders)
-    ]
-
-
-def group_way(keep, got, n_g):
-    g_bits = [("grp", k) for k in bits_of(n_g)]
-    names = g_bits[:0:-1]
-    view = (2,) * len(names) + keep.shape[1:]
-    return [keep.reshape(view), got.reshape(view)], g_bits[1:], names
+    return [first + rest + others, others + first + rest, rest + first + others]
+
+
+def row_cuts(rows):
+    unit = rows // 16
+    return [0, 16 * round(3 * unit / 8), 16 * round(5 * unit / 8), rows]
+
+
+def first_kernel(orders, cuts, k_ref, g_ref, *outs):
+    r = pl.program_id(0)
+    bit = lambda x, axis, k: (2 * x // k) % 2 if axis == "grp" else (r // k) % 2
+    for x in range(k_ref.shape[1]):
+        at = 0
+        for order, lo, hi in zip(orders, cuts, cuts[1:]):
+            if lo == hi:
+                continue
+            total = (k_ref[0, x, lo:hi, :].astype(F32) + g_ref[0, x, lo:hi, :].astype(F32)).astype(BF16)
+            index = 0
+            for step in order[1:]:
+                index = 2 * index + bit(x, *step)
+            goes = bit(x, *order[0])
+            for side in range(2):
+
+                @pl.when(goes == side)
+                def _():
+                    outs[at + side][index] = total
+
+            at += 2
+
+
+def first_sums(keep, got, orders):
+    n_e, n_x, rows, cols = keep.shape
+    cuts = row_cuts(rows)
+    used = [(o, hi - lo) for o, lo, hi in zip(orders, cuts, cuts[1:]) if hi > lo]
+    half = n_e * n_x // 2
+    shapes = [jax.ShapeDtypeStruct((half, n, cols), BF16) for _, n in used for _ in range(2)]
+    out = pl.pallas_call(
+        functools.partial(first_kernel, orders, cuts),
+        grid=(n_e,),
+        in_specs=[pl.BlockSpec((1, n_x, rows, cols), lambda r: (r, 0, 0, 0))] * 2,
+        out_specs=[pl.BlockSpec(s.shape, lambda r: (0, 0, 0)) for s in shapes],
+        out_shape=shapes,
+        compiler_params=params(),
+        cost_estimate=cost(n_e * n_x * rows * cols, 6 * n_e * n_x * rows * cols),
+        name="first_sums",
+    )(keep, got)
+    return [(out[2 * i], out[2 * i + 1], o) for i, (o, _) in enumerate(used)]
+
+
+def split_kernel(n_way, n_set, *refs):
+    ins, outs = refs[: 2 * n_way * n_set], refs[2 * n_way * n_set :]
+    for w in range(n_way):
+        keep_ref, send_ref = outs[2 * w : 2 * w + 2]
+        half, at = keep_ref.shape[0], 0
+        for i in range(n_set):
+            k_ref, g_ref = ins[2 * (w * n_set + i) : 2 * (w * n_set + i) + 2]
+            to = at + k_ref.shape[1]
+            keep_ref[:, at:to, :] = (k_ref[:half].astype(F32) + g_ref[:half].astype(F32)).astype(BF16)
+            send_ref[:, at:to, :] = (k_ref[half:].astype(F32) + g_ref[half:].astype(F32)).astype(BF16)
+            at = to
+
+
+def next_sums(sets):
+    ways = list(zip(*sets))
+    shapes = []
+    for way in ways:
+        blocks, _, cols = way[0][0].shape
+        shape = jax.ShapeDtypeStruct((blocks // 2, sum(one[0].shape[1] for one in way), cols), BF16)
+        shapes += [shape, shape]
+    ins = [v for way in ways for one in way for v in one[:2]]
+    total = sum(math.prod(s.shape) for s in shapes)
+    out = pl.pallas_call(
+        functools.partial(split_kernel, len(ways), len(sets)),
+        out_shape=shapes,
+        compiler_params=params(),
+        cost_estimate=cost(total, 6 * total),
+        name="split_sums",
+    )(*ins)
+    return [(out[2 * i], out[2 * i + 1], way[0][2]) for i, way in enumerate(ways)]
+
+
+def send_all(ways):
+    return [(keep, xor_send(send, *order[0]), order[1:]) for keep, send, order in ways]
+
+
+def last_sums(ways):
+    return [(keep[0].astype(F32) + got[0].astype(F32)) for keep, got, _ in ways]
+
+
+def last_kernel(*refs):
+    ins, (bias_ref, qkv_ref, out_ref) = refs[:-3], refs[-3:]
+    wide = qkv_ref.shape[1]
+    at = 0
+    for k_ref, g_ref in zip(ins[0::2], ins[1::2]):
+        n = k_ref.shape[1] // 2
+        total = k_ref[0].astype(F32) + g_ref[0].astype(F32)
+        bias_ref[at : at + n, :] = total[:n]
+        qkv_ref[at : at + n, :] = total[n:, :wide]
+        out_ref[at : at + n, :] = total[n:, wide:]
+        at += n
+
+
+def last_merged(ways, wide):
+    rows, cols = sum(w[0].shape[1] for w in ways) // 2, ways[0][0].shape[2]
+    return pl.pallas_call(
+        last_kernel,
+        out_shape=[jax.ShapeDtypeStruct((rows, n), F32) for n in (cols, wide, cols - wide)],
+        compiler_params=params(),
+        cost_estimate=cost(2 * rows * cols, 16 * rows * cols),
+        name="last_sums",
+    )(*[v for w in ways for v in w[:2]])
+
+
+def tied(ways, *others):
+    return [(after(ways[0][0], *others), *ways[0][1:])] + ways[1:]
 
 
 def place_kernel(experts, cap, chunks, routes_ref, v_ref, pos_ref, out_ref):
@@ -469,8 +543,8 @@
     return view[:, 0::2], view[:, 1::2]
 
 
-def gate_up_kernel(n_g, half, n_part, me_ref, *refs):
-    parts, (g_ref, u_ref, keep_ref, send_ref, full_ref, t_ref) = refs[:n_part], refs[n_part:]
+def gate_up_kernel(half, n_part, *refs):
+    parts, (g_ref, u_ref, out_ref, t_ref) = refs[:n_part], refs[n_part:]
     j = pl.program_id(0)
 
     @pl.when(j == 0)
@@ -482,78 +556,61 @@
 
     @pl.when(j < half)
     def _():
-        full_ref[...] = dot_f32(t_ref[...], g_ref[...], NN)
+        out_ref[...] = dot_f32(t_ref[...], g_ref[...], NN).astype(BF16)
 
     @pl.when(j >= half)
     def _():
-        full_ref[...] = dot_f32(t_ref[...], u_ref[...], NN)
-
-    share_rows(me_ref[0], n_g, full_ref, keep_ref, send_ref)
-
-
-def gate_up_grad(me, parts, dg, du, n_g):
+        out_ref[...] = dot_f32(t_ref[...], u_ref[...], NN).astype(BF16)
+
+
+def gate_up_grad(parts, dg, du):
     total, ff = dg.shape
     width = parts[0].shape[1]
     tile = 256
     half = ff // tile
-    spec = pl.BlockSpec((n_g // 2, width // n_g, tile), lambda j, m: (0, 0, j))
-    return pl.pallas_call(
-        functools.partial(gate_up_kernel, n_g, half, len(parts)),
-        grid_spec=pltpu.PrefetchScalarGridSpec(
-            num_scalar_prefetch=1,
-            grid=(2 * half,),
-            in_specs=[pl.BlockSpec(p.shape, lambda j, m: (0, 0)) for p in parts]
-            + [
-                pl.BlockSpec((total, tile), lambda j, m: (0, jnp.minimum(j, half - 1))),
-                pl.BlockSpec((total, tile), lambda j, m: (0, jnp.maximum(j - half, 0))),
-            ],
-            out_specs=[spec, spec],
-            scratch_shapes=[pltpu.VMEM((width, tile), F32), pltpu.VMEM((width, total), BF16)],
-        ),
-        out_shape=[jax.ShapeDtypeStruct((n_g // 2, width // n_g, 2 * ff), BF16)] * 2,
+    return pl.pallas_call(
+        functools.partial(gate_up_kernel, half, len(parts)),
+        grid=(2 * half,),
+        in_specs=[pl.BlockSpec(p.shape, lambda j: (0, 0)) for p in parts]
+        + [
+            pl.BlockSpec((total, tile), lambda j: (0, jnp.minimum(j, half - 1))),
+            pl.BlockSpec((total, tile), lambda j: (0, jnp.maximum(j - half, 0))),
+        ],
+        out_specs=pl.BlockSpec((width, tile), lambda j: (0, j)),
+        scratch_shapes=[pltpu.VMEM((width, total), BF16)],
+        out_shape=jax.ShapeDtypeStruct((width, 2 * ff), BF16),
         compiler_params=params(),
         cost_estimate=cost(4 * total * width * ff, 2 * total * (width + 2 * ff) + 4 * width * ff),
         name="gate_up_grad",
-    )(me, *parts, dg, du)
-
-
-def out_grad_kernel(n_g, n_part, me_ref, act_ref, *refs):
-    parts, (keep_ref, send_ref, full_ref, t_ref) = refs[:n_part], refs[n_part:]
-
-    @pl.when(pl.program_id(0) == 0)
-    def _():
-        t_ref[...] = act_ref[...].T
-
+    )(*parts, dg, du)
+
+
+def out_grad_kernel(n_part, act_ref, *refs):
+    parts, out_ref = refs[:n_part], refs[n_part]
     total, at = None, 0
     for part in parts:
         n = part.shape[0]
-        term = dot_f32(t_ref[:, at : at + n], part[...], NN)
+        term = dot_f32(act_ref[at : at + n, :], part[...], TN)
         total = term if total is None else total + term
         at += n
-    full_ref[...] = total
-    share_rows(me_ref[0], n_g, full_ref, keep_ref, send_ref)
-
-
-def out_grad(me, act, parts, n_g):
+    out_ref[...] = total.astype(BF16)
+
+
+def out_grad(act, parts):
     total, ff = act.shape
     width = parts[0].shape[1]
     tile = 256
-    spec = pl.BlockSpec((n_g // 2, ff // n_g, tile), lambda j, m: (0, 0, j))
-    return pl.pallas_call(
-        functools.partial(out_grad_kernel, n_g, len(parts)),
-        grid_spec=pltpu.PrefetchScalarGridSpec(
-            num_scalar_prefetch=1,
-            grid=(width // tile,),
-            in_specs=[pl.BlockSpec((total, ff), lambda j, m: (0, 0))]
-            + [pl.BlockSpec((p.shape[0], tile), lambda j, m: (0, j)) for p in parts],
-            out_specs=[spec, spec],
-            scratch_shapes=[pltpu.VMEM((ff, tile), F32), pltpu.VMEM((ff, total), BF16)],
-        ),
-        out_shape=[jax.ShapeDtypeStruct((n_g // 2, ff // n_g, width), BF16)] * 2,
+    return pl.pallas_call(
+        functools.partial(out_grad_kernel, len(parts)),
+        grid=(ff // tile,),
+        in_specs=[pl.BlockSpec((total, tile), lambda j: (0, j))]
+        + [pl.BlockSpec(p.shape, lambda j: (0, 0)) for p in parts],
+        out_specs=pl.BlockSpec((tile, width), lambda j: (j, 0)),
+        out_shape=jax.ShapeDtypeStruct((ff, width), BF16),
         compiler_params=params(),
         cost_estimate=cost(2 * total * width * ff, 2 * total * (width + ff) + 2 * width * ff),
         name="out_grad",
-    )(me, act, *parts)
+    )(act, *parts)
 
 
 def fill_mask(start, length, mask_ref):
@@ -780,32 +837,32 @@
     act, dg, du = state
 
     core = ("grp", 1)
-    gate_keep, gate_out = gate_up_grad(me, parts, after(dg, *back[:-1]), du, n_g)
-    gate = group_way(gate_keep, xor_send(gate_out, *core), n_g)
-    gated = gated_rows(after(act, gate_out, *back), w_eo, owns).reshape(slots, width)
-    gate_send = next_send(gate)
-    gate = exchange(gate, gate_send)
+    share = lambda v: lax.psum_scatter(v, "grp", scatter_dimension=0, tiled=True)
+    gated = gated_rows(after(act, *back[:-1]), w_eo, owns).reshape(slots, width)
+    gate_full = gate_up_grad(parts, after(dg, gated), du)
+    gate = share(after(gate_full, *back))
 
     grad_after, grad_attn_low, grad_gain_two = return_grads(
-        pos_cols, after_attn, cotangent, norm_gains[1:], [after(back[0], gated, gate_send)] + back[1:]
+        pos_cols, after(after_attn, gate_full), cotangent, norm_gains[1:], back
     )
     gated = swap_rows(after(gated, *back))
     grad_mixed = dot_f32(grad_attn_low, w_out_attn, NT).astype(BF16)
     rows_g, rows_t = width // n_g, tok // n_g
     per_owner = n_e * LANES == width
+    orders = halving_orders(n_g, n_e)
     *grad_bias, grad_qkv = attention_backward(
         me, qkv_rows, grad_mixed, rel_bias, lse, scale, n_g, n_e, per_owner
     )
     if not per_owner:
         bias = grad_bias[0].reshape(n_e, HEADS // n_e, n_g, rows_t, tok).transpose(0, 2, 1, 3, 4)
         grad_bias = own_blocks(bias.reshape(n_e, n_g, -1, tok), me_g, me_e, n_g, n_e)
-    bias = three_ways(grad_bias[0], xor_send(grad_bias[1], *core), n_g, n_e)
+    got = xor_send(grad_bias[1], *core)
     grad_a_one = sum(
         dot_f32(grad_qkv[i], w_qkv[:, i * width : (i + 1) * width], NT) for i in range(3)
     )
-    sends = [next_send(way) for way in bias]
-    bias = [exchange(way, send) for way, send in zip(bias, sends)]
-    grad_qkv_late = after(grad_qkv, *sends)
+    bias = first_sums(after(grad_bias[0], grad_a_one), got, orders)
+    grad_qkv_late = after(grad_qkv, bias[0][0])
+    bias = send_all(bias)
     if per_owner:
         weights = weight_grads(me, a_one, mixed_heads, grad_qkv_late, grad_attn_low, n_g, n_e)
     else:
@@ -814,38 +871,40 @@
         full = [f.astype(BF16).reshape(n_g, rows_g, n_e, -1) for f in full]
         full = jnp.concatenate(full, axis=-1).transpose(2, 0, 1, 3)
         weights = own_blocks(full, me_g, me_e, n_g, n_e)
-    deos[0] = after(deos[0], weights[1], gate[0][-1])
-    weights = three_ways(weights[0], xor_send(weights[1], *core), n_g, n_e)
-    out_keep, out_send = out_grad(me, act, deos, n_g)
-    expert_out = group_way(out_keep, xor_send(out_send, *core), n_g)
-    sends = [after(next_send(way), out_send) for way in weights]
-    weights = [exchange(way, send) for way, send in zip(weights, sends)]
-    output = combine(pos_cols, after(after_attn, *sends), gated)
-    out_send = next_send(expert_out)
-    expert_out = exchange(expert_out, out_send)
-    sends = [after(next_send(way), *sends) for way in bias]
-    bias = [exchange(way, send) for way, send in zip(bias, sends)]
+    out_full = out_grad(act, [after(deos[0], weights[0])] + deos[1:])
+    got = xor_send(after(weights[1], *[way[1] for way in bias]), *core)
+    weights = first_sums(after(weights[0], out_full), got, orders)
+    first_keep = weights[0][0]
+    expert_out = share(after(out_full, first_keep))
+    weights = send_all(weights)
+    output = combine(pos_cols, after(after_attn, first_keep), gated)
     grad_norm_one, grad_gain_one = norm_backward(grad_a_one, normed_one, inverse_one, norm_gains[0])
     grad_tokens = grad_after + grad_norm_one
     small = jnp.concatenate([grad_gain_one[None], grad_gain_two, grad_route])
-    small = lax.all_gather(small, ("grp", "ep"))
-    gate[0][-1] = after(gate[0][-1], *sends)
-    grad_w_gate = finish(gate)[None]
-    sends = [after(next_send(way), out_send) for way in weights]
-    weights = [exchange(way, send) for way, send in zip(weights, sends)]
-    sends = [after(next_send(way), grad_w_gate, output, *sends) for way in bias]
-    bias = [exchange(way, send) for way, send in zip(bias, sends)]
-    expert_out[0][0] = after(expert_out[0][0], *sends)
-    grad_w_expert = finish(expert_out)[None]
-    small = jnp.sum(after(small, *sends), axis=0)
-    g_bias = jnp.concatenate([finish(way) for way in bias]).reshape(HEADS // n_e, rows_t, tok)
-    g_weights = jnp.concatenate([finish(way) for way in weights])
+    for axis, k in [("grp", k) for k in bits_of(n_g)] + [("ep", k) for k in bits_of(n_e)]:
+        small = small + xor_send(small, axis, k)
+    grad_w_gate = after(gate, first_keep).astype(F32)[None]
     wide = 3 * width // n_e
+    merged = [[bias, weights]] if bias[0][0].shape == weights[0][0].shape else [[bias], [weights]]
+    ways = [send_all(next_sums(sets)) for sets in merged]
+    ways[0] = tied(ways[0], grad_w_gate, grad_tokens)
+    while ways[0][0][2]:
+        if len(ways[0][0][2]) == 1:
+            ways[0] = tied(ways[0], output)
+        ways = [send_all(next_sums([w])) for w in ways]
+    grad_w_expert = expert_out.astype(F32)[None]
+    ways[0] = tied(ways[0], grad_w_expert)
+    if len(ways) == 1:
+        g_bias, g_qkv, g_out = last_merged(ways[0], wide)
+    else:
+        g_bias, g_weights = [jnp.concatenate(last_sums(w)) for w in ways]
+        g_qkv, g_out = g_weights[:, :wide], g_weights[:, wide:]
+    g_bias = g_bias.reshape(HEADS // n_e, rows_t, tok)
     return (
         output,
         grad_tokens,
-        g_weights[:, :wide],
-        g_weights[:, wide:],
+        g_qkv,
+        g_out,
         g_bias,
         small[:2],
         small[2:].T,

time: 575 us -> 554 us (0.963)
  other arithmetic: 66.3 us -> 16.2 us
  waiting for transfers between devices: 128 us -> 158 us
  Pallas kernels: 219 us -> 247 us
  local copies, waits for them, and re-layouts: 32.3 us -> 10.3 us
    ppermute x30 -> x22, waiting for transfers between devices: 55.2 us -> 116 us  [xor_send(): return lax.ppermute(v, axis, [(i, i ^ k) for i in range(n)])]
    convert_element_type x22 -> x0, other arithmetic: 32.3 us -> none  [next_send(): total_of([lax.index_in_dim(t, 1, at, keepdims=False) for t in terms])]
    all_to_all x6, waiting for transfers between devices: 72.5 us -> 41.2 us  [swap_rows(): return lax.all_to_all(v, 'ep', split_axis=0, concat_axis=0, tiled=True)]
    pallas_call x2 -> x8, Pallas kernels: 46.2 us -> 72.8 us  [the longest x1 27.3 us: gate_up_grad(): pl.pallas_call(functools.partial(gate_up_kernel, half, len(parts)), grid=...]
    squeeze x15 -> x0, local copies, waits for them, and re-layouts: 13.6 us -> none  [exchange(): kept = [lax.index_in_dim(t, 0, at, keepdims=False) for t in terms]]
    ppermute x30 -> x22, starting transfers between devices: 33.8 us -> 20.8 us  [xor_send(): return lax.ppermute(v, axis, [(i, i ^ k) for i in range(n)])]
    slice x8 -> x1, local copies, waits for them, and re-layouts: 9.01 us -> 0.01 us  [body(): a_two = (normed_two * norm_gains[1]).astype(BF16)]
    reduce_scatter x0 -> x2, starting transfers between devices: none -> 8.81 us  [body(): lax.psum_scatter(v, 'grp', scatter_dimension=0, tiled=True)]
  transfers between devices with their start and end apart: 37 -> 30, of which waited for: 13 -> 12; matrix products, arithmetic and copies ran while one was open for 21% -> 11% of each run, Pallas kernels for 26% -> 43%
where the time goes in v3:
time: 554 us; the launch traced here: 547 us
  Pallas kernels  247 us (45%)
  waiting for transfers between devices  158 us (29%)
  starting transfers between devices  63.5 us (11%)
  matrix products  37.3 us (7%)
  other arithmetic  16.2 us (3%)
  between operations  14.6 us (3%)
  local copies, waits for them, and re-layouts  10.3 us (2%)
    ppermute x22, waiting for transfers between devices, xor_send(): return lax.ppermute(v, axis, [(i, i ^ k) for i in range(n)])  116 us
    pallas_call x2, Pallas kernels, expert_chunk(): call(me, rows, cot, dact, w_gate_up, w_gate_up, wr_pad, wr_pad_t, *(earli...  73.9 us
    all_to_all x6, waiting for transfers between devices, swap_rows(): return lax.all_to_all(v, 'ep', split_axis=0, concat_axis=0, tiled=True)  41.2 us
    dot_general x7, matrix products, dot_f32(): return lax.dot_general(a, b, (dims, ((), ())), preferred_element_type=F32)  37.3 us
    all_to_all x6, starting transfers between devices, swap_rows(): return lax.all_to_all(v, 'ep', split_axis=0, concat_axis=0, tiled=True)  33.9 us
    pallas_call x1, Pallas kernels, attention_backward(): pl.pallas_call(functools.partial(backward_kernel, n_g, scale, per_owner),...  30.3 us
    pallas_call x1, Pallas kernels, gate_up_grad(): pl.pallas_call(functools.partial(gate_up_kernel, half, len(parts)), grid=...  27.3 us
    ppermute x22, starting transfers between devices, xor_send(): return lax.ppermute(v, axis, [(i, i ^ k) for i in range(n)])  20.8 us
  transfers between devices with their start and end apart: 30, of which 12 were waited for; matrix products, arithmetic and copies ran while one was open for 11% of the time, Pallas kernels for 43%

profile of v3, /device:TPU:0, one launch (start us, length us, event | category | flops | bytes accessed | tf_op | source)
XLA Modules:
  0.0 546.7 jit_solution(14566351996875299458)
XLA Ops:
  7.2 4.7 place_rows.1
  11.9 7.4 %all-to-all-start = ((bf16[8,160,1024]{2,1,0:T(8,128)(2,1)}), bf16[8,160,1024]{2,1,0:T(8,128)(2,1)}, u32[]{:S(2)}, u32[]{:S(2)}) async-start(bf16[8,160,1024]{2,1,0:T(8,128)(2,1)} %bitcast.64), calls=%async_computation | async-start | bytes 5242880 | tf_op jit(solution)/shard_map/all_to_all | solution.py:45
  23.5 7.6 %convolution_convert_fusion.1.q_ref.k_ref.v_ref = bf16[512,3072]{1,0:T(8,128)(2,1)} fusion(bf16[512,1024]{1,0:T(8,128)(2,1)S(1)} %fusion.4.a_ref, bf16[1024,3072]{1,0:T(8,128)(2,1)} %param.13), kind=kOutput, calls=%fused_computation.1 | convolution fusion | flops 3222798336 | bytes 10485760 | tf_op jit(solution)/shard_map/dot_general | solution.py:31
  31.0 19.9 %attention_forward.1 = (bf16[512,1024]{1,0:T(8,128)(2,1)}, f32[512,128]{1,0:T(8,128)}) custom-call(s32[4]{0:T(128)} %pad_add_fusion.s_ref.refs_0_.me_ref, bf16[512,3072]{1,0:T(8,128)(2,1)} %convolution_convert_fusion.1.q_ref.k_ref.v_ref, bf16[512,3072]{1,0:T(8,128)(2,1)} %convolution_convert_fusion.1.q_ref.k_ref.v_ref, ...), custom_call_target="tpu_custom_call" | custom-call | flops 2147483648 | bytes 12582912 | tf_op jit(solution)/shard_map/attention_forward/pallas_call | solution.py:662
  56.0 22.9 %all-to-all-done = bf16[8,160,1024]{2,1,0:T(8,128)(2,1)} async-done(((bf16[8,160,1024]{2,1,0:T(8,128)(2,1)}), bf16[8,160,1024]{2,1,0:T(8,128)(2,1)}, u32[]{:S(2)}, u32[]{:S(2)}) %all-to-all-start) | async-done | bytes 2621472 | tf_op jit(solution)/shard_map/all_to_all | solution.py:45
  87.0 12.7 %convolution_convert_fusion = bf16[1280,2816]{1,0:T(8,128)(2,1)} fusion(bf16[1280,1024]{1,0:T(8,128)(2,1)} %bitcast.9, bf16[1,2816,1024]{2,1,0:T(8,128)(2,1)} %param.19), kind=kOutput, calls=%fused_computation | convolution fusion | flops 7385579520 | bytes 15597568 | tf_op jit(solution)/shard_map/dot_general | solution.py:31
  99.8 18.3 %all-to-all-done.1 = bf16[8,80,1024]{2,1,0:T(8,128)(2,1)} async-done(((bf16[8,80,1024]{2,1,0:T(8,128)(2,1)}), bf16[8,80,1024]{2,1,0:T(8,128)(2,1)}, u32[]{:S(2)}, u32[]{:S(2)}) %all-to-all-start.1) | async-done | bytes 1310752 | tf_op jit(solution)/shard_map/all_to_all | solution.py:45
  124.2 36.9 %expert_rows.2 = (bf16[1280,2816]{1,0:T(8,128)(2,1)}, bf16[1280,2816]{1,0:T(8,128)(2,1)}, bf16[1280,2816]{1,0:T(8,128)(2,1)}, bf16[640,1024]{1,0:T(8,128)(2,1)},...) custom-call(s32[4]{0:T(128)} %pad_add_fusion.s_ref.refs_0_.me_ref, ...), custom_call_target="tpu_custom_call" | custom-call | flops 14763950080 | bytes 32178176 | tf_op jit(solution)/shard_map/expert_rows/pallas_call | solution.py:436
  161.2 6.0 %all-to-all-start.3 = ((bf16[8,80,1024]{2,1,0:T(8,128)(2,1)}), bf16[8,80,1024]{2,1,0:T(8,128)(2,1)}, u32[]{:S(2)}, u32[]{:S(2)}) async-start(bf16[8,80,1024]{2,1,0:T(8,128)(2,1)} %bitcast.69), calls=%async_computation.3 | async-start | bytes 2621440 | tf_op jit(solution)/shard_map/all_to_all | solution.py:45
  167.2 36.9 %expert_rows.3 = (bf16[1280,2816]{1,0:T(8,128)(2,1)}, bf16[1280,2816]{1,0:T(8,128)(2,1)}, bf16[1280,2816]{1,0:T(8,128)(2,1)}, bf16[640,1024]{1,0:T(8,128)(2,1)},...) custom-call(s32[4]{0:T(128)} %pad_add_fusion.s_ref.refs_0_.me_ref, ...), custom_call_target="tpu_custom_call", output_to_operand_aliasing={{0}: (8, {}), {1}: (9, {}), {2}: (10, {})} | custom-call | flops 14763950080 | bytes 32178176 | tf_op jit(solution)/shard_map/expert_rows/pallas_call | solution.py:436
  204.1 6.0 %all-to-all-start.4 = ((bf16[8,80,1024]{2,1,0:T(8,128)(2,1)}), bf16[8,80,1024]{2,1,0:T(8,128)(2,1)}, u32[]{:S(2)}, u32[]{:S(2)}) async-start(bf16[8,80,1024]{2,1,0:T(8,128)(2,1)} %bitcast.67), calls=%async_computation.4 | async-start | bytes 2621440 | tf_op jit(solution)/shard_map/all_to_all | solution.py:45
  210.2 12.7 %gated_rows.1 = bf16[8,2,80,1024]{3,2,1,0:T(8,128)(2,1)} custom-call(bf16[1280,2816]{1,0:T(8,128)(2,1)} %get-tuple-element.103.act_ref, bf16[2816,1024]{1,0:T(8,128)(2,1)} %bitcast.77, f32[8,1,80,128]{3,2,1,0:T(8,128)} %get-tuple-element.104.refs_0_, f32[8,1,80,128]{3,2,1,0:T(8,128)} %get-tuple-element.105.refs_1_), custom_call_target="tpu_custom_call" | custom-call | flops 7381975040 | bytes 15597568 | tf_op jit(solution)/shard_map/gated_rows/pallas_call | solution.py:458
  222.9 27.3 %gate_up_grad.1 = bf16[1024,5632]{1,0:T(8,128)(2,1)} custom-call(bf16[640,1024]{1,0:T(8,128)(2,1)} %bitcast.11.refs_1_.refs_0_, bf16[640,1024]{1,0:T(8,128)(2,1)} %bitcast.14.refs_1_, bf16[1280,2816]{1,0:T(8,128)(2,1)} %get-tuple-element.106.refs_2_, bf16[1280,2816]{1,0:T(8,128)(2,1)} %get-tuple-element.107.refs_3_), custom_call_target="tpu_custom_call" | custom-call | flops 14763950080 | bytes 28573696 | tf_op jit(solution)/shard_map/gate_up_grad/pallas_call | solution.py:571
  250.2 8.8 %reduce-scatter.5.cloned.1.call-start = ((), (), s32[]{:S(2)}) async-start(), calls=%async_computation.9 | async-start | bytes 7208960 | tf_op jit(solution)/shard_map/reduce_scatter | solution.py:840
  259.9 8.5 %return_rows.1 = (f32[512,1024]{1,0:T(8,128)}, bf16[512,1024]{1,0:T(8,128)(2,1)}, f32[1,1024]{1,0:T(1,128)}) custom-call(s32[512,4]{1,0:T(8,128)} %bitcast.65, f32[512,1024]{1,0:T(8,128)} %copy-done.1, bf16[512,1024]{1,0:T(8,128)(2,1)} %cot_ref.1, f32[1,1024]{1,0:T(1,128)} %copy-done.14, bf16[640,1024]{1,0:T(8,128)(2,1)} %bitcast.20.refs_0_, ...), custom_call_target="tpu_custom_call" | custom-call | flops 1342177280 | bytes 8388608 | tf_op jit(solution)/shard_map/return_rows/pallas_call | solution.py:304
  271.9 30.3 %attention_backward.1 = (bf16[8,2,256,512]{3,2,1,0:T(8,128)(2,1)}, bf16[8,2,256,512]{3,2,1,0:T(8,128)(2,1)}, bf16[3,512,1024]{2,1,0:T(8,128)(2,1)}) custom-call(s32[4]{0:T(128)} %pad_add_fusion.s_ref.refs_0_.me_ref, bf16[512,3072]{1,0:T(8,128)(2,1)} %convolution_convert_fusion.1.q_ref.k_ref.v_ref, ...), custom_call_target="tpu_custom_call" | custom-call | flops 5368709120 | bytes 25165824 | tf_op jit(solution)/shard_map/attention_backward/pallas_call | solution.py:742
  308.6 4.6 fusion.9
  313.1 8.0 %first_sums.2 = (bf16[8,96,512]{2,1,0:T(8,128)(2,1)}, bf16[8,96,512]{2,1,0:T(8,128)(2,1)}, bf16[8,64,512]{2,1,0:T(8,128)(2,1)}, bf16[8,64,512]{2,1,0:T(8,128)(2,...) custom-call(bf16[8,2,256,512]{3,2,1,0:T(8,128)(2,1)} %get-tuple-element.114.k_ref, ...), custom_call_target="tpu_custom_call" | custom-call | flops 2097152 | bytes 12582912 | tf_op jit(solution)/shard_map/first_sums/pallas_call | solution.py:96
  326.2 15.8 %weight_grads.1 = (bf16[8,2,256,512]{3,2,1,0:T(8,128)(2,1)}, bf16[8,2,256,512]{3,2,1,0:T(8,128)(2,1)}) custom-call(s32[4]{0:T(128)} %pad_add_fusion.s_ref.refs_0_.me_ref, bf16[512,1024]{1,0:T(8,128)(2,1)} %copy-done.3, bf16[512,1024]{1,0:T(8,128)(2,1)} %get-tuple-element.92.o_ref, bf16[3,512,1024]{2,1,0:T(8,128)(2,1)} %get-tuple-element.117.b0_ref.b1_ref.b2_ref, ...), custom_call_target="tpu_custom_call" | custom-call | flops 4294967296 | bytes 14680064 | tf_op jit(solution)/shard_map/weight_grads/pallas_call | solution.py:510
  342.0 15.8 %collective-permute-done.3.refs_9_ = bf16[8,96,512]{2,1,0:T(8,128)(2,1)} collective-permute-done((bf16[8,96,512]{2,1,0:T(8,128)(2,1)}, bf16[8,96,512]{2,1,0:T(8,128)(2,1)}, u32[]{:S(2)}, u32[]{:S(2)}) %collective-permute-start.3) | collective-permute-done | bytes 786464 | tf_op jit(solution)/shard_map/ppermute | solution.py:41
  357.9 15.3 %out_grad.1 = bf16[2816,1024]{1,0:T(8,128)(2,1)} custom-call(bf16[1280,2816]{1,0:T(8,128)(2,1)} %get-tuple-element.103.act_ref, bf16[640,1024]{1,0:T(8,128)(2,1)} %get-tuple-element.120.refs_0_, bf16[640,1024]{1,0:T(8,128)(2,1)} %get-tuple-element.121.refs_1_), custom_call_target="tpu_custom_call" | custom-call | flops 7381975040 | bytes 15597568 | tf_op jit(solution)/shard_map/out_grad/pallas_call | solution.py:603
  373.2 8.3 %first_sums.3 = (bf16[8,96,512]{2,1,0:T(8,128)(2,1)}, bf16[8,96,512]{2,1,0:T(8,128)(2,1)}, bf16[8,64,512]{2,1,0:T(8,128)(2,1)}, bf16[8,64,512]{2,1,0:T(8,128)(2,...) custom-call(bf16[8,2,256,512]{3,2,1,0:T(8,128)(2,1)} %get-tuple-element.122.k_ref, ...), custom_call_target="tpu_custom_call" | custom-call | flops 2097152 | bytes 12582912 | tf_op jit(solution)/shard_map/first_sums/pallas_call | solution.py:96
  381.5 5.7 %all-to-all-start.5 = ((bf16[8,160,1024]{2,1,0:T(8,128)(2,1)}), bf16[8,160,1024]{2,1,0:T(8,128)(2,1)}, u32[]{:S(2)}, u32[]{:S(2)}) async-start(bf16[8,160,1024]{2,1,0:T(8,128)(2,1)} %bitcast.63), calls=%async_computation.5 | async-start | bytes 5242880 | tf_op jit(solution)/shard_map/all_to_all | solution.py:45
  391.5 26.6 %collective-permute-done.18 = f32[10,1024]{1,0:T(8,128)S(1)} collective-permute-done((f32[10,1024]{1,0:T(8,128)S(1)}, f32[10,1024]{1,0:T(8,128)S(1)}, u32[]{:S(2)}, u32[]{:S(2)}) %collective-permute-start.18) | collective-permute-done | bytes 40992 | tf_op jit(solution)/shard_map/ppermute | solution.py:41
  419.7 16.8 %collective-permute-done.19 = f32[10,1024]{1,0:T(8,128)S(1)} collective-permute-done((f32[10,1024]{1,0:T(8,128)S(1)}, f32[10,1024]{1,0:T(8,128)S(1)}, u32[]{:S(2)}, u32[]{:S(2)}) %collective-permute-start.19) | collective-permute-done | bytes 40992 | tf_op jit(solution)/shard_map/ppermute | solution.py:41
  440.7 8.0 %collective-permute-done.20 = f32[10,1024]{1,0:T(8,128)S(1)} collective-permute-done((f32[10,1024]{1,0:T(8,128)S(1)}, f32[10,1024]{1,0:T(8,128)S(1)}, u32[]{:S(2)}, u32[]{:S(2)}) %collective-permute-start.20) | collective-permute-done | bytes 40992 | tf_op jit(solution)/shard_map/ppermute | solution.py:41
  449.5 5.6 %split_sums.3 = (bf16[4,192,512]{2,1,0:T(8,128)(2,1)}, bf16[4,192,512]{2,1,0:T(8,128)(2,1)}, bf16[4,128,512]{2,1,0:T(8,128)(2,1)}, bf16[4,128,512]{2,1,0:T(8,128...) custom-call(bf16[8,96,512]{2,1,0:T(8,128)(2,1)} %get-tuple-element.116.refs_0_, ...), custom_call_target="tpu_custom_call" | custom-call | flops 2097152 | bytes 12582912 | tf_op jit(solution)/shard_map/split_sums/pallas_call | solution.py:131
  456.1 5.0 bitcast_convert_fusion
  461.1 20.2 %collective-permute-done.9.refs_3_ = bf16[4,128,512]{2,1,0:T(8,128)(2,1)S(1)} collective-permute-done((bf16[4,128,512]{2,1,0:T(8,128)(2,1)}, bf16[4,128,512]{2,1,0:T(8,128)(2,1)S(1)}, u32[]{:S(2)}, u32[]{:S(2)}) %collective-permute-start.9) | collective-permute-done | bytes 524320 | tf_op jit(solution)/shard_map/ppermute | solution.py:41
  488.2 16.7 %collective-permute-done.21 = f32[10,1024]{1,0:T(8,128)S(1)} collective-permute-done((f32[10,1024]{1,0:T(8,128)S(1)}, f32[10,1024]{1,0:T(8,128)S(1)}, u32[]{:S(2)}, u32[]{:S(2)}) %collective-permute-start.21) | collective-permute-done | bytes 40992 | tf_op jit(solution)/shard_map/ppermute | solution.py:41
  507.8 4.9 combine_rows.1
  525.4 8.5 %collective-permute-done.14.refs_1_ = bf16[1,192,512]{2,1,0:T(8,128)(2,1)S(1)} collective-permute-done((bf16[1,192,512]{2,1,0:T(8,128)(2,1)}, bf16[1,192,512]{2,1,0:T(8,128)(2,1)S(1)}, u32[]{:S(2)}, u32[]{:S(2)}) %collective-permute-start.14) | collective-permute-done | bytes 196640 | tf_op jit(solution)/shard_map/ppermute | solution.py:41
  (124 shorter events, 79.5 us)
Async XLA Ops:
  7.2 43.7 %copy-start = (bf16[1024,1024]{1,0:T(8,128)(2,1)S(1)}, bf16[1024,1024]{1,0:T(8,128)(2,1)}, u32[]{:S(2)}) copy-start(bf16[1024,1024]{1,0:T(8,128)(2,1)} %param.14) | copy-start | bytes 6291460
  11.9 67.0 %all-to-all-start = ((bf16[8,160,1024]{2,1,0:T(8,128)(2,1)}), bf16[8,160,1024]{2,1,0:T(8,128)(2,1)}, u32[]{:S(2)}, u32[]{:S(2)}) async-start(bf16[8,160,1024]{2,1,0:T(8,128)(2,1)} %bitcast.64), calls=%async_computation | async-start | bytes 5242880 | tf_op jit(solution)/shard_map/all_to_all | solution.py:45
  22.1 31.4 %copy-start.14 = (f32[1,1024]{1,0:T(1,128)}, f32[1,1024]{1,0:T(1,128)S(1)}, u32[]{:S(2)}) copy-start(f32[1,1024]{1,0:T(1,128)S(1)} %get-tuple-element.171.gain_ref) | copy-start | bytes 12292
  82.7 35.3 %all-to-all-start.1 = ((bf16[8,80,1024]{2,1,0:T(8,128)(2,1)}), bf16[8,80,1024]{2,1,0:T(8,128)(2,1)}, u32[]{:S(2)}, u32[]{:S(2)}) async-start(bf16[8,80,1024]{2,1,0:T(8,128)(2,1)} %bitcast.70), calls=%async_computation.1 | async-start | bytes 2621440 | tf_op jit(solution)/shard_map/all_to_all | solution.py:45
  118.0 43.2 %all-to-all-start.2 = ((bf16[8,80,1024]{2,1,0:T(8,128)(2,1)}), bf16[8,80,1024]{2,1,0:T(8,128)(2,1)}, u32[]{:S(2)}, u32[]{:S(2)}) async-start(bf16[8,80,1024]{2,1,0:T(8,128)(2,1)} %bitcast.68), calls=%async_computation.2 | async-start | bytes 2621440 | tf_op jit(solution)/shard_map/all_to_all | solution.py:45
  161.2 42.9 %all-to-all-start.3 = ((bf16[8,80,1024]{2,1,0:T(8,128)(2,1)}), bf16[8,80,1024]{2,1,0:T(8,128)(2,1)}, u32[]{:S(2)}, u32[]{:S(2)}) async-start(bf16[8,80,1024]{2,1,0:T(8,128)(2,1)} %bitcast.69), calls=%async_computation.3 | async-start | bytes 2621440 | tf_op jit(solution)/shard_map/all_to_all | solution.py:45
  204.1 46.1 %all-to-all-start.4 = ((bf16[8,80,1024]{2,1,0:T(8,128)(2,1)}), bf16[8,80,1024]{2,1,0:T(8,128)(2,1)}, u32[]{:S(2)}, u32[]{:S(2)}) async-start(bf16[8,80,1024]{2,1,0:T(8,128)(2,1)} %bitcast.67), calls=%async_computation.4 | async-start | bytes 2621440 | tf_op jit(solution)/shard_map/all_to_all | solution.py:45
  210.1 246.0 %reduce-scatter.3.cloned.1.call-start = ((), (), s32[]{:S(2)}) async-start(), calls=%async_computation.8 | async-start | bytes 14417920 | tf_op jit(solution)/shard_map/reduce_scatter | solution.py:840
  250.2 271.5 %reduce-scatter.5.cloned.1.call-start = ((), (), s32[]{:S(2)}) async-start(), calls=%async_computation.9 | async-start | bytes 7208960 | tf_op jit(solution)/shard_map/reduce_scatter | solution.py:840
  302.3 10.9 %collective-permute-start = (bf16[8,2,256,512]{3,2,1,0:T(8,128)(2,1)}, bf16[8,2,256,512]{3,2,1,0:T(8,128)(2,1)}, u32[]{:S(2)}, u32[]{:S(2)}) collective-permute-start(bf16[8,2,256,512]{3,2,1,0:T(8,128)(2,1)} %get-tuple-element.115), channel_id=1, source_target_pairs={{0,8},{8,0},{16,24},{24,16},{1,9},{9,1},{17,25},{25,17},{2,10},{10... | collective-permute-start | bytes 12582920 | tf_op jit(solution)/shard_map/ppermute | solution.py:41
  321.1 20.9 %collective-permute-start.1 = (bf16[8,96,512]{2,1,0:T(8,128)(2,1)}, bf16[8,96,512]{2,1,0:T(8,128)(2,1)}, u32[]{:S(2)}, u32[]{:S(2)}) collective-permute-start(bf16[8,96,512]{2,1,0:T(8,128)(2,1)} %get-tuple-element.124), channel_id=1, source_target_pairs={{0,1},{1,0},{2,3},{3,2},{4,5},{5,4},{6,7},{7,6},{8,9},{9,8},{10,11... | collective-permute-start | bytes 2359304 | tf_op jit(solution)/shard_map/ppermute | solution.py:41
  323.5 34.4 %collective-permute-start.3 = (bf16[8,96,512]{2,1,0:T(8,128)(2,1)}, bf16[8,96,512]{2,1,0:T(8,128)(2,1)}, u32[]{:S(2)}, u32[]{:S(2)}) collective-permute-start(bf16[8,96,512]{2,1,0:T(8,128)(2,1)} %get-tuple-element.126), channel_id=1, source_target_pairs={{0,16},{8,24},{16,0},{24,8},{1,17},{9,25},{17,1},{25,9},{2,18},{10... | collective-permute-start | bytes 2359304 | tf_op jit(solution)/shard_map/ppermute | solution.py:41
  324.8 17.2 %collective-permute-start.2 = (bf16[8,64,512]{2,1,0:T(8,128)(2,1)}, bf16[8,64,512]{2,1,0:T(8,128)(2,1)}, u32[]{:S(2)}, u32[]{:S(2)}) collective-permute-start(bf16[8,64,512]{2,1,0:T(8,128)(2,1)} %get-tuple-element.125), channel_id=1, source_target_pairs={{0,2},{1,3},{2,0},{3,1},{4,6},{5,7},{6,4},{7,5},{8,10},{9,11},{10,... | collective-permute-start | bytes 1572872 | tf_op jit(solution)/shard_map/ppermute | solution.py:41
  357.8 15.3 %collective-permute-start.4 = (bf16[8,2,256,512]{3,2,1,0:T(8,128)(2,1)}, bf16[8,2,256,512]{3,2,1,0:T(8,128)(2,1)}, u32[]{:S(2)}, u32[]{:S(2)}) collective-permute-start(bf16[8,2,256,512]{3,2,1,0:T(8,128)(2,1)} %get-tuple-element.127), channel_id=1, source_target_pairs={{0,8},{8,0},{16,24},{24,16},{1,9},{9,1},{17,25},{25,17},{2,10},{10... | collective-permute-start | bytes 12582920 | tf_op jit(solution)/shard_map/ppermute | solution.py:41
  381.5 126.3 %all-to-all-start.5 = ((bf16[8,160,1024]{2,1,0:T(8,128)(2,1)}), bf16[8,160,1024]{2,1,0:T(8,128)(2,1)}, u32[]{:S(2)}, u32[]{:S(2)}) async-start(bf16[8,160,1024]{2,1,0:T(8,128)(2,1)} %bitcast.63), calls=%async_computation.5 | async-start | bytes 5242880 | tf_op jit(solution)/shard_map/all_to_all | solution.py:45
  387.2 2.7 collective-permute-start.17
  387.5 61.2 %collective-permute-start.5 = (bf16[8,96,512]{2,1,0:T(8,128)(2,1)}, bf16[8,96,512]{2,1,0:T(8,128)(2,1)}, u32[]{:S(2)}, u32[]{:S(2)}) collective-permute-start(bf16[8,96,512]{2,1,0:T(8,128)(2,1)} %get-tuple-element.132), channel_id=1, source_target_pairs={{0,1},{1,0},{2,3},{3,2},{4,5},{5,4},{6,7},{7,6},{8,9},{9,8},{10,11... | collective-permute-start | bytes 2359304 | tf_op jit(solution)/shard_map/ppermute | solution.py:41
  389.4 59.4 %collective-permute-start.7 = (bf16[8,96,512]{2,1,0:T(8,128)(2,1)}, bf16[8,96,512]{2,1,0:T(8,128)(2,1)}, u32[]{:S(2)}, u32[]{:S(2)}) collective-permute-start(bf16[8,96,512]{2,1,0:T(8,128)(2,1)} %get-tuple-element.138), channel_id=1, source_target_pairs={{0,16},{8,24},{16,0},{24,8},{1,17},{9,25},{17,1},{25,9},{2,18},{10... | collective-permute-start | bytes 2359304 | tf_op jit(solution)/shard_map/ppermute | solution.py:41
  390.0 28.2 %collective-permute-start.18 = (f32[10,1024]{1,0:T(8,128)S(1)}, f32[10,1024]{1,0:T(8,128)S(1)}, u32[]{:S(2)}, u32[]{:S(2)}) collective-permute-start(f32[10,1024]{1,0:T(8,128)S(1)} %fusion.26), channel_id=1, source_target_pairs={{0,16},{8,24},{16,0},{24,8},{1,17},{9,25},{17,1},{25,9},{2,18},{10... | collective-permute-start | bytes 122888 | tf_op jit(solution)/shard_map/ppermute | solution.py:41
  418.1 18.4 %collective-permute-start.19 = (f32[10,1024]{1,0:T(8,128)S(1)}, f32[10,1024]{1,0:T(8,128)S(1)}, u32[]{:S(2)}, u32[]{:S(2)}) collective-permute-start(f32[10,1024]{1,0:T(8,128)S(1)} %add.60), channel_id=1, source_target_pairs={{0,1},{1,0},{2,3},{3,2},{4,5},{5,4},{6,7},{7,6},{8,9},{9,8},{10,11... | collective-permute-start | bytes 122888 | tf_op jit(solution)/shard_map/ppermute | solution.py:41
  418.2 30.5 %collective-permute-start.6 = (bf16[8,64,512]{2,1,0:T(8,128)(2,1)}, bf16[8,64,512]{2,1,0:T(8,128)(2,1)S(1)}, u32[]{:S(2)}, u32[]{:S(2)}) collective-permute-start(bf16[8,64,512]{2,1,0:T(8,128)(2,1)} %get-tuple-element.135), channel_id=1, source_target_pairs={{0,2},{1,3},{2,0},{3,1},{4,6},{5,7},{6,4},{7,5},{8,10},{9,11},{10,... | collective-permute-start | bytes 1572872 | tf_op jit(solution)/shard_map/ppermute | solution.py:41
  436.5 12.2 %collective-permute-start.20 = (f32[10,1024]{1,0:T(8,128)S(1)}, f32[10,1024]{1,0:T(8,128)S(1)}, u32[]{:S(2)}, u32[]{:S(2)}) collective-permute-start(f32[10,1024]{1,0:T(8,128)S(1)} %add.61), channel_id=1, source_target_pairs={{0,2},{1,3},{2,0},{3,1},{4,6},{5,7},{6,4},{7,5},{8,10},{9,11},{10,... | collective-permute-start | bytes 122888 | tf_op jit(solution)/shard_map/ppermute | solution.py:41
  455.1 26.2 %collective-permute-start.10 = (bf16[4,192,512]{2,1,0:T(8,128)(2,1)}, bf16[4,192,512]{2,1,0:T(8,128)(2,1)S(1)}, u32[]{:S(2)}, u32[]{:S(2)}) collective-permute-start(bf16[4,192,512]{2,1,0:T(8,128)(2,1)} %get-tuple-element.147), channel_id=1, source_target_pairs={{0,1},{1,0},{2,3},{3,2},{4,5},{5,4},{6,7},{7,6},{8,9},{9,8},{10,11... | collective-permute-start | bytes 2359304 | tf_op jit(solution)/shard_map/ppermute | solution.py:41
  455.1 26.2 %collective-permute-start.8 = (bf16[4,192,512]{2,1,0:T(8,128)(2,1)}, bf16[4,192,512]{2,1,0:T(8,128)(2,1)}, u32[]{:S(2)}, u32[]{:S(2)}) collective-permute-start(bf16[4,192,512]{2,1,0:T(8,128)(2,1)} %get-tuple-element.143), channel_id=1, source_target_pairs={{0,16},{8,24},{16,0},{24,8},{1,17},{9,25},{17,1},{25,9},{2,18},{10... | collective-permute-start | bytes 2359304 | tf_op jit(solution)/shard_map/ppermute | solution.py:41
  455.8 25.5 %collective-permute-start.9 = (bf16[4,128,512]{2,1,0:T(8,128)(2,1)}, bf16[4,128,512]{2,1,0:T(8,128)(2,1)S(1)}, u32[]{:S(2)}, u32[]{:S(2)}) collective-permute-start(bf16[4,128,512]{2,1,0:T(8,128)(2,1)} %get-tuple-element.145), channel_id=1, source_target_pairs={{0,4},{1,5},{2,6},{3,7},{4,0},{5,1},{6,2},{7,3},{8,12},{9,13},{10,... | collective-permute-start | bytes 1572872 | tf_op jit(solution)/shard_map/ppermute | solution.py:41
  486.0 27.4 %collective-permute-start.11 = (bf16[2,192,512]{2,1,0:T(8,128)(2,1)}, bf16[2,192,512]{2,1,0:T(8,128)(2,1)S(1)}, u32[]{:S(2)}, u32[]{:S(2)}) collective-permute-start(bf16[2,192,512]{2,1,0:T(8,128)(2,1)} %get-tuple-element.150), channel_id=1, source_target_pairs={{0,2},{1,3},{2,0},{3,1},{4,6},{5,7},{6,4},{7,5},{8,10},{9,11},{10,... | collective-permute-start | bytes 1179656 | tf_op jit(solution)/shard_map/ppermute | solution.py:41
  486.0 27.4 %collective-permute-start.13 = (bf16[2,192,512]{2,1,0:T(8,128)(2,1)}, bf16[2,192,512]{2,1,0:T(8,128)(2,1)S(1)}, u32[]{:S(2)}, u32[]{:S(2)}) collective-permute-start(bf16[2,192,512]{2,1,0:T(8,128)(2,1)} %get-tuple-element.154), channel_id=1, source_target_pairs={{0,2},{1,3},{2,0},{3,1},{4,6},{5,7},{6,4},{7,5},{8,10},{9,11},{10,... | collective-permute-start | bytes 1179656 | tf_op jit(solution)/shard_map/ppermute | solution.py:41
  488.0 16.9 %collective-permute-start.21 = (f32[10,1024]{1,0:T(8,128)S(1)}, f32[10,1024]{1,0:T(8,128)S(1)}, u32[]{:S(2)}, u32[]{:S(2)}) collective-permute-start(f32[10,1024]{1,0:T(8,128)S(1)} %add.62), channel_id=1, source_target_pairs={{0,4},{1,5},{2,6},{3,7},{4,0},{5,1},{6,2},{7,3},{8,12},{9,13},{10,... | collective-permute-start | bytes 122888 | tf_op jit(solution)/shard_map/ppermute | solution.py:41
  505.5 7.9 %collective-permute-start.12 = (bf16[2,128,512]{2,1,0:T(8,128)(2,1)}, bf16[2,128,512]{2,1,0:T(8,128)(2,1)S(1)}, u32[]{:S(2)}, u32[]{:S(2)}) collective-permute-start(bf16[2,128,512]{2,1,0:T(8,128)(2,1)} %get-tuple-element.152), channel_id=1, source_target_pairs={{0,1},{1,0},{2,3},{3,2},{4,5},{5,4},{6,7},{7,6},{8,9},{9,8},{10,11... | collective-permute-start | bytes 786440 | tf_op jit(solution)/shard_map/ppermute | solution.py:41
  516.8 17.1 %collective-permute-start.14 = (bf16[1,192,512]{2,1,0:T(8,128)(2,1)}, bf16[1,192,512]{2,1,0:T(8,128)(2,1)S(1)}, u32[]{:S(2)}, u32[]{:S(2)}) collective-permute-start(bf16[1,192,512]{2,1,0:T(8,128)(2,1)} %get-tuple-element.158), channel_id=1, source_target_pairs={{0,4},{1,5},{2,6},{3,7},{4,0},{5,1},{6,2},{7,3},{8,12},{9,13},{10,... | collective-permute-start | bytes 589832 | tf_op jit(solution)/shard_map/ppermute | solution.py:41
  520.2 16.5 %collective-permute-start.16 = (bf16[1,192,512]{2,1,0:T(8,128)(2,1)}, bf16[1,192,512]{2,1,0:T(8,128)(2,1)S(1)}, u32[]{:S(2)}, u32[]{:S(2)}) collective-permute-start(bf16[1,192,512]{2,1,0:T(8,128)(2,1)} %get-tuple-element.162), channel_id=1, source_target_pairs={{0,4},{1,5},{2,6},{3,7},{4,0},{5,1},{6,2},{7,3},{8,12},{9,13},{10,... | collective-permute-start | bytes 589832 | tf_op jit(solution)/shard_map/ppermute | solution.py:41
  520.2 5.2 collective-permute-start.15
  (20 other events, 102.2 us)
Sparse Core Ops, SparseCore 0:
  250.3 106.8 reduce-scatter.2
  381.6 61.6 reduce-scatter.4
